TPU v7x, 32 devices: a whole 2x2x4 slice. The times are simulated.
32 devices in a mesh: groups: 2 (over y), region: 4 (over z), stn: 2 (over x), chan: 2 (over core).
Axes of the slice: x: 2, y: 2, z: 4, core: 2. Of those that a mesh axis runs over, the one named last changes fastest.
Arguments:
- archive: bfloat16 [20, 3, 65536], P('stn', None, ('groups', 'region')), parts along dimension 2, may hold values from -10 to 10
- starts: int32 [512], P(('groups', 'region')), parts along dimension 0, may hold values from 0 to 32368, as said below
- event_owner: int32 [512], P('groups'), parts along dimension 0, may hold values from 0 to 3, as said below
- station_mask: int32 [512, 20], P('groups'), parts along dimension 0, may hold values 0 or 1
- pair_first: int32 [4096], P(('groups', 'region')), parts along dimension 0, may hold values from 0 to 255, as said below
- pair_second: int32 [4096], P(('groups', 'region')), parts along dimension 0, may hold values from 0 to 255, as said below
- pair_count: int32 [8], P(('groups', 'region')), parts along dimension 0, may hold values from 128 to 512, as said below
Outputs:
- pair_stack: float32 [101, 4096], P(None, ('groups', 'region')), parts along dimension 1
- event_profile: float32 [101, 1024], P(None, ('groups', 'region')), parts along dimension 1
There are 2 independent parts, one for each index of `groups`. A program takes and returns all parts, laid end to end along the dimension named above; each array names one. Nothing has to cross between parts.
Inputs may be any that keep to these rules, and one draw needn't show every extreme that they name: The window of event e lies in time segment e // 64: starts[e] - (e // 64) * 8192 is between 0 and 7792; in every segment some window starts at the segment's first sample and another ends at its last sample. `event_owner`: among the 64 events of one time segment at most 32 have the same owner; every owner holds at least one event of each segment, and one owner holds exactly 32 of every segment. `pair_first`: entry p names an event owned by region p // 512. `pair_second`: entry p names an event other than pair_first[p], owned by region p // 512 or the next region. Entries of region r at or past pair_count[r] are padding; some region uses all 512.
All inputs are finite; a program needn't handle non-finite values.
Results may differ from a plain program's by a relative error of at most 0.0047.
Values may be sent and summed in bfloat16 or wider, within the bound.
No kernel may reach another device: no remote copies, remote signals or barrier semaphores. Data moves between devices by JAX's collectives and lax.ppermute only.
A program may use at most 64 MiB of HBM per device.

v0:
```python
import math

import jax
import jax.numpy as jnp
from jax import lax
from jax.sharding import PartitionSpec as P

COMP = 3
WIN = 400
MAXLAG = 50
NFFT = 512
LAGS = 101


def passed_along(value, axis, steps):
    count = lax.axis_size(axis)
    first, last = (max(0, -steps), min(count, count - steps))
    return lax.ppermute(value, axis, [(source, source + steps) for source in range(first, last)])


def forward_table(chan_index, half):
    sample = jnp.arange(WIN, dtype=jnp.int32)[:, None]
    column = jnp.arange(2 * half, dtype=jnp.int32)[None, :]
    freq = chan_index * half + column % half
    phase = (sample * freq % NFFT).astype(jnp.float32) * jnp.float32(2.0 * math.pi / NFFT)
    nyquist = (sample * (NFFT // 2) % NFFT).astype(jnp.float32) * jnp.float32(2.0 * math.pi / NFFT)
    sine = jnp.where((chan_index == 0) & (column == half), jnp.cos(nyquist), jnp.sin(phase))
    return jnp.where(column < half, jnp.cos(phase), sine).astype(jnp.bfloat16)


def lag_table(chan_index, half):
    shift_lag = jnp.arange(LAGS, dtype=jnp.int32)[:, None] - MAXLAG
    freq = chan_index * half + jnp.arange(half, dtype=jnp.int32)[None, :]
    phase = (freq * shift_lag % NFFT).astype(jnp.float32) * jnp.float32(2.0 * math.pi / NFFT)
    nyquist = (shift_lag * (NFFT // 2) % NFFT).astype(jnp.float32) * jnp.float32(
        2.0 * math.pi / NFFT
    )
    weight = jnp.where(freq == 0, jnp.float32(1.0 / NFFT), jnp.float32(2.0 / NFFT))
    first_part = weight * jnp.cos(phase)
    second_part = jnp.where(
        freq == 0, jnp.cos(nyquist) * jnp.float32(1.0 / NFFT), weight * jnp.cos(phase)
    )
    third_part = jnp.where(freq == 0, jnp.float32(0.0), -weight * jnp.sin(phase))
    return jnp.concatenate([first_part, second_part, third_part], axis=1)


def slot_table(event_owner, regions, per_block, bucket, slots):
    blocks = event_owner.reshape(regions, per_block)
    onehot = (blocks[:, :, None] == jnp.arange(regions, dtype=jnp.int32)[None, None, :]).astype(
        jnp.int32
    )
    before = jnp.cumsum(onehot, axis=1) - onehot
    ranking = jnp.sum(before * onehot, axis=2)
    block_index = jnp.arange(regions, dtype=jnp.int32)[:, None]
    return (blocks * slots + block_index * bucket + ranking).reshape(-1)


def to_spectra(windows, table):
    shape = windows.shape
    flat = windows.reshape(-1, shape[-1])
    wide = flat.astype(jnp.float32)
    energy = jnp.sum(wide * wide, axis=1, keepdims=True)
    coefs = jnp.dot(flat, table, preferred_element_type=jnp.float32)
    spectra = (coefs * lax.rsqrt(energy + WIN * 1e-05)).astype(jnp.bfloat16)
    return spectra.reshape(shape[:-1] + (table.shape[1],))


def on_device(archive, starts, event_owner, station_mask, pair_first, pair_second, pair_count):
    regions = lax.axis_size("region")
    region_index = lax.axis_index("region")
    station_index = lax.axis_index("stn")
    chan_index = lax.axis_index("chan")
    half = NFFT // (2 * lax.axis_size("chan"))
    per_block = starts.shape[0]
    station_count = archive.shape[0]
    segment = archive.shape[2]
    bucket = max(2, 2 * per_block // regions)
    slots = regions * bucket
    slot_of = slot_table(event_owner, regions, per_block, bucket, slots)
    table = forward_table(chan_index, half)
    local_owner = lax.dynamic_slice_in_dim(event_owner, region_index * per_block, per_block)
    local_slot = lax.dynamic_slice_in_dim(slot_of, region_index * per_block, per_block)
    target = local_owner * bucket + (local_slot - local_owner * slots - region_index * bucket)
    matched = (target[None, :] == jnp.arange(slots, dtype=jnp.int32)[:, None]).astype(jnp.int32)
    source_event = jnp.sum(matched * jnp.arange(per_block, dtype=jnp.int32)[None, :], axis=1)
    filled = jnp.sum(matched, axis=1)
    offsets = starts - region_index * segment
    channels = archive.reshape(station_count * COMP, segment)

    def cut_window(offset):
        return lax.dynamic_slice_in_dim(channels, offset, WIN, axis=1)

    windows = jax.vmap(cut_window)(offsets)
    local_mask = lax.dynamic_slice(
        station_mask,
        (region_index * per_block, station_index * station_count),
        (per_block, station_count),
    )
    channel_mask = jnp.repeat(local_mask, COMP, axis=1)
    windows = windows * channel_mask[:, :, None].astype(jnp.bfloat16)
    outgoing = jnp.take(windows, source_event, axis=0) * filled[:, None, None].astype(jnp.bfloat16)
    outgoing = outgoing.reshape((regions, bucket) + windows.shape[1:])
    received = to_spectra(
        lax.all_to_all(outgoing, "region", split_axis=0, concat_axis=0, tiled=True), table
    )
    own_rows = received.reshape((slots,) + received.shape[2:])
    partner_slab = passed_along(own_rows, "region", -1)
    combined = jnp.concatenate([own_rows, partner_slab], axis=0)
    first_local = jnp.take(slot_of, pair_first) - region_index * slots
    second_local = jnp.take(slot_of, pair_second) - region_index * slots
    lag_weights = lag_table(chan_index, half)

    def pair_block(indices):
        firsts, seconds = indices
        left = jnp.take(combined, firsts, axis=0)
        right = jnp.take(combined, seconds, axis=0)
        left_cos = left[..., :half].astype(jnp.float32)
        left_sin = left[..., half:].astype(jnp.float32)
        right_cos = right[..., :half].astype(jnp.float32)
        right_sin = right[..., half:].astype(jnp.float32)
        prod_one = jnp.sum(left_cos * right_cos, axis=1)
        prod_two = jnp.sum(left_sin * right_sin, axis=1)
        prod_three = jnp.sum(left_sin * right_cos - left_cos * right_sin, axis=1)
        stacked = jnp.concatenate([prod_one, prod_two, prod_three], axis=-1)
        return lax.dot_general(
            lag_weights, stacked, (((1,), (1,)), ((), ())), precision=lax.Precision.HIGHEST
        )

    pair_blocks = pair_first.shape[0] // 128
    partial_cross = lax.map(
        pair_block, (first_local.reshape(pair_blocks, 128), second_local.reshape(pair_blocks, 128))
    )
    partial_cross = jnp.transpose(partial_cross, (1, 0, 2)).reshape(LAGS, -1)
    cross = lax.psum(partial_cross, ("stn", "chan"))
    live = COMP * jnp.sum(
        jnp.take(station_mask, pair_first, axis=0) * jnp.take(station_mask, pair_second, axis=0),
        axis=1,
    )
    valid = jnp.arange(pair_first.shape[0], dtype=jnp.int32) < pair_count[0]
    scaled = (
        jnp.float32(math.sqrt(WIN))
        * cross
        / jnp.sqrt(jnp.maximum(live, 1).astype(jnp.float32))[None, :]
    )
    stack = jnp.where(valid[None, :], scaled, jnp.float32(0.0))
    first_hot = (first_local[:, None] == jnp.arange(slots, dtype=jnp.int32)[None, :]).astype(
        jnp.float32
    )
    second_hot = (second_local[:, None] == jnp.arange(2 * slots, dtype=jnp.int32)[None, :]).astype(
        jnp.float32
    )
    own_terms = jnp.dot(stack, first_hot, precision=lax.Precision.HIGHEST)
    back_terms = jnp.dot(stack[::-1], second_hot, precision=lax.Precision.HIGHEST)
    returned = passed_along(back_terms[:, slots:], "region", 1)
    profile = own_terms + back_terms[:, :slots] + returned
    return (stack, profile)


def solution(mesh):
    placed = (
        P("stn", None, ("groups", "region")),
        P(("groups", "region")),
        P("groups"),
        P("groups", None),
        P(("groups", "region")),
        P(("groups", "region")),
        P(("groups", "region")),
    )
    return jax.shard_map(
        on_device,
        mesh=mesh,
        in_specs=placed,
        out_specs=(P(None, ("groups", "region")), P(None, ("groups", "region"))),
        check_vma=False,
    )
```

profile of v0, /device:TPU:0, one launch (start us, length us, event | category | flops | bytes accessed | tf_op | source)
XLA Modules:
  0.0 422.5 jit_solution(4301259347090034743)
XLA Ops:
  12.0 1.5 reshape.213
  13.6 121.6 %while.12 = (s32[]{:T(128)}, bf16[30,8192]{1,0:T(8,128)(2,1)S(1)}, s32[64,2]{0,1:T(2,128)S(1)}, bf16[64,30,400]{2,1,0:T(8,128)(2,1)}, s32[]{:T(128)}) while((s32[]{:T(128)}, bf16[30,8192]{1,0:T(8,128)(2,1)S(1)}, s32[64,2]{0,1:T(2,128)S(1)}, bf16[64,30,400]{2,1,0:T(8,128)(2,1)}, s32[]{:T(128)}) %tuple.55), condition=%wide.while_cond, body=%wide.while_body.sunk | while | flops 2 | bytes 57381 | solution.py:91
  19.9 1.3 bitcast_dynamic-update-slice_fusion.2
  23.7 1.3 bitcast_dynamic-update-slice_fusion.2
  27.5 1.3 bitcast_dynamic-update-slice_fusion.2
  33.2 1.3 bitcast_dynamic-update-slice_fusion.2
  35.1 1.3 bitcast_dynamic-update-slice_fusion.2
  46.5 1.3 bitcast_dynamic-update-slice_fusion.2
  50.3 1.3 bitcast_dynamic-update-slice_fusion.2
  54.1 1.3 bitcast_dynamic-update-slice_fusion.2
  71.1 1.3 bitcast_dynamic-update-slice_fusion.2
  73.1 1.3 bitcast_dynamic-update-slice_fusion.2
  76.9 1.3 bitcast_dynamic-update-slice_fusion.2
  78.8 1.3 bitcast_dynamic-update-slice_fusion.2
  80.7 1.3 bitcast_dynamic-update-slice_fusion.2
  84.5 1.3 bitcast_dynamic-update-slice_fusion.2
  88.3 1.3 bitcast_dynamic-update-slice_fusion.2
  95.9 1.3 bitcast_dynamic-update-slice_fusion.2
  99.7 1.3 bitcast_dynamic-update-slice_fusion.2
  118.7 1.3 bitcast_dynamic-update-slice_fusion.2
  126.2 1.3 bitcast_dynamic-update-slice_fusion.2
  133.8 1.3 bitcast_dynamic-update-slice_fusion.2
  135.2 1.9 broadcast_multiply_fusion
  137.1 2.7 gather_fusion.2
  139.8 4.4 %copy.52 = bf16[128,30,400]{2,0,1:T(8,128)(2,1)S(1)} copy(bf16[128,30,400]{2,1,0:T(8,128)(2,1)} %gather_fusion.2) | data formatting | bytes 6144000 | tf_op jit(solution)/shard_map/jit(_take)/gather | solution.py:101
  144.7 2.3 copy.53
  147.0 6.3 %all-to-all-start = ((bf16[4,32,30,400]{3,1,2,0:T(8,128)(2,1)}), bf16[4,32,30,400]{3,1,2,0:T(8,128)(2,1)}, u32[]{:S(2)}, u32[]{:S(2)}) async-start(bf16[4,32,30,400]{3,1,2,0:T(8,128)(2,1)} %copy.53), calls=%async_computation | async-start | bytes 7864320 | tf_op jit(solution)/shard_map/all_to_all | solution.py:104
  153.4 87.7 %all-to-all-done = bf16[4,32,30,400]{3,1,2,0:T(8,128)(2,1)} async-done(((bf16[4,32,30,400]{3,1,2,0:T(8,128)(2,1)}), bf16[4,32,30,400]{3,1,2,0:T(8,128)(2,1)}, u32[]{:S(2)}, u32[]{:S(2)}) %all-to-all-start) | async-done | bytes 3072032 | tf_op jit(solution)/shard_map/all_to_all | solution.py:104
  241.1 3.0 multiply_reduce_fusion
  244.4 6.3 %copy.54 = bf16[4,32,30,400]{3,2,1,0:T(8,128)(2,1)} copy(bf16[4,32,30,400]{3,1,2,0:T(8,128)(2,1)} %all-to-all-done) | data formatting | bytes 6144000 | tf_op jit(solution)/shard_map/all_to_all | solution.py:104
  250.7 6.9 %reshape.214 = bf16[3840,400]{1,0:T(8,128)(2,1)} reshape(bf16[4,32,30,400]{3,2,1,0:T(8,128)(2,1)} %copy.54) | data formatting | bytes 6144000 | tf_op jit(solution)/shard_map/reshape | solution.py:60
  257.6 6.2 %fusion.13 = bf16[3840,256]{1,0:T(8,128)(2,1)} fusion(bf16[3840,400]{1,0:T(8,128)(2,1)} %reshape.214, f32[3840]{0:T(1024)S(1)} %rsqrt.12, bf16[400]{0:T(512)(128)(2,1)S(1)} %fusion.40, s32[256]{0:T(256)S(1)} %fusion.41, pred[256]{0:T(512)(128)(4,1)S(1)} %get-tuple-element.88, pred[256]{0:T(512)(128)(4,1)S(1)} %get-tuple-element.89), kind=kOutput, calls=%fused_computation.39 | convolution fusion | flops 790036480 | bytes 5055776 | tf_op jit(solution)/shard_map/dot_general | solution.py:63
  263.9 2.5 reshape_reshape.3
  266.4 2.4 copy.56
  268.8 1.6 collective-permute-start
  270.6 3.5 gather_fusion.4
  274.2 3.5 gather_fusion.3
  281.2 33.7 %collective-permute-done = bf16[128,30,256]{2,0,1:T(8,128)(2,1)} collective-permute-done((bf16[128,30,256]{2,0,1:T(8,128)(2,1)}, bf16[128,30,256]{2,0,1:T(8,128)(2,1)}, u32[]{:S(2)}, u32[]{:S(2)}) %collective-permute-start) | collective-permute-done | bytes 1966112 | tf_op jit(solution)/shard_map/ppermute | solution.py:18
  314.9 2.7 copy.57
  317.6 2.3 pad_maximum_fusion
  319.9 57.4 %while.11 = (s32[]{:T(128)}, f32[4,101,128]{2,1,0:T(8,128)S(1)}, s32[4,128]{1,0:T(4,128)S(1)}, bf16[256,30,256]{2,1,0:T(8,128)(2,1)}, s32[4,128]{1,0:T(4,128)S(1)}, /*index=5*/f32[101,384]{1,0:T(8,128)S(1)}, s32[]{:T(128)}) while((s32[]{:T(128)}, f32[4,101,128]{2,1,0:T(8,128)S(1)}, s32[4,128]{1,0:T(4,128)S(1)}, ...), condition=%wide.region_9.12_spmd, body=%wide.region_5.11_spmd.sunk | while | flops 67489280 | bytes 20279900 | solution.py:130
  319.9 4.2 gather_fusion.1
  324.1 1.9 broadcast_select_fusion.7
  326.0 4.2 gather_fusion
  330.2 1.9 broadcast_select_fusion.6
  332.1 1.8 fusion.64
  334.3 4.2 gather_fusion.1
  338.5 1.9 broadcast_select_fusion.7
  340.3 4.2 gather_fusion
  344.5 1.9 broadcast_select_fusion.6
  346.4 1.8 fusion.64
  348.6 4.2 gather_fusion.1
  352.8 1.9 broadcast_select_fusion.7
  354.7 4.2 gather_fusion
  358.9 1.9 broadcast_select_fusion.6
  360.8 1.8 fusion.64
  363.0 4.2 gather_fusion.1
  367.2 1.9 broadcast_select_fusion.7
  369.0 4.2 gather_fusion
  373.2 1.9 broadcast_select_fusion.6
  375.1 1.8 fusion.64
  378.1 29.8 %all-reduce.3.cloned.1.call-done = f32[101,512]{1,0:T(8,128)} async-done(((f32[101,512]{1,0:T(8,128)}), f32[101,512]{1,0:T(8,128)}) %all-reduce.3.cloned.1.call-update) | async-done | bytes 206864 | tf_op jit(solution)/shard_map/psum | solution.py:134
  409.5 3.4 collective-permute-start.1
  412.9 1.8 collective-permute-done.1
  (256 shorter events, 108.8 us)
Async XLA Ops:
  147.0 94.1 %all-to-all-start = ((bf16[4,32,30,400]{3,1,2,0:T(8,128)(2,1)}), bf16[4,32,30,400]{3,1,2,0:T(8,128)(2,1)}, u32[]{:S(2)}, u32[]{:S(2)}) async-start(bf16[4,32,30,400]{3,1,2,0:T(8,128)(2,1)} %copy.53), calls=%async_computation | async-start | bytes 7864320 | tf_op jit(solution)/shard_map/all_to_all | solution.py:104
  153.3 254.6 %all-reduce.3.cloned.1.call-start = ((), (), s32[]{:S(2)}) async-start(), calls=%async_computation.1 | async-start | bytes 425984 | tf_op jit(solution)/shard_map/psum | solution.py:134
  266.4 4.1 copy-start.2
  266.4 4.1 copy-start.1
  268.8 5.3 %copy-start.3 = (s32[512]{0:T(512)S(1)}, s32[512]{0:T(512)}, u32[]{:S(2)}) copy-start(s32[512]{0:T(512)} %param.19) | copy-start | bytes 6148
  268.8 46.1 %collective-permute-start = (bf16[128,30,256]{2,0,1:T(8,128)(2,1)}, bf16[128,30,256]{2,0,1:T(8,128)(2,1)}, u32[]{:S(2)}, u32[]{:S(2)}) collective-permute-start(bf16[128,30,256]{2,0,1:T(8,128)(2,1)} %copy.56), channel_id=1, source_target_pairs={{4,0},{8,4},{12,8},{5,1},{9,5},{13,9},{6,2},{10,6},{14,10},{7,3},{... | collective-permute-start | bytes 5898248 | tf_op jit(solution)/shard_map/ppermute | solution.py:18
  408.9 6.8 %copy-start = (f32[101,512]{1,0:T(8,128)}, f32[101,512]{1,0:T(8,128)S(1)}, u32[]{:S(2)}) copy-start(f32[101,512]{1,0:T(8,128)S(1)} %divide_select_fusion) | copy-start | bytes 620548
  409.5 5.2 %collective-permute-start.1 = (f32[101,128]{1,0:T(8,128)S(1)}, f32[101,128]{1,0:T(8,128)S(1)}, u32[]{:S(2)}, u32[]{:S(2)}) collective-permute-start(f32[101,128]{1,0:T(8,128)S(1)} %slice.50), channel_id=1, source_target_pairs={{0,4},{4,8},{8,12},{1,5},{5,9},{9,13},{2,6},{6,10},{10,14},{3,7},{... | collective-permute-start | bytes 155144 | tf_op jit(solution)/shard_map/ppermute | solution.py:18
Sparse Core Ops, SparseCore 0:
  378.2 29.6 all-reduce.2
where the time goes:
time: 425 us; the launch traced here: 422 us
  local copies, waits for them, and re-layouts  199 us (47%)
  waiting for transfers between devices  153 us (36%)
  other arithmetic  35 us (8%)
  between operations  15 us (4%)
  starting transfers between devices  11.4 us (3%)
  matrix products  9.15 us (2%)
    gather x192, local copies, waits for them, and re-layouts  121 us
    all_to_all x1, waiting for transfers between devices, on_device(): lax.all_to_all(outgoing, 'region', split_axis=0, concat_axis=0, tiled=True)  87.7 us
    ppermute x2, waiting for transfers between devices, passed_along(): lax.ppermute(value, axis, [(source, source + steps) for source in range(f...  35.5 us
    psum x1, waiting for transfers between devices, on_device(): cross = lax.psum(partial_cross, ('stn', 'chan'))  29.8 us
    gather x4, local copies, waits for them, and re-layouts, pair_block(): left = jnp.take(combined, firsts, axis=0)  16.8 us
    gather x4, local copies, waits for them, and re-layouts, pair_block(): right = jnp.take(combined, seconds, axis=0)  16.8 us
  transfers between devices with their start and end apart: 4, of which 4 were waited for; matrix products, arithmetic and copies ran while one was open for 2% of the time, Pallas kernels for 0%

commit v1 on v0

v1 whole, which is shorter than its diff:
```python
import math

import jax
import jax.numpy as jnp
import numpy as np
from jax import lax
from jax.experimental import pallas as pl
from jax.experimental.pallas import tpu as pltpu
from jax.sharding import PartitionSpec as P

COMP = 3
WIN = 400
MAXLAG = 50
NFFT = 512
LAGS = 101
BINS = NFFT // 2
LANES = 128
LAG_ROWS = 112
NT = (((1,), (1,)), ((), ()))


def forward_table():
    sample = np.arange(NFFT)[:, None]
    freq = np.arange(BINS)[None, :]
    angle = (sample * freq % NFFT) * (2.0 * math.pi / NFFT)
    sine = np.sin(angle)
    sine[:, 0] = np.cos(math.pi * (np.arange(NFFT) % 2))
    table = np.concatenate([np.cos(angle), sine], axis=1)
    table[WIN:] = 0.0
    return jnp.asarray(table, jnp.float32).astype(jnp.bfloat16)


def lag_table():
    shift = np.arange(LANES)[:, None] - MAXLAG
    freq = np.arange(BINS)[None, :]
    angle = (freq * shift % NFFT) * (2.0 * math.pi / NFFT)
    weight = np.where(freq == 0, 1.0 / NFFT, 2.0 / NFFT)
    even = weight * np.cos(angle)
    odd = -weight * np.sin(angle)
    odd[:, 0] = np.cos(math.pi * (shift[:, 0] % 2)) / NFFT
    table = np.concatenate([even, odd], axis=1) * math.sqrt(WIN)
    table[LAGS:] = 0.0
    high = jnp.asarray(table, jnp.float32).astype(jnp.bfloat16)
    low = (jnp.asarray(table, jnp.float32) - high.astype(jnp.float32)).astype(jnp.bfloat16)
    return jnp.concatenate([high, low], axis=0)


def slot_table(event_owner, regions, per_block, bucket, slots):
    blocks = event_owner.reshape(regions, per_block)
    owned = blocks[:, :, None] == jnp.arange(regions, dtype=jnp.int32)[None, None, :]
    onehot = owned.astype(jnp.int32)
    before = jnp.cumsum(onehot, axis=1) - onehot
    ranking = jnp.sum(before * onehot, axis=2)
    block_index = jnp.arange(regions, dtype=jnp.int32)[:, None]
    return (blocks * slots + block_index * bucket + ranking).reshape(-1)


def split(value):
    high = value.astype(jnp.bfloat16)
    return high, (value - high.astype(jnp.float32)).astype(jnp.bfloat16)


def correlate(regions, per_block, pair_cap, segment, slots, nch):
    rows = 2 * nch
    tiles = segment // LANES + 2

    def kernel(recv, mask, slot_event, table, weights, out, shifted, windows, cos_rows, sin_rows, even, odd,
               index_vmem, index, profile, sem):
        for part in range(regions):
            digits = recv[part, :, segment:].astype(jnp.float32)
            first = digits[0:1, :pair_cap] * 128.0 + digits[1:2, :pair_cap]
            second = digits[2:3, :pair_cap] * 128.0 + digits[3:4, :pair_cap]
            index_vmem[part, 0:1, :] = first.astype(jnp.int32) * rows
            index_vmem[part, 1:2, :] = second.astype(jnp.int32) * rows
            offset = digits[1:2, pair_cap:] * 128.0 + digits[2:3, pair_cap:]
            index_vmem[part, 2:3, :] = offset.astype(jnp.int32)
        copy = pltpu.make_async_copy(index_vmem, index, sem)
        copy.start()

        half = 2 * LANES

        def widen(part, carry):
            for k in range(tiles + 2):
                data = recv[part, :, k * LANES : (k + 1) * LANES].astype(jnp.float32)
                if k < tiles:
                    shifted[part, k, pl.ds(0, nch, stride=2), :] = data
                if k >= 2:
                    shifted[part, k - 2, pl.ds(1, nch, stride=2), :] = data
            return carry

        lax.fori_loop(0, regions, widen, 0)
        copy.wait()

        lane = lax.broadcasted_iota(jnp.int32, (rows, LANES), 1)
        odd_row = lax.broadcasted_iota(jnp.int32, (rows, LANES), 0) % 2
        keep = odd_row * half + LANES + lane < WIN

        def one_segment(part, carry):
            def one_event(group, inner):
                for step in range(4):
                    event = group * 4 + step
                    start = index[part, 2, event]
                    base = start // LANES
                    off = start % LANES
                    turn = (LANES - off) % LANES
                    data = [shifted[part, base + k] for k in range(3)]
                    later = lane >= off
                    row = pl.multiple_of(event * rows, rows)
                    near = pltpu.roll(jnp.where(later, data[0], data[1]), turn, 1)
                    far = pltpu.roll(jnp.where(later, data[1], data[2]), turn, 1)
                    windows[0, pl.ds(row, rows), :] = near
                    windows[1, pl.ds(row, rows), :] = jnp.where(keep, far, 0.0)
                return inner

            lax.fori_loop(0, per_block // 4, one_event, 0)
            count = per_block * nch
            early, late = (
                jnp.concatenate([windows[t, pl.ds(k, count, stride=2), :] for t in range(2)], axis=1)
                for k in range(2))
            energy = jnp.sum(early * early + late * late, axis=1, keepdims=True)
            coefs = jnp.dot(early.astype(jnp.bfloat16), table[:half, :], preferred_element_type=jnp.float32)
            coefs += jnp.dot(late.astype(jnp.bfloat16), table[half:, :], preferred_element_type=jnp.float32)
            place = pl.multiple_of(part * count, count)
            factor = mask[pl.ds(place, count), :] * lax.rsqrt(energy + WIN * 1e-05)
            for k in range(2):
                piece = coefs[:, k * LANES : (k + 1) * LANES] * factor
                cos_rows[pl.ds(2 * place + k, count, stride=2), :] = piece.astype(jnp.bfloat16).astype(jnp.float32)
                piece = coefs[:, BINS + k * LANES : BINS + (k + 1) * LANES] * factor
                sin_rows[pl.ds(2 * place + k, count, stride=2), :] = piece.astype(jnp.bfloat16).astype(jnp.float32)
            return carry

        lax.fori_loop(0, regions, one_segment, 0)

        special = (odd_row == 0) & (lane == 0)
        profile[...] = jnp.zeros_like(profile)

        def one_region(part, carry):
            def some_pairs(group, inner):
                for step in range(8):
                    pair = group * 8 + step
                    a = pl.multiple_of(index[part, 0, pair], rows)
                    b = pl.multiple_of(index[part, 1, pair], rows)
                    cos_a, sin_a = cos_rows[pl.ds(a, rows), :], sin_rows[pl.ds(a, rows), :]
                    cos_b, sin_b = cos_rows[pl.ds(b, rows), :], sin_rows[pl.ds(b, rows), :]
                    sines = sin_a * sin_b
                    place = pl.multiple_of(pair * rows, rows)
                    even[pl.ds(place, rows), :] = cos_a * cos_b + jnp.where(special, 0.0, sines)
                    odd[pl.ds(place, rows), :] = jnp.where(special, sines, sin_a * cos_b - cos_a * sin_b)
                return inner

            lax.fori_loop(0, pair_cap // 8, some_pairs, 0)
            sums = []
            for store in (even, odd):
                for k in range(2):
                    total = store[pl.ds(k, pair_cap, stride=rows), :]
                    for c in range(1, nch):
                        total += store[pl.ds(2 * c + k, pair_cap, stride=rows), :]
                    sums.append(total)
            high, low = split(jnp.concatenate(sums, axis=1))
            both = lax.dot_general(weights[...], high, NT, preferred_element_type=jnp.float32)
            rest = lax.dot_general(weights[:LANES, :], low, NT, preferred_element_type=jnp.float32)
            cross = both[:LANES] + both[LANES:] + rest
            digits = recv[part, :, segment:].astype(jnp.float32)
            code = digits[0:1, pair_cap:]
            live = jnp.maximum((code - 1.0) * COMP, 1.0)
            stack = cross * jnp.where(code > 0.0, lax.rsqrt(live), 0.0)
            out[part, :, :pair_cap] = stack[:LAG_ROWS]
            first = digits[0:1, :pair_cap] * 128.0 + digits[1:2, :pair_cap]
            second = digits[2:3, :pair_cap] * 128.0 + digits[3:4, :pair_cap]
            high, low = split(stack)

            def gathered(names, event):
                hot = (jnp.concatenate([names] * (pair_cap // LANES), axis=1) == event).astype(jnp.float32)
                hot = hot.astype(jnp.bfloat16)
                return lax.dot_general(high, hot, NT, preferred_element_type=jnp.float32) + lax.dot_general(
                    low, hot, NT, preferred_element_type=jnp.float32)

            own = slot_event[pl.ds(pl.multiple_of(part * slots, slots), slots), :]
            profile[0, part] += gathered(own, first)
            profile[1, part] += gathered(own, second)

            @pl.when(part + 1 < regions)
            def _():
                then = slot_event[pl.ds(pl.multiple_of((part + 1) * slots, slots), slots), :]
                profile[1, part + 1] += gathered(then, second)
            return carry

        lax.fori_loop(0, regions, one_region, 0)
        mirrored = lax.broadcasted_iota(jnp.int32, (LANES, LANES), 0) + lax.broadcasted_iota(
            jnp.int32, (LANES, LANES), 1) == LAGS - 1
        mirror = mirrored.astype(jnp.float32).astype(jnp.bfloat16)

        def finish(part, carry):
            high, low = split(profile[1, part])
            flipped = jnp.dot(mirror, high, preferred_element_type=jnp.float32) + jnp.dot(
                mirror, low, preferred_element_type=jnp.float32)
            out[part, :, pair_cap:] = (profile[0, part] + flipped)[:LAG_ROWS]
            return carry

        lax.fori_loop(0, regions, finish, 0)

    events = regions * per_block
    return pl.pallas_call(
        kernel,
        out_shape=jax.ShapeDtypeStruct((regions, LAG_ROWS, pair_cap + slots), jnp.float32),
        in_specs=[pl.BlockSpec(memory_space=pltpu.VMEM)] * 5,
        out_specs=pl.BlockSpec(memory_space=pltpu.VMEM),
        scratch_shapes=[
            pltpu.VMEM((regions, tiles, rows, LANES), jnp.float32),
            pltpu.VMEM((2, per_block * rows, LANES), jnp.float32),
            pltpu.VMEM((events * rows, LANES), jnp.float32),
            pltpu.VMEM((events * rows, LANES), jnp.float32),
            pltpu.VMEM((pair_cap * rows, LANES), jnp.float32),
            pltpu.VMEM((pair_cap * rows, LANES), jnp.float32),
            pltpu.VMEM((regions, 3, pair_cap), jnp.int32),
            pltpu.SMEM((regions, 3, pair_cap), jnp.int32),
            pltpu.VMEM((2, regions, LANES, slots), jnp.float32),
            pltpu.SemaphoreType.DMA(()),
        ],
        name="correlate",
    )


def on_device(archive, starts, event_owner, station_mask, pair_first, pair_second, pair_count):
    regions = lax.axis_size("region")
    region_index = lax.axis_index("region")
    station_index = lax.axis_index("stn")
    chan_index = lax.axis_index("chan")
    chans = lax.axis_size("chan")
    per_block = starts.shape[0]
    pair_cap = pair_first.shape[0]
    station_count = archive.shape[0]
    segment = archive.shape[2]
    channels = station_count * COMP
    bucket = max(2, 2 * per_block // regions)
    slots = regions * bucket
    nch = 4 * -(-channels // (4 * chans * regions))
    events = regions * per_block

    offsets = starts - region_index * segment
    mask_bf16 = station_mask.astype(jnp.bfloat16)
    names = jnp.arange(events, dtype=jnp.int32)[None, :]
    mask_first = jnp.dot((pair_first[:, None] == names).astype(jnp.bfloat16), mask_bf16,
                         preferred_element_type=jnp.float32)
    mask_second = jnp.dot((pair_second[:, None] == names).astype(jnp.bfloat16), mask_bf16,
                          preferred_element_type=jnp.float32)
    common = jnp.sum(mask_first * mask_second, axis=1)
    valid = jnp.arange(pair_cap, dtype=jnp.int32) < pair_count[0]
    code = jnp.where(valid, common + 1.0, 0.0).astype(jnp.bfloat16)
    pad = jnp.zeros((pair_cap - per_block,), jnp.bfloat16)
    digit_rows = jnp.stack([
        jnp.concatenate([(pair_first // 128).astype(jnp.bfloat16), code]),
        jnp.concatenate([(pair_first % 128).astype(jnp.bfloat16), (offsets // 128).astype(jnp.bfloat16), pad]),
        jnp.concatenate([(pair_second // 128).astype(jnp.bfloat16), (offsets % 128).astype(jnp.bfloat16), pad]),
        jnp.concatenate([(pair_second % 128).astype(jnp.bfloat16), jnp.zeros((pair_cap,), jnp.bfloat16)]),
    ])
    if nch > 4:
        digit_rows = jnp.pad(digit_rows, ((0, nch - 4), (0, 0)))
    flat = archive.reshape(channels, segment)
    flat = jnp.pad(flat, ((0, chans * regions * nch - channels), (0, 0)))
    mine = lax.dynamic_slice_in_dim(flat, chan_index * regions * nch, regions * nch)
    digits = jnp.broadcast_to(digit_rows[None], (regions,) + digit_rows.shape)
    payload = jnp.concatenate([mine.reshape(regions, nch, segment), digits], axis=2)
    received = lax.all_to_all(payload, "region", split_axis=0, concat_axis=0, tiled=True)

    slot_of = slot_table(event_owner, regions, per_block, bucket, slots)
    hit = slot_of[None, :] == jnp.arange(regions * slots, dtype=jnp.int32)[:, None]
    slot_event = jnp.sum(jnp.where(hit, names + 1, 0), axis=1) - 1
    slot_event = jnp.broadcast_to(slot_event.astype(jnp.float32)[:, None], (regions * slots, LANES))
    channel = (chan_index * regions + region_index) * nch + jnp.arange(nch, dtype=jnp.int32)
    station = station_index * station_count + channel // COMP
    pick = (jnp.arange(station_mask.shape[1], dtype=jnp.int32)[:, None] == station[None, :]) & (
        channel < channels)[None, :]
    picked = jnp.dot(mask_bf16, pick.astype(jnp.bfloat16), preferred_element_type=jnp.float32)
    event_mask = jnp.broadcast_to(picked[:, :, None], (events, nch, LANES)).reshape(events * nch, LANES)

    partial = correlate(regions, per_block, pair_cap, segment, slots, nch)(
        received, event_mask, slot_event, forward_table(), lag_table())

    share = LAG_ROWS // chans
    swap = [(0, 1), (1, 0)]
    keep = lax.dynamic_slice_in_dim(partial, chan_index * share, share, axis=1)
    give = lax.dynamic_slice_in_dim(partial, (1 - chan_index) * share, share, axis=1)
    keep = keep + lax.ppermute(give, "chan", swap)
    spread = lax.all_to_all(keep.astype(jnp.bfloat16), "region", split_axis=0, concat_axis=0, tiled=True)
    total = jnp.sum(spread.astype(jnp.float32), axis=0)
    count = lax.axis_size("stn")
    step = 1
    whole = total
    while step < count:
        whole = whole + lax.ppermute(whole, "stn", [(i, i ^ step) for i in range(count)])
        step *= 2
    other = lax.ppermute(whole, "chan", swap)
    low = jnp.where(chan_index == 0, whole, other)
    high = jnp.where(chan_index == 0, other, whole)
    full = jnp.concatenate([low, high], axis=0)[:LAGS]
    return full[:, :pair_cap], full[:, pair_cap:]


def solution(mesh):
    placed = (
        P("stn", None, ("groups", "region")),
        P(("groups", "region")),
        P("groups"),
        P("groups", None),
        P(("groups", "region")),
        P(("groups", "region")),
        P(("groups", "region")),
    )
    return jax.shard_map(
        on_device,
        mesh=mesh,
        in_specs=placed,
        out_specs=(P(None, ("groups", "region")), P(None, ("groups", "region"))),
        check_vma=False,
    )
```

time: 425 us -> 76.6 us (0.18)
  local copies, waits for them, and re-layouts: 199 us -> 5.39 us
  waiting for transfers between devices: 153 us -> 15.1 us
  other arithmetic: 35 us -> 5.14 us
  Pallas kernels: 0 us -> 26.3 us
  between operations: 15 us -> 1.5 us
  blocking collectives: 0 us -> 12.4 us
  matrix products: 9.15 us -> 2.25 us
    gather x206 -> x0, local copies, waits for them, and re-layouts: 171 us -> none
    all_to_all x1, waiting for transfers between devices: 87.7 us -> 8.13 us  [on_device(): lax.all_to_all(payload, 'region', split_axis=0, concat_axis=0, tiled=True)]
    psum x1 -> x0, waiting for transfers between devices: 29.8 us -> none  [on_device(): cross = lax.psum(partial_cross, ('stn', 'chan'))]
    ppermute x2 -> x3, waiting for transfers between devices: 35.5 us -> 6.92 us  [the longest x1 3.61 us: on_device(): lax.ppermute(whole, 'stn', [(i, i ^ step) for i in range(count)])]
    pallas_call x0 -> x1, Pallas kernels: none -> 26.3 us  [on_device(): correlate(regions, per_block, pair_cap, segment, slots, nch)]
    select_n x13 -> x1, other arithmetic: 15.8 us -> 0.03 us  [on_device(): high = jnp.where(chan_index == 0, other, whole)]
    all_to_all x0 -> x1, blocking collectives: none -> 12.4 us  [on_device(): lax.all_to_all(keep.astype(jnp.bfloat16), 'region', split_axis=0, concat_...]
    reduce_sum x7 -> x2, other arithmetic: 10.5 us -> 0.19 us  [the longest x1 0.15 us: on_device(): slot_event = jnp.sum(jnp.where(hit, names + 1, 0), axis=1) - 1]
where the time goes in v1:
time: 76.6 us; the launch traced here: 76.1 us
  Pallas kernels  26.3 us (34%)
  waiting for transfers between devices  15.1 us (20%)
  blocking collectives  12.4 us (16%)
  starting transfers between devices  8.04 us (10%)
  local copies, waits for them, and re-layouts  5.39 us (7%)
  other arithmetic  5.14 us (7%)
  matrix products  2.25 us (3%)
  between operations  1.5 us (2%)
    pallas_call x1, Pallas kernels, on_device(): correlate(regions, per_block, pair_cap, segment, slots, nch)  26.3 us
    all_to_all x1, blocking collectives, on_device(): lax.all_to_all(keep.astype(jnp.bfloat16), 'region', split_axis=0, concat_...  12.4 us
    all_to_all x1, waiting for transfers between devices, on_device(): lax.all_to_all(payload, 'region', split_axis=0, concat_axis=0, tiled=True)  8.13 us
    all_to_all x1, starting transfers between devices, on_device(): lax.all_to_all(payload, 'region', split_axis=0, concat_axis=0, tiled=True)  6.35 us
    ppermute x1, waiting for transfers between devices, on_device(): lax.ppermute(whole, 'stn', [(i, i ^ step) for i in range(count)])  3.61 us
    ppermute x1, waiting for transfers between devices, on_device(): keep = keep + lax.ppermute(give, 'chan', swap)  1.96 us
    ppermute x1, starting transfers between devices, on_device(): lax.ppermute(whole, 'stn', [(i, i ^ step) for i in range(count)])  1.55 us
    reshape x1, local copies, waits for them, and re-layouts, on_device(): flat = archive.reshape(channels, segment)  1.53 us
  transfers between devices with their start and end apart: 4, of which 4 were waited for; matrix products, arithmetic and copies ran while one was open for 2% of the time, Pallas kernels for 0%

profile of v1, /device:TPU:0, one launch (start us, length us, event | category | flops | bytes accessed | tf_op | source)
XLA Modules:
  0.0 76.1 jit_solution(7058963723641473136)
XLA Ops:
  0.6 0.7 fusion.19
  1.3 0.7 fusion.10
  2.0 0.7 fusion.12
  2.7 1.0 %fusion.1 = f32[512,20]{0,1:T(8,128)S(1)} fusion(s32[512]{0:T(512)} %param.14, s32[256,20]{0,1:T(8,128)} %param.13), kind=kOutput, calls=%fused_computation.10 | convolution fusion | flops 5379072 | bytes 63488 | tf_op jit(solution)/shard_map/dot_general | solution.py:243
  3.7 1.0 %fusion = f32[512]{0:T(512)S(1)} fusion(f32[512,20]{0,1:T(8,128)S(1)} %fusion.1, s32[512]{0:T(512)} %param.15, s32[256,20]{0,1:T(8,128)} %param.13), kind=kOutput, calls=%fused_computation.1 | convolution fusion | flops 5399040 | bytes 65536 | tf_op jit(solution)/shard_map/dot_general | solution.py:245
  5.4 0.1 pad_maximum_fusion.4
  5.6 1.5 %reshape.60 = bf16[30,8192]{1,0:T(8,128)(2,1)S(1)} reshape(bf16[10,3,8192]{2,1,0:T(4,128)(2,1)} %param.10) | data formatting | bytes 983040 | tf_op jit(solution)/shard_map/reshape | solution.py:259
  7.1 0.0 copy-start.3
  7.1 0.1 pad_dynamic-slice_fusion
  7.2 0.0 copy-start.2
  7.2 0.1 reshape.61
  7.4 0.8 %pad_maximum_fusion = bf16[4,4,9216]{2,1,0:T(4,128)(2,1)} fusion(bf16[4,4,1024]{2,1,0:T(4,128)(2,1)S(1)} %broadcast_in_dim.28, bf16[4,4,8192]{2,1,0:T(4,128)(2,1)S(1)} %reshape.61), kind=kLoop, calls=%fused_computation.11 | loop fusion | flops 589824 | bytes 589824 | tf_op jit(solution)/shard_map/concatenate | solution.py:263
  8.2 6.3 %all-to-all-start = ((bf16[4,4,9216]{2,1,0:T(4,128)(2,1)}), bf16[4,4,9216]{2,1,0:T(4,128)(2,1)S(1)}, u32[]{:S(2)}, u32[]{:S(2)}) async-start(bf16[4,4,9216]{2,1,0:T(4,128)(2,1)} %pad_maximum_fusion), calls=%async_computation | async-start | bytes 589824 | tf_op jit(solution)/shard_map/all_to_all | solution.py:264
  14.6 0.0 copy-done.3
  14.6 0.1 eq.86
  14.7 0.1 fusion.5
  14.8 0.1 reduce_window_sum.11
  14.9 0.2 select_reduce_fusion.1
  15.2 0.1 reduce_sum.40
  15.2 0.1 add.119
  15.3 0.1 add.120
  15.4 0.0 copy-done.2
  15.4 0.2 convolution_bitcast_fusion
  15.6 0.1 copy.13
  15.8 0.1 broadcast_in_dim.29
  15.9 0.1 select_reduce_fusion
  16.0 8.1 %all-to-all-done.recv = bf16[4,4,9216]{2,1,0:T(4,128)(2,1)S(1)} async-done(((bf16[4,4,9216]{2,1,0:T(4,128)(2,1)}), bf16[4,4,9216]{2,1,0:T(4,128)(2,1)S(1)}, u32[]{:S(2)}, u32[]{:S(2)}) %all-to-all-start) | async-done | bytes 294944 | tf_op jit(solution)/shard_map/all_to_all | solution.py:264
  24.2 0.0 copy-start.1
  24.2 1.0 %broadcast_in_dim.30.mask = f32[1024,128]{1,0:T(8,128)} broadcast(f32[1024]{0:T(1024)S(1)} %broadcast_in_dim.29), dimensions={0} | broadcast | bytes 528384 | tf_op jit(solution)/shard_map/broadcast_in_dim | solution.py:275
  25.2 0.8 %broadcast_in_dim.56.slot_event = f32[512,128]{1,0:T(8,128)} broadcast(f32[512]{0:T(512)S(1)} %add_convert_fusion.1), dimensions={0} | broadcast | bytes 264192 | tf_op jit(solution)/shard_map/broadcast_in_dim | solution.py:269
  26.0 0.0 copy-done.1
  26.0 26.3 %correlate.1 = f32[4,112,640]{2,1,0:T(8,128)} custom-call(bf16[4,4,9216]{2,1,0:T(4,128)(2,1)} %copy-done.1, f32[1024,128]{1,0:T(8,128)} %broadcast_in_dim.30.mask, f32[512,128]{1,0:T(8,128)} %broadcast_in_dim.56.slot_event, bf16[512,512]{1,0:T(8,128)(2,1)} %constant.122.table, bf16[256,512]{1,0:T(8,128)(2,1)} %constant.127.weights), custom_call_target="tpu_custom_call" | custom-call | tf_op jit(solution)/shard_map/correlate/pallas_call | solution.py:277
  52.4 0.0 copy-start
  52.4 1.2 %constant_dynamic-slice_fusion = f32[4,56,640]{2,1,0:T(8,128)S(1)} fusion(f32[4,112,640]{2,1,0:T(8,128)} %correlate.1, s32[]{:T(128)S(6)} %select_n.80), kind=kLoop, calls=%fused_computation.62 | loop fusion | bytes 1146884 | tf_op jit(solution)/shard_map/dynamic_slice | solution.py:283
  53.6 0.1 collective-permute-start
  53.7 2.0 %collective-permute-done = f32[4,56,640]{2,1,0:T(8,128)S(1)} collective-permute-done((f32[4,56,640]{2,1,0:T(8,128)S(1)}, f32[4,56,640]{2,1,0:T(8,128)S(1)}, u32[]{:S(2)}, u32[]{:S(2)}) %collective-permute-start) | collective-permute-done | bytes 573472 | tf_op jit(solution)/shard_map/ppermute | solution.py:284
  55.6 0.0 copy-done
  55.6 0.1 add_convert_fusion
  55.7 12.4 %all_to_all.10 = bf16[4,56,640]{2,1,0:T(8,128)(2,1)S(1)} all-to-all(bf16[4,56,640]{2,1,0:T(8,128)(2,1)S(1)} %add_convert_fusion), channel_id=1, replica_groups=mesh['groups'=2,'region'=4,'stn'=2,'chan'=2] {'region'}, dimensions={0} | all-to-all | bytes 573440 | tf_op jit(solution)/shard_map/all_to_all | solution.py:285
  68.1 1.6 %collective-permute-start.1 = (f32[56,640]{1,0:T(8,128)S(1)}, f32[56,640]{1,0:T(8,128)S(1)}, u32[]{:S(2)}, u32[]{:S(2)}) collective-permute-start(f32[56,640]{1,0:T(8,128)S(1)} %convert_reduce_fusion), channel_id=1, source_target_pairs={{0,2},{2,0},{1,3},{3,1},{4,6},{6,4},{5,7},{7,5},{8,10},{10,8},{9,1... | collective-permute-start | bytes 430088 | tf_op jit(solution)/shard_map/ppermute | solution.py:291
  69.7 3.6 %collective-permute-done.1 = f32[56,640]{1,0:T(8,128)S(1)} collective-permute-done((f32[56,640]{1,0:T(8,128)S(1)}, f32[56,640]{1,0:T(8,128)S(1)}, u32[]{:S(2)}, u32[]{:S(2)}) %collective-permute-start.1) | collective-permute-done | bytes 143392 | tf_op jit(solution)/shard_map/ppermute | solution.py:291
  73.3 0.1 collective-permute-start.2
  73.4 1.3 %collective-permute-done.2 = f32[56,640]{1,0:T(8,128)S(1)} collective-permute-done((f32[56,640]{1,0:T(8,128)S(1)}, f32[56,640]{1,0:T(8,128)S(1)}, u32[]{:S(2)}, u32[]{:S(2)}) %collective-permute-start.2) | collective-permute-done | bytes 143392 | tf_op jit(solution)/shard_map/ppermute | solution.py:293
  74.7 0.6 pad_maximum_fusion.1
  75.4 0.7 fusion.4
  (18 shorter events, 0.2 us)
Async XLA Ops:
  7.1 7.5 %copy-start.3 = (s32[256]{0:T(256)S(1)}, s32[256]{0:T(256)}, u32[]{:S(2)}) copy-start(s32[256]{0:T(256)} %param.12) | copy-start | bytes 3076
  7.2 8.2 %copy-start.2 = (s32[256,20]{0,1:T(8,128)S(1)}, s32[256,20]{0,1:T(8,128)}, u32[]{:S(2)}) copy-start(s32[256,20]{0,1:T(8,128)} %param.13) | copy-start | bytes 61444
  8.2 16.0 %all-to-all-start = ((bf16[4,4,9216]{2,1,0:T(4,128)(2,1)}), bf16[4,4,9216]{2,1,0:T(4,128)(2,1)S(1)}, u32[]{:S(2)}, u32[]{:S(2)}) async-start(bf16[4,4,9216]{2,1,0:T(4,128)(2,1)} %pad_maximum_fusion), calls=%async_computation | async-start | bytes 589824 | tf_op jit(solution)/shard_map/all_to_all | solution.py:264
  24.2 1.9 %copy-start.1 = (bf16[4,4,9216]{2,1,0:T(4,128)(2,1)}, bf16[4,4,9216]{2,1,0:T(4,128)(2,1)S(1)}, u32[]{:S(2)}) copy-start(bf16[4,4,9216]{2,1,0:T(4,128)(2,1)S(1)} %all-to-all-done.recv) | copy-start | bytes 884740
  52.4 3.3 %copy-start = (f32[4,112,640]{2,1,0:T(8,128)S(1)}, f32[4,112,640]{2,1,0:T(8,128)}, u32[]{:S(2)}) copy-start(f32[4,112,640]{2,1,0:T(8,128)} %correlate.1) | copy-start | bytes 3440644
  53.6 2.0 %collective-permute-start = (f32[4,56,640]{2,1,0:T(8,128)S(1)}, f32[4,56,640]{2,1,0:T(8,128)S(1)}, u32[]{:S(2)}, u32[]{:S(2)}) collective-permute-start(f32[4,56,640]{2,1,0:T(8,128)S(1)} %constant_dynamic-slice_fusion), channel_id=1, source_target_pairs={{0,1},{1,0},{2,3},{3,2},{4,5},{5,4},{6,7},{7,6},{8,9},{9,8},{10,11... | collective-permute-start | bytes 1720328 | tf_op jit(solution)/shard_map/ppermute | solution.py:284
  68.1 5.2 %collective-permute-start.1 = (f32[56,640]{1,0:T(8,128)S(1)}, f32[56,640]{1,0:T(8,128)S(1)}, u32[]{:S(2)}, u32[]{:S(2)}) collective-permute-start(f32[56,640]{1,0:T(8,128)S(1)} %convert_reduce_fusion), channel_id=1, source_target_pairs={{0,2},{2,0},{1,3},{3,1},{4,6},{6,4},{5,7},{7,5},{8,10},{10,8},{9,1... | collective-permute-start | bytes 430088 | tf_op jit(solution)/shard_map/ppermute | solution.py:291
  73.3 1.4 %collective-permute-start.2 = (f32[56,640]{1,0:T(8,128)S(1)}, f32[56,640]{1,0:T(8,128)S(1)}, u32[]{:S(2)}, u32[]{:S(2)}) collective-permute-start(f32[56,640]{1,0:T(8,128)S(1)} %add.128), channel_id=1, source_target_pairs={{0,1},{1,0},{2,3},{3,2},{4,5},{5,4},{6,7},{7,6},{8,9},{9,8},{10,11... | collective-permute-start | bytes 430088 | tf_op jit(solution)/shard_map/ppermute | solution.py:293

commit v2 on v1

v2 whole, which is shorter than its diff:
```python
import math

import jax
import jax.numpy as jnp
import numpy as np
from jax import lax
from jax.experimental import pallas as pl
from jax.experimental.pallas import tpu as pltpu
from jax.sharding import PartitionSpec as P

COMP = 3
WIN = 400
MAXLAG = 50
NFFT = 512
LAGS = 101
BINS = NFFT // 2
LANES = 128
LAG_ROWS = 112
VMEM_ONLY = pl.BlockSpec(memory_space=pltpu.VMEM)
SMEM_ONLY = pl.BlockSpec(memory_space=pltpu.SMEM)
NT = (((1,), (1,)), ((), ()))
TN = (((0,), (0,)), ((), ()))


def forward_table():
    sample = np.arange(NFFT)[:, None]
    freq = np.arange(BINS)[None, :]
    angle = (sample * freq % NFFT) * (2.0 * math.pi / NFFT)
    sine = np.sin(angle)
    sine[:, 0] = np.cos(math.pi * (np.arange(NFFT) % 2))
    table = np.concatenate([np.cos(angle), sine], axis=1)
    table[WIN:] = 0.0
    return jnp.asarray(table, jnp.float32).astype(jnp.bfloat16)


def lag_table():
    shift = np.arange(LANES)[:, None] - MAXLAG
    freq = np.arange(BINS)[None, :]
    angle = (freq * shift % NFFT) * (2.0 * math.pi / NFFT)
    weight = np.where(freq == 0, 1.0 / NFFT, 2.0 / NFFT)
    even = weight * np.cos(angle)
    odd = -weight * np.sin(angle)
    odd[:, 0] = (np.cos(math.pi * (shift[:, 0] % 2)) - 1.0) / NFFT
    table = np.concatenate([even, odd], axis=1) * math.sqrt(WIN)
    table[LAGS:] = 0.0
    return jnp.asarray(table, jnp.float32).astype(jnp.bfloat16)


def slot_table(event_owner, regions, per_block, bucket, slots):
    blocks = event_owner.reshape(regions, per_block)
    owned = blocks[:, :, None] == jnp.arange(regions, dtype=jnp.int32)[None, None, :]
    onehot = owned.astype(jnp.int32)
    before = jnp.cumsum(onehot, axis=1) - onehot
    ranking = jnp.sum(before * onehot, axis=2)
    block_index = jnp.arange(regions, dtype=jnp.int32)[:, None]
    return (blocks * slots + block_index * bucket + ranking).reshape(-1)


def as_bf16(flags):
    return flags.astype(jnp.float32).astype(jnp.bfloat16)


def digits_of(value):
    return (value >> 7).astype(jnp.float32).astype(jnp.bfloat16), (value & 127).astype(jnp.float32).astype(jnp.bfloat16)


def station_share(stations, chans):
    return -(-stations // chans)


def pack(archive, starts, station_mask, pair_first, pair_second, pair_count, regions, chans, nch):
    stations, _, segment = archive.shape
    events, listed = station_mask.shape
    per_block = starts.shape[1]
    pair_cap = pair_first.shape[1]
    share = station_share(stations, chans)
    total = regions * nch

    def kernel(archive, starts, mask, first, second, count, out, flat):
        chan = lax.axis_index("chan")
        base = jnp.minimum(chan * share, stations - share)
        flat[pl.ds(total - nch, nch), :] = jnp.zeros((nch, segment), jnp.float32)
        for station in range(share):
            flat[pl.ds(station * COMP, COMP), :] = archive[base + station].astype(jnp.float32)
        if share * COMP < total - nch:
            flat[share * COMP : total - nch, :] = jnp.zeros((total - nch - share * COMP, segment), jnp.float32)
        names = lax.broadcasted_iota(jnp.int32, (events, pair_cap), 0)
        usable = mask[...].astype(jnp.float32).astype(jnp.bfloat16)
        chosen = [lax.dot_general(usable, as_bf16(names == ref[...]), TN, preferred_element_type=jnp.float32)
                  for ref in (first, second)]
        common = jnp.sum(chosen[0] * chosen[1], axis=0, keepdims=True)
        position = lax.broadcasted_iota(jnp.int32, (1, pair_cap), 1)
        code = jnp.where(position < count[0], common + 1.0, 0.0).astype(jnp.bfloat16)
        offset = digits_of(starts[...] - lax.axis_index("region") * segment)
        rows = digits_of(first[...]) + digits_of(second[...])
        for part in range(regions):
            out[part, :, :segment] = flat[pl.ds(part * nch, nch), :].astype(jnp.bfloat16)
            for k in range(4):
                out[part, k : k + 1, segment : segment + pair_cap] = rows[k]
            out[part, 0:1, segment + pair_cap :] = code
            out[part, 1:2, segment + pair_cap : segment + pair_cap + per_block] = offset[0]
            out[part, 2:3, segment + pair_cap : segment + pair_cap + per_block] = offset[1]

    return pl.pallas_call(
        kernel,
        out_shape=jax.ShapeDtypeStruct((regions, nch, segment + 2 * pair_cap), jnp.bfloat16),
        in_specs=[VMEM_ONLY] * 5 + [SMEM_ONLY],
        out_specs=VMEM_ONLY,
        scratch_shapes=[pltpu.VMEM((total, segment), jnp.float32)],
        name="pack",
    )(archive, starts, station_mask, pair_first, pair_second, pair_count)


def correlate(regions, per_block, pair_cap, segment, slots, nch):
    rows = 2 * nch
    tiles = segment // LANES + 2
    events = regions * per_block
    half = 2 * LANES
    cols = pair_cap // LANES
    per_row = min(per_block, LANES)
    share = LAG_ROWS // 2

    def kernel(recv, mask, station, slot_of, table, weights, kept, given, shifted, windows, spec, prod, weight_rows,
               index_vmem, index, whole, profile, sem):
        for part in range(regions):
            digits = recv[part, :, segment:].astype(jnp.float32)
            for k in range(2):
                event = (digits[2 * k : 2 * k + 1, :pair_cap] * 128.0 + digits[2 * k + 1 : 2 * k + 2, :pair_cap])
                event = event.astype(jnp.int32) * rows
                for c in range(cols):
                    row = k * cols + c
                    index_vmem[part, row : row + 1, :] = event[:, c * LANES : (c + 1) * LANES]
            for k in range(2):
                row = 2 * cols + k
                digit = digits[k + 1 : k + 2, pair_cap : pair_cap + LANES]
                index_vmem[part, row : row + 1, :] = digit.astype(jnp.int32)
        copy = pltpu.make_async_copy(index_vmem, index, sem)
        copy.start()

        def widen(part, carry):
            for k in range(tiles + 2):
                data = recv[part, :, k * LANES : (k + 1) * LANES].astype(jnp.float32)
                if k < tiles:
                    shifted[part, k, pl.ds(0, nch, stride=2), :] = data
                if k >= 2:
                    shifted[part, k - 2, pl.ds(1, nch, stride=2), :] = data
            return carry

        lax.fori_loop(0, regions, widen, 0)

        listed = lax.broadcasted_iota(jnp.int32, (mask.shape[1], LANES), 0)
        usable = mask[...].astype(jnp.float32).astype(jnp.bfloat16)
        for c in range(nch):
            weight_rows[pl.ds(c, events, stride=nch), :] = jnp.dot(
                usable, as_bf16(listed == station[c]), preferred_element_type=jnp.float32)
        copy.wait()

        lane = lax.broadcasted_iota(jnp.int32, (rows, LANES), 1)
        sublane = lax.broadcasted_iota(jnp.int32, (rows, LANES), 0)
        count = per_block * nch
        inside = lax.broadcasted_iota(jnp.int32, (count, LANES), 1) < WIN - half - LANES

        def one_segment(part, carry):
            def some_events(group, inner):
                for step in range(per_row):
                    base = index[part, 2 * cols, group * per_row + step]
                    off = index[part, 2 * cols + 1, group * per_row + step]
                    turn = (LANES - off) & (LANES - 1)
                    data = [shifted[part, base + k] for k in range(3)]
                    later = lane >= off
                    row = pl.multiple_of((group * per_row + step) * rows, rows)
                    windows[0, pl.ds(row, rows), :] = pltpu.roll(jnp.where(later, data[0], data[1]), turn, 1)
                    windows[1, pl.ds(row, rows), :] = pltpu.roll(jnp.where(later, data[1], data[2]), turn, 1)
                return inner

            if per_block == per_row:
                some_events(0, 0)
            else:
                lax.fori_loop(0, per_block // per_row, some_events, 0)
            pieces = [[windows[t, pl.ds(k, count, stride=2), :] for t in range(2)] for k in range(2)]
            squares = pieces[0][0] * pieces[0][0] + pieces[0][1] * pieces[0][1] + pieces[1][0] * pieces[1][0]
            squares += jnp.where(inside, pieces[1][1] * pieces[1][1], 0.0)
            energy = jnp.sum(squares, axis=1, keepdims=True)
            early, late = (jnp.concatenate(piece, axis=1).astype(jnp.bfloat16) for piece in pieces)
            coefs = jnp.dot(early, table[:half, :], preferred_element_type=jnp.float32)
            coefs += jnp.dot(late, table[half:, :], preferred_element_type=jnp.float32)
            place = pl.multiple_of(part * count, count)
            factor = weight_rows[pl.ds(place, count), :] * lax.rsqrt(energy + WIN * 1e-05)
            for s in range(2):
                for k in range(2):
                    column = s * BINS + k * LANES
                    piece = (coefs[:, column : column + LANES] * factor).astype(jnp.bfloat16)
                    spec[s, pl.ds(2 * place + k, count, stride=2), :] = piece.astype(jnp.float32)
            return carry

        lax.fori_loop(0, regions, one_segment, 0)

        special = (sublane % 2 == 0) & (lane == 0)
        upper = sublane < nch
        profile[...] = jnp.zeros_like(profile)
        names = lax.broadcasted_iota(jnp.int32, (events, LANES), 0) + 1
        name_digits = digits_of(names)
        slot_lane = slot_of[...]
        place_of = lax.broadcasted_iota(jnp.int32, (slots, events), 0)

        def names_in(part):
            hit = as_bf16(place_of + part * slots == slot_lane)
            high, low = (jnp.dot(hit, digit, preferred_element_type=jnp.float32) for digit in name_digits)
            return high * 128.0 + low - 1.0

        def one_region(part, carry):
            def some_pairs(row, inner):
                for step in range(LANES):
                    a = pl.multiple_of(index[part, row, step], rows)
                    b = pl.multiple_of(index[part, cols + row, step], rows)
                    cos_a, sin_a = spec[0, pl.ds(a, rows), :], spec[1, pl.ds(a, rows), :]
                    cos_b, sin_b = spec[0, pl.ds(b, rows), :], spec[1, pl.ds(b, rows), :]
                    sines = sin_a * sin_b
                    even = cos_a * cos_b + sines
                    odd = jnp.where(special, sines, sin_a * cos_b - cos_a * sin_b)
                    even += pltpu.roll(even, nch, 0)
                    odd += pltpu.roll(odd, nch, 0)
                    both = jnp.where(upper, even, odd)
                    place = pl.multiple_of((row * LANES + step) * rows, rows)
                    prod[pl.ds(place, rows), :] = both + pltpu.roll(both, rows - 2, 0)
                return inner

            lax.fori_loop(0, cols, some_pairs, 0)
            sums = [prod[pl.ds(k, pair_cap, stride=rows), :] for k in (0, 1, nch, nch + 1)]
            sums = jnp.concatenate(sums, axis=1).astype(jnp.bfloat16)
            cross = lax.dot_general(weights[...], sums, NT, preferred_element_type=jnp.float32)
            digits = recv[part, :, segment:].astype(jnp.float32)
            code = digits[0:1, pair_cap:]
            live = jnp.maximum((code - 1.0) * COMP, 1.0)
            stack = cross * jnp.where(code > 0.0, lax.rsqrt(live), 0.0)
            whole[part, :, :pair_cap] = stack[:LAG_ROWS]
            first = digits[0:1, :pair_cap] * 128.0 + digits[1:2, :pair_cap]
            second = digits[2:3, :pair_cap] * 128.0 + digits[3:4, :pair_cap]
            stack = stack.astype(jnp.bfloat16)

            def gathered(column, event):
                hot = as_bf16(jnp.concatenate([column] * cols, axis=1) == event)
                return lax.dot_general(stack, hot, NT, preferred_element_type=jnp.float32)

            own = names_in(part)
            profile[0, part] += gathered(own, first)
            profile[1, part] += gathered(own, second)

            @pl.when(part + 1 < regions)
            def _():
                profile[1, part + 1] += gathered(names_in(part + 1), second)
            return carry

        lax.fori_loop(0, regions, one_region, 0)
        mirror = as_bf16(lax.broadcasted_iota(jnp.int32, (LANES, LANES), 0) + lax.broadcasted_iota(
            jnp.int32, (LANES, LANES), 1) == LAGS - 1)
        chan = lax.axis_index("chan")
        mine = pl.multiple_of(chan * share, 8)
        theirs = pl.multiple_of((1 - chan) * share, 8)

        def finish(part, carry):
            value = profile[1, part]
            high = value.astype(jnp.bfloat16)
            low = (value - high.astype(jnp.float32)).astype(jnp.bfloat16)
            flipped = jnp.dot(mirror, high, preferred_element_type=jnp.float32) + jnp.dot(
                mirror, low, preferred_element_type=jnp.float32)
            whole[part, :, pair_cap:] = (profile[0, part] + flipped)[:LAG_ROWS]
            kept[part] = whole[part, pl.ds(mine, share), :]
            given[part] = whole[part, pl.ds(theirs, share), :].astype(jnp.bfloat16)
            return carry

        lax.fori_loop(0, regions, finish, 0)

    shape = (regions, share, pair_cap + slots)
    index_rows = 8 * -(-(2 * cols + 2) // 8)
    return pl.pallas_call(
        kernel,
        out_shape=(jax.ShapeDtypeStruct(shape, jnp.float32), jax.ShapeDtypeStruct(shape, jnp.bfloat16)),
        in_specs=[VMEM_ONLY, VMEM_ONLY, SMEM_ONLY] + [VMEM_ONLY] * 3,
        out_specs=(VMEM_ONLY, VMEM_ONLY),
        scratch_shapes=[
            pltpu.VMEM((regions, tiles, rows, LANES), jnp.float32),
            pltpu.VMEM((2, per_block * rows, LANES), jnp.float32),
            pltpu.VMEM((2, events * rows, LANES), jnp.float32),
            pltpu.VMEM((pair_cap * rows, LANES), jnp.float32),
            pltpu.VMEM((events * nch, LANES), jnp.float32),
            pltpu.VMEM((regions, index_rows, LANES), jnp.int32),
            pltpu.SMEM((regions, index_rows, LANES), jnp.int32),
            pltpu.VMEM((regions, LAG_ROWS, pair_cap + slots), jnp.float32),
            pltpu.VMEM((2, regions, LANES, slots), jnp.float32),
            pltpu.SemaphoreType.DMA(()),
        ],
        name="correlate",
    )


def on_device(archive, starts, event_owner, station_mask, pair_first, pair_second, pair_count):
    regions = lax.axis_size("region")
    chans = lax.axis_size("chan")
    chan_index = lax.axis_index("chan")
    per_block = starts.shape[0]
    pair_cap = pair_first.shape[0]
    stations = archive.shape[0]
    segment = archive.shape[2]
    bucket = max(2, 2 * per_block // regions)
    slots = regions * bucket
    share = station_share(stations, chans)
    nch = 4 * -(-share * COMP // (4 * regions))

    payload = pack(archive, starts.reshape(1, -1), station_mask, pair_first.reshape(1, -1),
                   pair_second.reshape(1, -1), pair_count, regions, chans, nch)
    received = lax.all_to_all(payload, "region", split_axis=0, concat_axis=0, tiled=True)

    slot_of = slot_table(event_owner, regions, per_block, bucket, slots).reshape(1, -1)
    channel = lax.axis_index("region") * nch + jnp.arange(nch, dtype=jnp.int32)
    local = jnp.minimum(chan_index * share, stations - share) + channel // COMP
    used = (channel < share * COMP) & (local >= chan_index * share)
    station = jnp.where(used, lax.axis_index("stn") * stations + local, -1)

    kept, given = correlate(regions, per_block, pair_cap, segment, slots, nch)(
        received, station_mask, station, slot_of, forward_table(), lag_table())

    swap = [(0, 1), (1, 0)]
    kept = kept + lax.ppermute(given, "chan", swap).astype(jnp.float32)
    spread = lax.all_to_all(kept.astype(jnp.bfloat16), "region", split_axis=0, concat_axis=0, tiled=True)
    whole = jnp.sum(spread.astype(jnp.float32), axis=0)
    count = lax.axis_size("stn")
    step = 1
    while step < count:
        sent = whole.astype(jnp.bfloat16)
        other = lax.ppermute(sent, "stn", [(i, i ^ step) for i in range(count)])
        whole = sent.astype(jnp.float32) + other.astype(jnp.float32)
        step *= 2
    other = lax.ppermute(whole, "chan", swap)
    low = jnp.where(chan_index == 0, whole, other)
    high = jnp.where(chan_index == 0, other, whole)
    full = jnp.concatenate([low, high], axis=0)[:LAGS]
    return full[:, :pair_cap], full[:, pair_cap:]


def solution(mesh):
    placed = (
        P("stn", None, ("groups", "region")),
        P(("groups", "region")),
        P("groups"),
        P("groups", None),
        P(("groups", "region")),
        P(("groups", "region")),
        P(("groups", "region")),
    )
    return jax.shard_map(
        on_device,
        mesh=mesh,
        in_specs=placed,
        out_specs=(P(None, ("groups", "region")), P(None, ("groups", "region"))),
        check_vma=False,
    )
```

time: 76.6 us -> 58.4 us (0.76)
  Pallas kernels: 26.3 us -> 16 us
  local copies, waits for them, and re-layouts: 5.39 us -> 3.12 us
  matrix products: 2.25 us -> 0 us
  waiting for transfers between devices: 15.1 us -> 13 us
  other arithmetic: 5.14 us -> 4.17 us
    pallas_call x1, Pallas kernels: 26.3 us -> 13.8 us  [on_device(): correlate(regions, per_block, pair_cap, segment, slots, nch)]
    unnamed x8 -> x5, local copies, waits for them, and re-layouts: 0.02 us -> 2.8 us
    dot_general x3 -> x0, matrix products: 2.25 us -> none  [the longest x1 1.04 us: on_device(): jnp.dot((pair_second[:, None] == names).astype(jnp.bfloat16), mask_bf16,...]
    pallas_call x0 -> x1, Pallas kernels: none -> 2.18 us  [pack(): pl.pallas_call(kernel, out_shape=jax.ShapeDtypeStruct((regions, nch, segm...]
    broadcast_in_dim x5 -> x0, local copies, waits for them, and re-layouts: 1.98 us -> none  [the longest x2 1.12 us: on_device(): jnp.broadcast_to(picked[:, :, None], (events, nch, LANES))]
    reshape x2 -> x0, local copies, waits for them, and re-layouts: 1.64 us -> none  [the longest x1 1.53 us: on_device(): flat = archive.reshape(channels, segment)]
    dynamic_slice x2 -> x0, local copies, waits for them, and re-layouts: 1.26 us -> none  [the longest x1 1.2 us: on_device(): lax.dynamic_slice_in_dim(partial, (1 - chan_index) * share, share, axis=1)]
    all_to_all x1, waiting for transfers between devices: 8.13 us -> 7.05 us  [on_device(): lax.all_to_all(payload, 'region', split_axis=0, concat_axis=0, tiled=True)]
  transfers between devices with their start and end apart: 4 -> 4, of which waited for: 4 -> 4; matrix products, arithmetic and copies ran while one was open for 2% -> 3% of each run, Pallas kernels for 0% -> 0%
where the time goes in v2:
time: 58.4 us; the launch traced here: 58 us
  Pallas kernels  16 us (27%)
  waiting for transfers between devices  13 us (22%)
  blocking collectives  12.3 us (21%)
  starting transfers between devices  8.05 us (14%)
  other arithmetic  4.17 us (7%)
  local copies, waits for them, and re-layouts  3.12 us (5%)
  between operations  1.34 us (2%)
    pallas_call x1, Pallas kernels, on_device(): correlate(regions, per_block, pair_cap, segment, slots, nch)  13.8 us
    all_to_all x1, blocking collectives, on_device(): lax.all_to_all(kept.astype(jnp.bfloat16), 'region', split_axis=0, concat_...  12.3 us
    all_to_all x1, waiting for transfers between devices, on_device(): lax.all_to_all(payload, 'region', split_axis=0, concat_axis=0, tiled=True)  7.05 us
    all_to_all x1, starting transfers between devices, on_device(): lax.all_to_all(payload, 'region', split_axis=0, concat_axis=0, tiled=True)  6.35 us
    ppermute x1, waiting for transfers between devices, on_device(): other = lax.ppermute(sent, 'stn', [(i, i ^ step) for i in range(count)])  2.83 us
    unnamed x5, local copies, waits for them, and re-layouts  2.8 us
    pallas_call x1, Pallas kernels, pack(): pl.pallas_call(kernel, out_shape=jax.ShapeDtypeStruct((regions, nch, segm...  2.18 us
    ppermute x1, waiting for transfers between devices, on_device(): kept = kept + lax.ppermute(given, 'chan', swap).astype(jnp.float32)  1.77 us
  transfers between devices with their start and end apart: 4, of which 4 were waited for; matrix products, arithmetic and copies ran while one was open for 3% of the time, Pallas kernels for 0%

profile of v2, /device:TPU:0, one launch (start us, length us, event | category | flops | bytes accessed | tf_op | source)
XLA Modules:
  0.0 58.0 jit_solution(16820697835540826832)
XLA Ops:
  1.3 1.5 %copy.11.mask = s32[256,20]{1,0:T(8,128)} copy(s32[256,20]{0,1:T(8,128)} %param.12) | data formatting | bytes 40960 | tf_op args[3]
  2.8 2.2 %pack.1 = bf16[4,4,9216]{2,1,0:T(4,128)(2,1)} custom-call(bf16[10,3,8192]{2,1,0:T(4,128)(2,1)} %archive.1, s32[1,64]{1,0:T(1,128)} %bitcast.7, s32[256,20]{1,0:T(8,128)} %copy.11.mask, s32[1,512]{1,0:T(1,128)} %bitcast.5, s32[1,512]{1,0:T(1,128)} %bitcast.6, s32[1]{0:T(128)S(6)} %copy.13.count), custom_call_target="tpu_custom_call" | custom-call | tf_op jit(solution)/shard_map/pack/pallas_call | solution.py:104
  5.0 6.3 %all-to-all-start = ((bf16[4,4,9216]{2,1,0:T(4,128)(2,1)}), bf16[4,4,9216]{2,1,0:T(4,128)(2,1)S(1)}, u32[]{:S(2)}, u32[]{:S(2)}) async-start(bf16[4,4,9216]{2,1,0:T(4,128)(2,1)} %pack.1), calls=%async_computation | async-start | bytes 589824 | tf_op jit(solution)/shard_map/all_to_all | solution.py:312
  11.3 0.1 add.50
  11.4 0.0 copy-start.1
  11.4 0.1 add.51
  11.5 0.6 %copy-done.1 = s32[256]{0:T(256)S(1)} copy-done((s32[256]{0:T(256)S(1)}, s32[256]{0:T(256)}, u32[]{:S(2)}) %copy-start.1) | copy-done | bytes 1048
  12.1 0.1 eq.20
  12.1 0.1 fusion.1
  12.2 0.1 reduce_window_sum.11
  12.4 0.2 select_reduce_fusion
  12.6 0.1 reduce_sum.24
  12.7 0.6 %and_select_fusion.station = s32[4]{0:T(128)} fusion(s32[]{:T(128)S(6)} %mul.31, s32[]{:T(128)S(6)} %mul.30, s32[]{:T(128)S(6)} %min.3, s32[]{:T(128)S(6)} %mul.29), kind=kLoop, calls=%fused_computation.11 | loop fusion | flops 60 | bytes 32 | tf_op jit(solution)/shard_map/jit(_where)/select_n | solution.py:318
  13.3 0.6 add_add_fusion
  13.9 7.1 %all-to-all-done.recv = bf16[4,4,9216]{2,1,0:T(4,128)(2,1)S(1)} async-done(((bf16[4,4,9216]{2,1,0:T(4,128)(2,1)}), bf16[4,4,9216]{2,1,0:T(4,128)(2,1)S(1)}, u32[]{:S(2)}, u32[]{:S(2)}) %all-to-all-start) | async-done | bytes 294944 | tf_op jit(solution)/shard_map/all_to_all | solution.py:312
  20.9 0.0 copy-start
  20.9 0.7 %copy-done = bf16[4,4,9216]{2,1,0:T(4,128)(2,1)} copy-done((bf16[4,4,9216]{2,1,0:T(4,128)(2,1)}, bf16[4,4,9216]{2,1,0:T(4,128)(2,1)S(1)}, u32[]{:S(2)}) %copy-start) | copy-done | bytes 294936
  21.6 13.8 %correlate.1 = (f32[4,56,640]{2,1,0:T(8,128)}, bf16[4,56,640]{2,1,0:T(8,128)(2,1)}) custom-call(bf16[4,4,9216]{2,1,0:T(4,128)(2,1)} %copy-done, s32[256,20]{1,0:T(8,128)} %copy.11.mask, s32[4]{0:T(128)} %and_select_fusion.station, s32[1,256]{1,0:T(1,128)} %bitcast.4, bf16[512,512]{1,0:T(8,128)(2,1)} %constant.50.table, bf16[128,512]{1,0:T(8,128)(2,1)} %constant.51.weights), custom_call_target="tpu_custom_call" | custom-call | tf_op jit(solution)/shard_map/correlate/pallas_call | solution.py:320
  35.4 0.1 collective-permute-start
  35.5 1.8 %collective-permute-done = bf16[4,56,640]{2,1,0:T(8,128)(2,1)S(1)} collective-permute-done((bf16[4,56,640]{2,1,0:T(8,128)(2,1)}, bf16[4,56,640]{2,1,0:T(8,128)(2,1)S(1)}, u32[]{:S(2)}, u32[]{:S(2)}) %collective-permute-start) | collective-permute-done | bytes 286752 | tf_op jit(solution)/shard_map/ppermute | solution.py:324
  37.3 1.1 %add_convert_fusion = bf16[4,56,640]{2,1,0:T(8,128)(2,1)S(1)} fusion(f32[4,56,640]{2,1,0:T(8,128)} %get-tuple-element.4, bf16[4,56,640]{2,1,0:T(8,128)(2,1)S(1)} %collective-permute-done), kind=kLoop, calls=%fused_computation | loop fusion | flops 430080 | bytes 1146880 | tf_op jit(solution)/shard_map/convert_element_type | solution.py:325
  38.4 12.3 %all_to_all.10 = bf16[4,56,640]{2,1,0:T(8,128)(2,1)S(1)} all-to-all(bf16[4,56,640]{2,1,0:T(8,128)(2,1)S(1)} %add_convert_fusion), channel_id=1, replica_groups=mesh['groups'=2,'region'=4,'stn'=2,'chan'=2] {'region'}, dimensions={0} | all-to-all | bytes 573440 | tf_op jit(solution)/shard_map/all_to_all | solution.py:325
  50.8 1.6 %collective-permute-start.1 = (bf16[56,640]{1,0:T(8,128)(2,1)S(1)}, bf16[56,640]{1,0:T(8,128)(2,1)S(1)}, u32[]{:S(2)}, u32[]{:S(2)}) collective-permute-start(bf16[56,640]{1,0:T(8,128)(2,1)S(1)} %reduce_sum.25), channel_id=1, source_target_pairs={{0,2},{2,0},{1,3},{3,1},{4,6},{6,4},{5,7},{7,5},{8,10},{10,8},{9,1... | collective-permute-start | bytes 215048 | tf_op jit(solution)/shard_map/ppermute | solution.py:331
  52.3 2.8 %collective-permute-done.1 = bf16[56,640]{1,0:T(8,128)(2,1)S(1)} collective-permute-done((bf16[56,640]{1,0:T(8,128)(2,1)S(1)}, bf16[56,640]{1,0:T(8,128)(2,1)S(1)}, u32[]{:S(2)}, u32[]{:S(2)}) %collective-permute-start.1) | collective-permute-done | bytes 71712 | tf_op jit(solution)/shard_map/ppermute | solution.py:331
  55.2 0.1 collective-permute-start.2
  55.3 1.3 %collective-permute-done.2 = f32[56,640]{1,0:T(8,128)S(1)} collective-permute-done((f32[56,640]{1,0:T(8,128)S(1)}, f32[56,640]{1,0:T(8,128)S(1)}, u32[]{:S(2)}, u32[]{:S(2)}) %collective-permute-start.2) | collective-permute-done | bytes 143392 | tf_op jit(solution)/shard_map/ppermute | solution.py:334
  56.6 0.6 %pad_maximum_fusion = f32[101,128]{1,0:T(8,128)} fusion(f32[56,640]{1,0:T(8,128)S(1)} %get-tuple-element.6, f32[56,640]{1,0:T(8,128)S(1)} %get-tuple-element.7), kind=kLoop, calls=%fused_computation.10 | loop fusion | flops 12928 | bytes 338432 | tf_op jit(solution)/shard_map/concatenate | solution.py:337
  57.3 0.7 %fusion = f32[101,512]{1,0:T(8,128)} fusion(f32[56,640]{1,0:T(8,128)S(1)} %get-tuple-element.7, f32[56,640]{1,0:T(8,128)S(1)} %get-tuple-element.6), kind=kLoop, calls=%fused_computation.3 | loop fusion | flops 51712 | bytes 493568 | tf_op jit(solution)/shard_map/concatenate | solution.py:337
  (4 shorter events, 0.1 us)
Async XLA Ops:
  5.0 16.0 %all-to-all-start = ((bf16[4,4,9216]{2,1,0:T(4,128)(2,1)}), bf16[4,4,9216]{2,1,0:T(4,128)(2,1)S(1)}, u32[]{:S(2)}, u32[]{:S(2)}) async-start(bf16[4,4,9216]{2,1,0:T(4,128)(2,1)} %pack.1), calls=%async_computation | async-start | bytes 589824 | tf_op jit(solution)/shard_map/all_to_all | solution.py:312
  11.4 0.7 %copy-start.1 = (s32[256]{0:T(256)S(1)}, s32[256]{0:T(256)}, u32[]{:S(2)}) copy-start(s32[256]{0:T(256)} %param.11) | copy-start | bytes 3076
  20.9 0.7 %copy-start = (bf16[4,4,9216]{2,1,0:T(4,128)(2,1)}, bf16[4,4,9216]{2,1,0:T(4,128)(2,1)S(1)}, u32[]{:S(2)}) copy-start(bf16[4,4,9216]{2,1,0:T(4,128)(2,1)S(1)} %all-to-all-done.recv) | copy-start | bytes 884740
  35.4 1.8 %collective-permute-start = (bf16[4,56,640]{2,1,0:T(8,128)(2,1)}, bf16[4,56,640]{2,1,0:T(8,128)(2,1)S(1)}, u32[]{:S(2)}, u32[]{:S(2)}) collective-permute-start(bf16[4,56,640]{2,1,0:T(8,128)(2,1)} %get-tuple-element.5), channel_id=1, source_target_pairs={{0,1},{1,0},{2,3},{3,2},{4,5},{5,4},{6,7},{7,6},{8,9},{9,8},{10,11... | collective-permute-start | bytes 860168 | tf_op jit(solution)/shard_map/ppermute | solution.py:324
  50.8 4.4 %collective-permute-start.1 = (bf16[56,640]{1,0:T(8,128)(2,1)S(1)}, bf16[56,640]{1,0:T(8,128)(2,1)S(1)}, u32[]{:S(2)}, u32[]{:S(2)}) collective-permute-start(bf16[56,640]{1,0:T(8,128)(2,1)S(1)} %reduce_sum.25), channel_id=1, source_target_pairs={{0,2},{2,0},{1,3},{3,1},{4,6},{6,4},{5,7},{7,5},{8,10},{10,8},{9,1... | collective-permute-start | bytes 215048 | tf_op jit(solution)/shard_map/ppermute | solution.py:331
  55.2 1.4 %collective-permute-start.2 = (f32[56,640]{1,0:T(8,128)S(1)}, f32[56,640]{1,0:T(8,128)S(1)}, u32[]{:S(2)}, u32[]{:S(2)}) collective-permute-start(f32[56,640]{1,0:T(8,128)S(1)} %convert_add_fusion), channel_id=1, source_target_pairs={{0,1},{1,0},{2,3},{3,2},{4,5},{5,4},{6,7},{7,6},{8,9},{9,8},{10,11... | collective-permute-start | bytes 430088 | tf_op jit(solution)/shard_map/ppermute | solution.py:334

commit v3 on v2

--- a/solution.py
+++ b/solution.py
@@ -43,7 +43,9 @@
     odd[:, 0] = (np.cos(math.pi * (shift[:, 0] % 2)) - 1.0) / NFFT
     table = np.concatenate([even, odd], axis=1) * math.sqrt(WIN)
     table[LAGS:] = 0.0
-    return jnp.asarray(table, jnp.float32).astype(jnp.bfloat16)
+    table = jnp.asarray(table, jnp.float32)
+    high = table.astype(jnp.bfloat16)
+    return jnp.concatenate([high, (table - high.astype(jnp.float32)).astype(jnp.bfloat16)], axis=0)
 
 
 def slot_table(event_owner, regions, per_block, bucket, slots):
@@ -70,7 +72,7 @@
 
 def pack(archive, starts, station_mask, pair_first, pair_second, pair_count, regions, chans, nch):
     stations, _, segment = archive.shape
-    events, listed = station_mask.shape
+    events = station_mask.shape[1]
     per_block = starts.shape[1]
     pair_cap = pair_first.shape[1]
     share = station_share(stations, chans)
@@ -86,7 +88,7 @@
             flat[share * COMP : total - nch, :] = jnp.zeros((total - nch - share * COMP, segment), jnp.float32)
         names = lax.broadcasted_iota(jnp.int32, (events, pair_cap), 0)
         usable = mask[...].astype(jnp.float32).astype(jnp.bfloat16)
-        chosen = [lax.dot_general(usable, as_bf16(names == ref[...]), TN, preferred_element_type=jnp.float32)
+        chosen = [jnp.dot(usable, as_bf16(names == ref[...]), preferred_element_type=jnp.float32)
                   for ref in (first, second)]
         common = jnp.sum(chosen[0] * chosen[1], axis=0, keepdims=True)
         position = lax.broadcasted_iota(jnp.int32, (1, pair_cap), 1)
@@ -107,8 +109,49 @@
         in_specs=[VMEM_ONLY] * 5 + [SMEM_ONLY],
         out_specs=VMEM_ONLY,
         scratch_shapes=[pltpu.VMEM((total, segment), jnp.float32)],
+        compiler_params=pltpu.CompilerParams(
+            vmem_limit_bytes=grant((3 * total + 5 * stations) * segment // LANES + events * pair_cap * 2 // LANES)),
         name="pack",
     )(archive, starts, station_mask, pair_first, pair_second, pair_count)
+
+
+def describe(station_mask, station, slot_of, regions, slots, nch):
+    events = station_mask.shape[1]
+    per_block = events // regions
+
+    def kernel(mask, station, slot_of, slot_event, weight_rows):
+        listed = lax.broadcasted_iota(jnp.int32, (mask.shape[0], LANES), 0)
+        usable = mask[...].astype(jnp.float32).astype(jnp.bfloat16)
+        for c in range(nch):
+            value = lax.dot_general(usable, as_bf16(listed == station[c]), TN, preferred_element_type=jnp.float32)
+            for part in range(regions):
+                row = (part * nch + c) * per_block
+                weight_rows[row : row + per_block, :] = value[part * per_block : (part + 1) * per_block]
+        names = digits_of(lax.broadcasted_iota(jnp.int32, (events, LANES), 0) + 1)
+        place = lax.broadcasted_iota(jnp.int32, (slots, events), 0)
+        slot_lane = slot_of[...]
+
+        def one_region(part, carry):
+            hit = as_bf16(place + part * slots == slot_lane)
+            high, low = (jnp.dot(hit, digit, preferred_element_type=jnp.float32) for digit in names)
+            slot_event[pl.ds(pl.multiple_of(part * slots, slots), slots), :] = high * 128.0 + low - 1.0
+            return carry
+
+        lax.fori_loop(0, regions, one_region, 0)
+
+    return pl.pallas_call(
+        kernel,
+        out_shape=(jax.ShapeDtypeStruct((regions * slots, LANES), jnp.float32),
+                   jax.ShapeDtypeStruct((events * nch, LANES), jnp.float32)),
+        in_specs=[VMEM_ONLY, SMEM_ONLY, VMEM_ONLY],
+        out_specs=(VMEM_ONLY, VMEM_ONLY),
+        compiler_params=pltpu.CompilerParams(vmem_limit_bytes=grant(regions * slots + 2 * events * nch)),
+        name="describe",
+    )(station_mask, station, slot_of)
+
+
+def grant(rows):
+    return min(rows * LANES * 4 * 5 // 4 + (4 << 20), 60 * 1024 * 1024)
 
 
 def correlate(regions, per_block, pair_cap, segment, slots, nch):
@@ -119,14 +162,15 @@
     cols = pair_cap // LANES
     per_row = min(per_block, LANES)
     share = LAG_ROWS // 2
-
-    def kernel(recv, mask, station, slot_of, table, weights, kept, given, shifted, windows, spec, prod, weight_rows,
+    batch = regions if regions <= 4 else 1
+
+    def kernel(recv, slot_event, weight_rows, table, weights, kept, given, shifted, windows, spec, prod,
                index_vmem, index, whole, profile, sem):
         for part in range(regions):
             digits = recv[part, :, segment:].astype(jnp.float32)
             for k in range(2):
                 event = (digits[2 * k : 2 * k + 1, :pair_cap] * 128.0 + digits[2 * k + 1 : 2 * k + 2, :pair_cap])
-                event = event.astype(jnp.int32) * rows
+                event = event.astype(jnp.int32) * (2 * rows)
                 for c in range(cols):
                     row = k * cols + c
                     index_vmem[part, row : row + 1, :] = event[:, c * LANES : (c + 1) * LANES]
@@ -148,11 +192,6 @@
 
         lax.fori_loop(0, regions, widen, 0)
 
-        listed = lax.broadcasted_iota(jnp.int32, (mask.shape[1], LANES), 0)
-        usable = mask[...].astype(jnp.float32).astype(jnp.bfloat16)
-        for c in range(nch):
-            weight_rows[pl.ds(c, events, stride=nch), :] = jnp.dot(
-                usable, as_bf16(listed == station[c]), preferred_element_type=jnp.float32)
         copy.wait()
 
         lane = lax.broadcasted_iota(jnp.int32, (rows, LANES), 1)
@@ -177,7 +216,8 @@
                 some_events(0, 0)
             else:
                 lax.fori_loop(0, per_block // per_row, some_events, 0)
-            pieces = [[windows[t, pl.ds(k, count, stride=2), :] for t in range(2)] for k in range(2)]
+            pieces = [[jnp.concatenate([windows[t, pl.ds(2 * c + k, per_block, stride=rows), :] for c in range(nch)])
+                       for t in range(2)] for k in range(2)]
             squares = pieces[0][0] * pieces[0][0] + pieces[0][1] * pieces[0][1] + pieces[1][0] * pieces[1][0]
             squares += jnp.where(inside, pieces[1][1] * pieces[1][1], 0.0)
             energy = jnp.sum(squares, axis=1, keepdims=True)
@@ -189,8 +229,10 @@
             for s in range(2):
                 for k in range(2):
                     column = s * BINS + k * LANES
-                    piece = (coefs[:, column : column + LANES] * factor).astype(jnp.bfloat16)
-                    spec[s, pl.ds(2 * place + k, count, stride=2), :] = piece.astype(jnp.float32)
+                    piece = (coefs[:, column : column + LANES] * factor).astype(jnp.bfloat16).astype(jnp.float32)
+                    for c in range(nch):
+                        row = 2 * rows * per_block * part + s * rows + 2 * c + k
+                        spec[pl.ds(row, per_block, stride=2 * rows), :] = piece[c * per_block : (c + 1) * per_block]
             return carry
 
         lax.fori_loop(0, regions, one_segment, 0)
@@ -198,60 +240,59 @@
         special = (sublane % 2 == 0) & (lane == 0)
         upper = sublane < nch
         profile[...] = jnp.zeros_like(profile)
-        names = lax.broadcasted_iota(jnp.int32, (events, LANES), 0) + 1
-        name_digits = digits_of(names)
-        slot_lane = slot_of[...]
-        place_of = lax.broadcasted_iota(jnp.int32, (slots, events), 0)
-
-        def names_in(part):
-            hit = as_bf16(place_of + part * slots == slot_lane)
-            high, low = (jnp.dot(hit, digit, preferred_element_type=jnp.float32) for digit in name_digits)
-            return high * 128.0 + low - 1.0
-
-        def one_region(part, carry):
-            def some_pairs(row, inner):
+
+        def one_group(group, carry):
+            def some_pairs(line, inner):
+                part = group * batch + line // cols
+                row = line % cols
                 for step in range(LANES):
-                    a = pl.multiple_of(index[part, row, step], rows)
-                    b = pl.multiple_of(index[part, cols + row, step], rows)
-                    cos_a, sin_a = spec[0, pl.ds(a, rows), :], spec[1, pl.ds(a, rows), :]
-                    cos_b, sin_b = spec[0, pl.ds(b, rows), :], spec[1, pl.ds(b, rows), :]
+                    a = pl.multiple_of(index[part, row, step], 2 * rows)
+                    b = pl.multiple_of(index[part, cols + row, step], 2 * rows)
+                    cos_a, sin_a = spec[pl.ds(a, rows), :], spec[pl.ds(a + rows, rows), :]
+                    cos_b, sin_b = spec[pl.ds(b, rows), :], spec[pl.ds(b + rows, rows), :]
                     sines = sin_a * sin_b
                     even = cos_a * cos_b + sines
                     odd = jnp.where(special, sines, sin_a * cos_b - cos_a * sin_b)
                     even += pltpu.roll(even, nch, 0)
                     odd += pltpu.roll(odd, nch, 0)
-                    both = jnp.where(upper, even, odd)
-                    place = pl.multiple_of((row * LANES + step) * rows, rows)
-                    prod[pl.ds(place, rows), :] = both + pltpu.roll(both, rows - 2, 0)
+                    place = pl.multiple_of((line * LANES + step) * rows, rows)
+                    prod[pl.ds(place, rows), :] = jnp.where(upper, even, odd)
                 return inner
 
-            lax.fori_loop(0, cols, some_pairs, 0)
-            sums = [prod[pl.ds(k, pair_cap, stride=rows), :] for k in (0, 1, nch, nch + 1)]
-            sums = jnp.concatenate(sums, axis=1).astype(jnp.bfloat16)
-            cross = lax.dot_general(weights[...], sums, NT, preferred_element_type=jnp.float32)
-            digits = recv[part, :, segment:].astype(jnp.float32)
-            code = digits[0:1, pair_cap:]
-            live = jnp.maximum((code - 1.0) * COMP, 1.0)
-            stack = cross * jnp.where(code > 0.0, lax.rsqrt(live), 0.0)
-            whole[part, :, :pair_cap] = stack[:LAG_ROWS]
-            first = digits[0:1, :pair_cap] * 128.0 + digits[1:2, :pair_cap]
-            second = digits[2:3, :pair_cap] * 128.0 + digits[3:4, :pair_cap]
-            stack = stack.astype(jnp.bfloat16)
-
-            def gathered(column, event):
-                hot = as_bf16(jnp.concatenate([column] * cols, axis=1) == event)
-                return lax.dot_general(stack, hot, NT, preferred_element_type=jnp.float32)
-
-            own = names_in(part)
-            profile[0, part] += gathered(own, first)
-            profile[1, part] += gathered(own, second)
-
-            @pl.when(part + 1 < regions)
-            def _():
-                profile[1, part + 1] += gathered(names_in(part + 1), second)
+            lax.fori_loop(0, batch * cols, some_pairs, 0)
+            for member in range(batch):
+                part = group * batch + member
+                first_row = member * pair_cap * rows
+                sums = []
+                for k in (0, 1, nch, nch + 1):
+                    total = prod[pl.ds(first_row + k, pair_cap, stride=rows), :]
+                    for c in range(1, nch // 2):
+                        total += prod[pl.ds(first_row + k + 2 * c, pair_cap, stride=rows), :]
+                    sums.append(total.astype(jnp.bfloat16))
+                both = lax.dot_general(weights[...], jnp.concatenate(sums, axis=1), NT,
+                                       preferred_element_type=jnp.float32)
+                cross = both[:LANES] + both[LANES:]
+                digits = recv[part, :, segment:].astype(jnp.float32)
+                code = digits[0:1, pair_cap:]
+                live = jnp.maximum((code - 1.0) * COMP, 1.0)
+                stack = cross * jnp.where(code > 0.0, lax.rsqrt(live), 0.0)
+                whole[part, :, :pair_cap] = stack[:LAG_ROWS]
+                first = digits[0:1, :pair_cap] * 128.0 + digits[1:2, :pair_cap]
+                second = digits[2:3, :pair_cap] * 128.0 + digits[3:4, :pair_cap]
+                stack = stack.astype(jnp.bfloat16)
+
+                def gathered(owner, event):
+                    column = slot_event[pl.ds(pl.multiple_of(owner * slots, slots), slots), :]
+                    hot = as_bf16(jnp.concatenate([column] * cols, axis=1) == event)
+                    return lax.dot_general(stack, hot, NT, preferred_element_type=jnp.float32)
+
+                profile[0, part] += gathered(part, first)
+                profile[1, part] += gathered(part, second)
+                after = (part + 1) % regions
+                profile[1, after] += gathered(after, second)
             return carry
 
-        lax.fori_loop(0, regions, one_region, 0)
+        lax.fori_loop(0, regions // batch, one_group, 0)
         mirror = as_bf16(lax.broadcasted_iota(jnp.int32, (LANES, LANES), 0) + lax.broadcasted_iota(
             jnp.int32, (LANES, LANES), 1) == LAGS - 1)
         chan = lax.axis_index("chan")
@@ -273,23 +314,26 @@
 
     shape = (regions, share, pair_cap + slots)
     index_rows = 8 * -(-(2 * cols + 2) // 8)
+    width = (pair_cap + slots) // LANES
+    used = regions * (tiles * rows + 2 * LAG_ROWS * width + 2 * LANES + index_rows + 4 * tiles + slots)
+    used += (2 * per_block + 2 * events + batch * pair_cap) * rows + events * nch + 2 * NFFT
     return pl.pallas_call(
         kernel,
         out_shape=(jax.ShapeDtypeStruct(shape, jnp.float32), jax.ShapeDtypeStruct(shape, jnp.bfloat16)),
-        in_specs=[VMEM_ONLY, VMEM_ONLY, SMEM_ONLY] + [VMEM_ONLY] * 3,
+        in_specs=[VMEM_ONLY] * 5,
         out_specs=(VMEM_ONLY, VMEM_ONLY),
         scratch_shapes=[
             pltpu.VMEM((regions, tiles, rows, LANES), jnp.float32),
             pltpu.VMEM((2, per_block * rows, LANES), jnp.float32),
-            pltpu.VMEM((2, events * rows, LANES), jnp.float32),
-            pltpu.VMEM((pair_cap * rows, LANES), jnp.float32),
-            pltpu.VMEM((events * nch, LANES), jnp.float32),
+            pltpu.VMEM((2 * events * rows, LANES), jnp.float32),
+            pltpu.VMEM((batch * pair_cap * rows, LANES), jnp.float32),
             pltpu.VMEM((regions, index_rows, LANES), jnp.int32),
             pltpu.SMEM((regions, index_rows, LANES), jnp.int32),
             pltpu.VMEM((regions, LAG_ROWS, pair_cap + slots), jnp.float32),
             pltpu.VMEM((2, regions, LANES, slots), jnp.float32),
             pltpu.SemaphoreType.DMA(()),
         ],
+        compiler_params=pltpu.CompilerParams(vmem_limit_bytes=grant(used)),
         name="correlate",
     )
 
@@ -307,7 +351,8 @@
     share = station_share(stations, chans)
     nch = 4 * -(-share * COMP // (4 * regions))
 
-    payload = pack(archive, starts.reshape(1, -1), station_mask, pair_first.reshape(1, -1),
+    mask = station_mask.T
+    payload = pack(archive, starts.reshape(1, -1), mask, pair_first.reshape(1, -1),
                    pair_second.reshape(1, -1), pair_count, regions, chans, nch)
     received = lax.all_to_all(payload, "region", split_axis=0, concat_axis=0, tiled=True)
 
@@ -317,8 +362,9 @@
     used = (channel < share * COMP) & (local >= chan_index * share)
     station = jnp.where(used, lax.axis_index("stn") * stations + local, -1)
 
+    slot_event, weight_rows = describe(mask, station, slot_of, regions, slots, nch)
     kept, given = correlate(regions, per_block, pair_cap, segment, slots, nch)(
-        received, station_mask, station, slot_of, forward_table(), lag_table())
+        received, slot_event, weight_rows, forward_table(), lag_table())
 
     swap = [(0, 1), (1, 0)]
     kept = kept + lax.ppermute(given, "chan", swap).astype(jnp.float32)

time: 58.4 us -> 53 us (0.908)
  Pallas kernels: 16 us -> 12.9 us
  other arithmetic: 4.17 us -> 1.98 us
  waiting for transfers between devices: 13 us -> 12 us
  local copies, waits for them, and re-layouts: 3.12 us -> 3.81 us
    pallas_call x1, Pallas kernels: 13.8 us -> 10.4 us  [on_device(): correlate(regions, per_block, pair_cap, segment, slots, nch)]
    pallas_call x0 -> x1, Pallas kernels: none -> 1.49 us  [describe(): pl.pallas_call(kernel, out_shape=(jax.ShapeDtypeStruct((regions * slots,...]
    pallas_call x1, Pallas kernels: 2.18 us -> 1.03 us  [pack(): pl.pallas_call(kernel, out_shape=jax.ShapeDtypeStruct((regions, nch, segm...]
    convert_element_type x1, other arithmetic: 1.13 us -> 0.07 us  [on_device(): kept.astype(jnp.bfloat16)]
    all_to_all x1, waiting for transfers between devices: 7.05 us -> 6.28 us  [on_device(): lax.all_to_all(payload, 'region', split_axis=0, concat_axis=0, tiled=True)]
    unnamed x5 -> x18, local copies, waits for them, and re-layouts: 2.8 us -> 3.49 us
  transfers between devices with their start and end apart: 4 -> 4, of which waited for: 4 -> 4; matrix products, arithmetic and copies ran while one was open for 3% -> 2% of each run, Pallas kernels for 0% -> 3%
where the time goes in v3:
time: 53 us; the launch traced here: 52.6 us
  Pallas kernels  12.9 us (24%)
  blocking collectives  12.3 us (23%)
  waiting for transfers between devices  12 us (23%)
  starting transfers between devices  8.17 us (15%)
  local copies, waits for them, and re-layouts  3.81 us (7%)
  other arithmetic  1.98 us (4%)
  between operations  1.39 us (3%)
    all_to_all x1, blocking collectives, on_device(): lax.all_to_all(kept.astype(jnp.bfloat16), 'region', split_axis=0, concat_...  12.3 us
    pallas_call x1, Pallas kernels, on_device(): correlate(regions, per_block, pair_cap, segment, slots, nch)  10.4 us
    all_to_all x1, starting transfers between devices, on_device(): lax.all_to_all(payload, 'region', split_axis=0, concat_axis=0, tiled=True)  6.48 us
    all_to_all x1, waiting for transfers between devices, on_device(): lax.all_to_all(payload, 'region', split_axis=0, concat_axis=0, tiled=True)  6.28 us
    unnamed x18, local copies, waits for them, and re-layouts  3.49 us
    ppermute x1, waiting for transfers between devices, on_device(): other = lax.ppermute(sent, 'stn', [(i, i ^ step) for i in range(count)])  2.84 us
    ppermute x1, waiting for transfers between devices, on_device(): kept = kept + lax.ppermute(given, 'chan', swap).astype(jnp.float32)  1.56 us
    ppermute x1, starting transfers between devices, on_device(): other = lax.ppermute(sent, 'stn', [(i, i ^ step) for i in range(count)])  1.55 us
  transfers between devices with their start and end apart: 4, of which 4 were waited for; matrix products, arithmetic and copies ran while one was open for 2% of the time, Pallas kernels for 3%

profile of v3, /device:TPU:0, one launch (start us, length us, event | category | flops | bytes accessed | tf_op | source)
XLA Modules:
  0.0 52.6 jit_solution(14030341427595094667)
XLA Ops:
  1.3 0.0 copy-start.6
  1.3 0.0 copy-start.5
  1.3 0.0 copy-start.7
  1.3 0.7 %copy-done.6 = s32[512]{0:T(512)S(1)} copy-done((s32[512]{0:T(512)S(1)}, s32[512]{0:T(512)}, u32[]{:S(2)}) %copy-start.6) | copy-done | bytes 2072
  2.0 0.0 copy-done.5
  2.0 0.0 copy-done.7
  2.0 0.0 copy-start
  2.0 1.1 %copy-done = bf16[10,3,8192]{2,1,0:T(4,128)(2,1)S(1)} copy-done((bf16[10,3,8192]{2,1,0:T(4,128)(2,1)S(1)}, bf16[10,3,8192]{2,1,0:T(4,128)(2,1)}, u32[]{:S(2)}) %copy-start) | copy-done | bytes 491544
  3.1 0.0 copy-start.3
  3.1 0.7 %copy-done.3 = s32[256,20]{0,1:T(8,128)S(1)} copy-done((s32[256,20]{0,1:T(8,128)S(1)}, s32[256,20]{0,1:T(8,128)}, u32[]{:S(2)}) %copy-start.3) | copy-done | bytes 20504
  3.8 1.0 %pack.1 = bf16[4,4,9216]{2,1,0:T(4,128)(2,1)} custom-call(bf16[10,3,8192]{2,1,0:T(4,128)(2,1)S(1)} %copy-done, s32[1,64]{1,0:T(1,128)S(1)} %bitcast.10, s32[20,256]{1,0:T(8,128)S(1)} %bitcast.5, s32[1,512]{1,0:T(1,128)S(1)} %bitcast.8, s32[1,512]{1,0:T(1,128)S(1)} %bitcast.9, s32[1]{0:T(128)S(6)} %copy.11.count), custom_call_target="tpu_custom_call" | custom-call | tf_op jit(solution)/shard_map/pack/pallas_call | solution.py:106
  4.8 0.0 copy-start.1
  4.8 6.5 %all-to-all-start = ((bf16[4,4,9216]{2,1,0:T(4,128)(2,1)}), bf16[4,4,9216]{2,1,0:T(4,128)(2,1)S(1)}, u32[]{:S(2)}, u32[]{:S(2)}) async-start(bf16[4,4,9216]{2,1,0:T(4,128)(2,1)} %pack.1), calls=%async_computation | async-start | bytes 589824 | tf_op jit(solution)/shard_map/all_to_all | solution.py:357
  11.3 0.1 add.50
  11.4 0.0 copy-start.8
  11.4 0.1 add.51
  11.5 0.6 %copy-done.8 = s32[256]{0:T(256)S(1)} copy-done((s32[256]{0:T(256)S(1)}, s32[256]{0:T(256)}, u32[]{:S(2)}) %copy-start.8) | copy-done | bytes 1048
  12.1 0.1 eq.20
  12.1 0.0 copy-start.2
  12.2 0.1 fusion.1
  12.3 0.1 reduce_window_sum.11
  12.4 0.0 copy-start.4
  12.4 0.2 select_reduce_fusion
  12.6 0.1 reduce_sum.24
  12.8 0.4 copy-done.4
  13.1 1.5 %describe.1 = (f32[512,128]{1,0:T(8,128)S(1)}, f32[1024,128]{1,0:T(8,128)S(1)}) custom-call(s32[20,256]{1,0:T(8,128)S(1)} %bitcast.6, s32[4]{0:T(128)S(1)} %and_select_fusion.station, s32[1,256]{1,0:T(1,128)S(1)} %bitcast.7), custom_call_target="tpu_custom_call" | custom-call | tf_op jit(solution)/shard_map/describe/pallas_call | solution.py:142
  14.6 6.3 %all-to-all-done.recv = bf16[4,4,9216]{2,1,0:T(4,128)(2,1)S(1)} async-done(((bf16[4,4,9216]{2,1,0:T(4,128)(2,1)}), bf16[4,4,9216]{2,1,0:T(4,128)(2,1)S(1)}, u32[]{:S(2)}, u32[]{:S(2)}) %all-to-all-start) | async-done | bytes 294944 | tf_op jit(solution)/shard_map/all_to_all | solution.py:357
  20.9 0.0 copy-done.1
  20.9 0.0 copy-done.2
  20.9 10.4 %correlate.1 = (f32[4,56,640]{2,1,0:T(8,128)S(1)}, bf16[4,56,640]{2,1,0:T(8,128)(2,1)S(1)}) custom-call(bf16[4,4,9216]{2,1,0:T(4,128)(2,1)S(1)} %all-to-all-done.recv, f32[512,128]{1,0:T(8,128)S(1)} %get-tuple-element.6.slot_event, f32[1024,128]{1,0:T(8,128)S(1)} %get-tuple-element.7.weight_rows, bf16[512,512]{1,0:T(8,128)(2,1)S(1)} %copy-done.1, ...), custom_call_target="tpu_custom_call" | custom-call | tf_op jit(solution)/shard_map/correlate/pallas_call | solution.py:366
  31.3 0.1 collective-permute-start
  31.4 1.6 %collective-permute-done = bf16[4,56,640]{2,1,0:T(8,128)(2,1)S(1)} collective-permute-done((bf16[4,56,640]{2,1,0:T(8,128)(2,1)S(1)}, bf16[4,56,640]{2,1,0:T(8,128)(2,1)S(1)}, u32[]{:S(2)}, u32[]{:S(2)}) %collective-permute-start) | collective-permute-done | bytes 286752 | tf_op jit(solution)/shard_map/ppermute | solution.py:370
  33.0 0.1 add_convert_fusion
  33.0 12.3 %all_to_all.10 = bf16[4,56,640]{2,1,0:T(8,128)(2,1)S(1)} all-to-all(bf16[4,56,640]{2,1,0:T(8,128)(2,1)S(1)} %add_convert_fusion), channel_id=1, replica_groups=mesh['groups'=2,'region'=4,'stn'=2,'chan'=2] {'region'}, dimensions={0} | all-to-all | bytes 573440 | tf_op jit(solution)/shard_map/all_to_all | solution.py:371
  45.4 1.6 %collective-permute-start.1 = (bf16[56,640]{1,0:T(8,128)(2,1)S(1)}, bf16[56,640]{1,0:T(8,128)(2,1)S(1)}, u32[]{:S(2)}, u32[]{:S(2)}) collective-permute-start(bf16[56,640]{1,0:T(8,128)(2,1)S(1)} %reduce_sum.25), channel_id=1, source_target_pairs={{0,2},{2,0},{1,3},{3,1},{4,6},{6,4},{5,7},{7,5},{8,10},{10,8},{9,1... | collective-permute-start | bytes 215048 | tf_op jit(solution)/shard_map/ppermute | solution.py:377
  47.0 2.8 %collective-permute-done.1 = bf16[56,640]{1,0:T(8,128)(2,1)S(1)} collective-permute-done((bf16[56,640]{1,0:T(8,128)(2,1)S(1)}, bf16[56,640]{1,0:T(8,128)(2,1)S(1)}, u32[]{:S(2)}, u32[]{:S(2)}) %collective-permute-start.1) | collective-permute-done | bytes 71712 | tf_op jit(solution)/shard_map/ppermute | solution.py:377
  49.8 0.1 collective-permute-start.2
  49.9 1.3 %collective-permute-done.2 = f32[56,640]{1,0:T(8,128)S(1)} collective-permute-done((f32[56,640]{1,0:T(8,128)S(1)}, f32[56,640]{1,0:T(8,128)S(1)}, u32[]{:S(2)}, u32[]{:S(2)}) %collective-permute-start.2) | collective-permute-done | bytes 143392 | tf_op jit(solution)/shard_map/ppermute | solution.py:380
  51.3 0.6 %pad_maximum_fusion = f32[101,128]{1,0:T(8,128)} fusion(f32[56,640]{1,0:T(8,128)S(1)} %get-tuple-element.10, f32[56,640]{1,0:T(8,128)S(1)} %get-tuple-element.11), kind=kLoop, calls=%fused_computation.10 | loop fusion | flops 12928 | bytes 338432 | tf_op jit(solution)/shard_map/concatenate | solution.py:383
  51.9 0.7 %fusion = f32[101,512]{1,0:T(8,128)} fusion(f32[56,640]{1,0:T(8,128)S(1)} %get-tuple-element.11, f32[56,640]{1,0:T(8,128)S(1)} %get-tuple-element.10), kind=kLoop, calls=%fused_computation.3 | loop fusion | flops 51712 | bytes 493568 | tf_op jit(solution)/shard_map/concatenate | solution.py:383
  (6 shorter events, 0.1 us)
Async XLA Ops:
  1.3 0.7 %copy-start.6 = (s32[512]{0:T(512)S(1)}, s32[512]{0:T(512)}, u32[]{:S(2)}) copy-start(s32[512]{0:T(512)} %param.14) | copy-start | bytes 6148
  1.3 0.7 %copy-start.5 = (s32[512]{0:T(512)S(1)}, s32[512]{0:T(512)}, u32[]{:S(2)}) copy-start(s32[512]{0:T(512)} %param.13) | copy-start | bytes 6148
  1.3 0.7 %copy-start.7 = (s32[64]{0:T(128)S(1)}, s32[64]{0:T(128)}, u32[]{:S(2)}) copy-start(s32[64]{0:T(128)} %param.10) | copy-start | bytes 772
  2.0 1.1 %copy-start = (bf16[10,3,8192]{2,1,0:T(4,128)(2,1)S(1)}, bf16[10,3,8192]{2,1,0:T(4,128)(2,1)}, u32[]{:S(2)}) copy-start(bf16[10,3,8192]{2,1,0:T(4,128)(2,1)} %archive.1) | copy-start | bytes 1474564
  3.1 0.7 %copy-start.3 = (s32[256,20]{0,1:T(8,128)S(1)}, s32[256,20]{0,1:T(8,128)}, u32[]{:S(2)}) copy-start(s32[256,20]{0,1:T(8,128)} %param.12) | copy-start | bytes 61444
  4.8 16.1 %copy-start.1 = (bf16[512,512]{1,0:T(8,128)(2,1)S(1)}, bf16[512,512]{1,0:T(8,128)(2,1)}, u32[]{:S(2)}) copy-start(bf16[512,512]{1,0:T(8,128)(2,1)} %constant.50.table) | copy-start | bytes 1572868
  4.8 16.1 %all-to-all-start = ((bf16[4,4,9216]{2,1,0:T(4,128)(2,1)}), bf16[4,4,9216]{2,1,0:T(4,128)(2,1)S(1)}, u32[]{:S(2)}, u32[]{:S(2)}) async-start(bf16[4,4,9216]{2,1,0:T(4,128)(2,1)} %pack.1), calls=%async_computation | async-start | bytes 589824 | tf_op jit(solution)/shard_map/all_to_all | solution.py:357
  11.4 0.7 %copy-start.8 = (s32[256]{0:T(256)S(1)}, s32[256]{0:T(256)}, u32[]{:S(2)}) copy-start(s32[256]{0:T(256)} %param.11) | copy-start | bytes 3076
  12.1 8.8 %copy-start.2 = (bf16[256,512]{1,0:T(8,128)(2,1)S(1)}, bf16[256,512]{1,0:T(8,128)(2,1)}, u32[]{:S(2)}) copy-start(bf16[256,512]{1,0:T(8,128)(2,1)} %constant.55.weights) | copy-start | bytes 786436
  12.4 0.7 %copy-start.4 = (s32[256,20]{0,1:T(8,128)S(1)}, s32[256,20]{0,1:T(8,128)}, u32[]{:S(2)}) copy-start(s32[256,20]{0,1:T(8,128)} %param.12) | copy-start | bytes 61444
  31.3 1.6 %collective-permute-start = (bf16[4,56,640]{2,1,0:T(8,128)(2,1)S(1)}, bf16[4,56,640]{2,1,0:T(8,128)(2,1)S(1)}, u32[]{:S(2)}, u32[]{:S(2)}) collective-permute-start(bf16[4,56,640]{2,1,0:T(8,128)(2,1)S(1)} %get-tuple-element.9), channel_id=1, source_target_pairs={{0,1},{1,0},{2,3},{3,2},{4,5},{5,4},{6,7},{7,6},{8,9},{9,8},{10,11... | collective-permute-start | bytes 860168 | tf_op jit(solution)/shard_map/ppermute | solution.py:370
  45.4 4.4 %collective-permute-start.1 = (bf16[56,640]{1,0:T(8,128)(2,1)S(1)}, bf16[56,640]{1,0:T(8,128)(2,1)S(1)}, u32[]{:S(2)}, u32[]{:S(2)}) collective-permute-start(bf16[56,640]{1,0:T(8,128)(2,1)S(1)} %reduce_sum.25), channel_id=1, source_target_pairs={{0,2},{2,0},{1,3},{3,1},{4,6},{6,4},{5,7},{7,5},{8,10},{10,8},{9,1... | collective-permute-start | bytes 215048 | tf_op jit(solution)/shard_map/ppermute | solution.py:377
  49.8 1.4 %collective-permute-start.2 = (f32[56,640]{1,0:T(8,128)S(1)}, f32[56,640]{1,0:T(8,128)S(1)}, u32[]{:S(2)}, u32[]{:S(2)}) collective-permute-start(f32[56,640]{1,0:T(8,128)S(1)} %convert_add_fusion), channel_id=1, source_target_pairs={{0,1},{1,0},{2,3},{3,2},{4,5},{5,4},{6,7},{7,6},{8,9},{9,8},{10,11... | collective-permute-start | bytes 430088 | tf_op jit(solution)/shard_map/ppermute | solution.py:380

commit v4 on v3

--- a/solution.py
+++ b/solution.py
@@ -16,6 +16,7 @@
 BINS = NFFT // 2
 LANES = 128
 LAG_ROWS = 112
+HALF_ROWS = LAG_ROWS // 2
 VMEM_ONLY = pl.BlockSpec(memory_space=pltpu.VMEM)
 SMEM_ONLY = pl.BlockSpec(memory_space=pltpu.SMEM)
 NT = (((1,), (1,)), ((), ()))
@@ -34,7 +35,7 @@
 
 
 def lag_table():
-    shift = np.arange(LANES)[:, None] - MAXLAG
+    shift = np.arange(LAG_ROWS)[:, None] - MAXLAG
     freq = np.arange(BINS)[None, :]
     angle = (freq * shift % NFFT) * (2.0 * math.pi / NFFT)
     weight = np.where(freq == 0, 1.0 / NFFT, 2.0 / NFFT)
@@ -43,9 +44,12 @@
     odd[:, 0] = (np.cos(math.pi * (shift[:, 0] % 2)) - 1.0) / NFFT
     table = np.concatenate([even, odd], axis=1) * math.sqrt(WIN)
     table[LAGS:] = 0.0
+    filler = np.zeros((LANES - LAG_ROWS, NFFT))
+    halves = table[:HALF_ROWS], table[HALF_ROWS:]
+    table = np.stack([np.concatenate([halves[c], halves[1 - c], filler]) for c in range(2)])
     table = jnp.asarray(table, jnp.float32)
     high = table.astype(jnp.bfloat16)
-    return jnp.concatenate([high, (table - high.astype(jnp.float32)).astype(jnp.bfloat16)], axis=0)
+    return jnp.concatenate([high, (table - high.astype(jnp.float32)).astype(jnp.bfloat16)], axis=1)
 
 
 def slot_table(event_owner, regions, per_block, bucket, slots):
@@ -64,6 +68,14 @@
 
 def digits_of(value):
     return (value >> 7).astype(jnp.float32).astype(jnp.bfloat16), (value & 127).astype(jnp.float32).astype(jnp.bfloat16)
+
+
+def digit_count(events):
+    return 1 if events <= 256 else 2
+
+
+def field_width(events, pair_cap):
+    return -(-(2 * digit_count(events) + 2) // 4) * pair_cap
 
 
 def station_share(stations, chans):
@@ -94,23 +106,27 @@
         position = lax.broadcasted_iota(jnp.int32, (1, pair_cap), 1)
         code = jnp.where(position < count[0], common + 1.0, 0.0).astype(jnp.bfloat16)
         offset = digits_of(starts[...] - lax.axis_index("region") * segment)
-        rows = digits_of(first[...]) + digits_of(second[...])
+        used = [jnp.full((1, per_block), digit, jnp.int32) for digit in (count[0] >> 7, count[0] & 127)]
+        used = [digit.astype(jnp.float32).astype(jnp.bfloat16) for digit in used]
+        rest = jnp.zeros((1, pair_cap - 4 * per_block), jnp.bfloat16)
+        scalars = jnp.concatenate(list(offset) + used + [rest], axis=1)
+        if digit_count(events) == 1:
+            fields = [first[...].astype(jnp.float32).astype(jnp.bfloat16), second[...].astype(jnp.float32).astype(jnp.bfloat16)]
+        else:
+            fields = list(digits_of(first[...]) + digits_of(second[...]))
+        fields += [code, scalars]
         for part in range(regions):
             out[part, :, :segment] = flat[pl.ds(part * nch, nch), :].astype(jnp.bfloat16)
-            for k in range(4):
-                out[part, k : k + 1, segment : segment + pair_cap] = rows[k]
-            out[part, 0:1, segment + pair_cap :] = code
-            out[part, 1:2, segment + pair_cap : segment + pair_cap + per_block] = offset[0]
-            out[part, 2:3, segment + pair_cap : segment + pair_cap + per_block] = offset[1]
+            for k, field in enumerate(fields):
+                lane = segment + k // 4 * pair_cap
+                out[part, k % 4 : k % 4 + 1, lane : lane + pair_cap] = field
 
     return pl.pallas_call(
         kernel,
-        out_shape=jax.ShapeDtypeStruct((regions, nch, segment + 2 * pair_cap), jnp.bfloat16),
+        out_shape=jax.ShapeDtypeStruct((regions, nch, segment + field_width(events, pair_cap)), jnp.bfloat16),
         in_specs=[VMEM_ONLY] * 5 + [SMEM_ONLY],
         out_specs=VMEM_ONLY,
         scratch_shapes=[pltpu.VMEM((total, segment), jnp.float32)],
-        compiler_params=pltpu.CompilerParams(
-            vmem_limit_bytes=grant((3 * total + 5 * stations) * segment // LANES + events * pair_cap * 2 // LANES)),
         name="pack",
     )(archive, starts, station_mask, pair_first, pair_second, pair_count)
 
@@ -161,23 +177,29 @@
     half = 2 * LANES
     cols = pair_cap // LANES
     per_row = min(per_block, LANES)
-    share = LAG_ROWS // 2
     batch = regions if regions <= 4 else 1
+    digits = digit_count(events)
 
     def kernel(recv, slot_event, weight_rows, table, weights, kept, given, shifted, windows, spec, prod,
-               index_vmem, index, whole, profile, sem):
+               index_vmem, index, profile, sem):
+        def field(part, k):
+            lane = segment + k // 4 * pair_cap
+            return recv[part, :, lane : lane + pair_cap].astype(jnp.float32)[k % 4 : k % 4 + 1]
+
+        def listed(part, k):
+            if digits == 1:
+                return field(part, k)
+            return field(part, 2 * k) * 128.0 + field(part, 2 * k + 1)
+
         for part in range(regions):
-            digits = recv[part, :, segment:].astype(jnp.float32)
+            rows_out = []
             for k in range(2):
-                event = (digits[2 * k : 2 * k + 1, :pair_cap] * 128.0 + digits[2 * k + 1 : 2 * k + 2, :pair_cap])
-                event = event.astype(jnp.int32) * (2 * rows)
-                for c in range(cols):
-                    row = k * cols + c
-                    index_vmem[part, row : row + 1, :] = event[:, c * LANES : (c + 1) * LANES]
-            for k in range(2):
-                row = 2 * cols + k
-                digit = digits[k + 1 : k + 2, pair_cap : pair_cap + LANES]
-                index_vmem[part, row : row + 1, :] = digit.astype(jnp.int32)
+                event = listed(part, k).astype(jnp.int32) * (2 * rows)
+                rows_out += [event[:, c * LANES : (c + 1) * LANES] for c in range(cols)]
+            scalars = field(part, 2 * digits + 1).astype(jnp.int32)
+            rows_out += [scalars[:, c * LANES : (c + 1) * LANES] for c in range(2)]
+            for row, value in enumerate(rows_out):
+                index_vmem[part, row : row + 1, :] = value
         copy = pltpu.make_async_copy(index_vmem, index, sem)
         copy.start()
 
@@ -199,24 +221,17 @@
         count = per_block * nch
         inside = lax.broadcasted_iota(jnp.int32, (count, LANES), 1) < WIN - half - LANES
 
-        def one_segment(part, carry):
-            def some_events(group, inner):
-                for step in range(per_row):
-                    base = index[part, 2 * cols, group * per_row + step]
-                    off = index[part, 2 * cols + 1, group * per_row + step]
-                    turn = (LANES - off) & (LANES - 1)
-                    data = [shifted[part, base + k] for k in range(3)]
-                    later = lane >= off
-                    row = pl.multiple_of((group * per_row + step) * rows, rows)
-                    windows[0, pl.ds(row, rows), :] = pltpu.roll(jnp.where(later, data[0], data[1]), turn, 1)
-                    windows[1, pl.ds(row, rows), :] = pltpu.roll(jnp.where(later, data[1], data[2]), turn, 1)
-                return inner
-
-            if per_block == per_row:
-                some_events(0, 0)
-            else:
-                lax.fori_loop(0, per_block // per_row, some_events, 0)
-            pieces = [[jnp.concatenate([windows[t, pl.ds(2 * c + k, per_block, stride=rows), :] for c in range(nch)])
+        def one_segment(part, slot):
+            for event in range(per_block):
+                base = index[part, 2 * cols, event]
+                off = index[part, 2 * cols, per_block + event]
+                turn = (LANES - off) & (LANES - 1)
+                data = [shifted[part, base + k] for k in range(3)]
+                later = lane >= off
+                row = event * rows
+                windows[slot, 0, row : row + rows, :] = pltpu.roll(jnp.where(later, data[0], data[1]), turn, 1)
+                windows[slot, 1, row : row + rows, :] = pltpu.roll(jnp.where(later, data[1], data[2]), turn, 1)
+            pieces = [[jnp.concatenate([windows[slot, t, pl.ds(2 * c + k, per_block, stride=rows), :] for c in range(nch)])
                        for t in range(2)] for k in range(2)]
             squares = pieces[0][0] * pieces[0][0] + pieces[0][1] * pieces[0][1] + pieces[1][0] * pieces[1][0]
             squares += jnp.where(inside, pieces[1][1] * pieces[1][1], 0.0)
@@ -224,7 +239,7 @@
             early, late = (jnp.concatenate(piece, axis=1).astype(jnp.bfloat16) for piece in pieces)
             coefs = jnp.dot(early, table[:half, :], preferred_element_type=jnp.float32)
             coefs += jnp.dot(late, table[half:, :], preferred_element_type=jnp.float32)
-            place = pl.multiple_of(part * count, count)
+            place = part * count if batch == regions else pl.multiple_of(part * count, count)
             factor = weight_rows[pl.ds(place, count), :] * lax.rsqrt(energy + WIN * 1e-05)
             for s in range(2):
                 for k in range(2):
@@ -233,18 +248,25 @@
                     for c in range(nch):
                         row = 2 * rows * per_block * part + s * rows + 2 * c + k
                         spec[pl.ds(row, per_block, stride=2 * rows), :] = piece[c * per_block : (c + 1) * per_block]
+
+        def looped_segment(part, carry):
+            one_segment(part, 0)
             return carry
 
-        lax.fori_loop(0, regions, one_segment, 0)
-
+        if batch == regions:
+            for part in range(regions):
+                one_segment(part, part)
+        else:
+            lax.fori_loop(0, regions, looped_segment, 0)
+
+        chan = lax.axis_index("chan")
         special = (sublane % 2 == 0) & (lane == 0)
         upper = sublane < nch
         profile[...] = jnp.zeros_like(profile)
 
         def one_group(group, carry):
-            def some_pairs(line, inner):
-                part = group * batch + line // cols
-                row = line % cols
+            def some_pairs(member, row):
+                part = group * batch + member
                 for step in range(LANES):
                     a = pl.multiple_of(index[part, row, step], 2 * rows)
                     b = pl.multiple_of(index[part, cols + row, step], 2 * rows)
@@ -255,11 +277,18 @@
                     odd = jnp.where(special, sines, sin_a * cos_b - cos_a * sin_b)
                     even += pltpu.roll(even, nch, 0)
                     odd += pltpu.roll(odd, nch, 0)
-                    place = pl.multiple_of((line * LANES + step) * rows, rows)
+                    place = pl.multiple_of(((member * cols + row) * LANES + step) * rows, rows)
                     prod[pl.ds(place, rows), :] = jnp.where(upper, even, odd)
+                return member
+
+            def pairs_of(member, inner):
+                part = group * batch + member
+                pairs = index[part, 2 * cols + 1, 0] * LANES + index[part, 2 * cols + 1, per_block]
+                lax.fori_loop(0, jnp.minimum((pairs + LANES - 1) // LANES, cols), lambda row, m: some_pairs(m, row),
+                              member)
                 return inner
 
-            lax.fori_loop(0, batch * cols, some_pairs, 0)
+            lax.fori_loop(0, batch, pairs_of, 0)
             for member in range(batch):
                 part = group * batch + member
                 first_row = member * pair_cap * rows
@@ -269,16 +298,15 @@
                     for c in range(1, nch // 2):
                         total += prod[pl.ds(first_row + k + 2 * c, pair_cap, stride=rows), :]
                     sums.append(total.astype(jnp.bfloat16))
-                both = lax.dot_general(weights[...], jnp.concatenate(sums, axis=1), NT,
+                both = lax.dot_general(weights[chan], jnp.concatenate(sums, axis=1), NT,
                                        preferred_element_type=jnp.float32)
                 cross = both[:LANES] + both[LANES:]
-                digits = recv[part, :, segment:].astype(jnp.float32)
-                code = digits[0:1, pair_cap:]
+                code = field(part, 2 * digits)
                 live = jnp.maximum((code - 1.0) * COMP, 1.0)
-                stack = cross * jnp.where(code > 0.0, lax.rsqrt(live), 0.0)
-                whole[part, :, :pair_cap] = stack[:LAG_ROWS]
-                first = digits[0:1, :pair_cap] * 128.0 + digits[1:2, :pair_cap]
-                second = digits[2:3, :pair_cap] * 128.0 + digits[3:4, :pair_cap]
+                stack = jnp.where(code > 0.0, cross * lax.rsqrt(live), 0.0)
+                kept[part, :, :pair_cap] = stack[:HALF_ROWS]
+                given[part, :, :pair_cap] = stack[HALF_ROWS:LAG_ROWS].astype(jnp.bfloat16)
+                first, second = listed(part, 0), listed(part, 1)
                 stack = stack.astype(jnp.bfloat16)
 
                 def gathered(owner, event):
@@ -293,11 +321,11 @@
             return carry
 
         lax.fori_loop(0, regions // batch, one_group, 0)
-        mirror = as_bf16(lax.broadcasted_iota(jnp.int32, (LANES, LANES), 0) + lax.broadcasted_iota(
-            jnp.int32, (LANES, LANES), 1) == LAGS - 1)
-        chan = lax.axis_index("chan")
-        mine = pl.multiple_of(chan * share, 8)
-        theirs = pl.multiple_of((1 - chan) * share, 8)
+        def lag_of(axis):
+            row = lax.broadcasted_iota(jnp.int32, (LANES, LANES), axis)
+            return jnp.where(row < HALF_ROWS, row + chan * HALF_ROWS, row - chan * HALF_ROWS)
+
+        mirror = as_bf16(lag_of(0) + lag_of(1) == LAGS - 1)
 
         def finish(part, carry):
             value = profile[1, part]
@@ -305,18 +333,18 @@
             low = (value - high.astype(jnp.float32)).astype(jnp.bfloat16)
             flipped = jnp.dot(mirror, high, preferred_element_type=jnp.float32) + jnp.dot(
                 mirror, low, preferred_element_type=jnp.float32)
-            whole[part, :, pair_cap:] = (profile[0, part] + flipped)[:LAG_ROWS]
-            kept[part] = whole[part, pl.ds(mine, share), :]
-            given[part] = whole[part, pl.ds(theirs, share), :].astype(jnp.bfloat16)
+            total = profile[0, part] + flipped
+            kept[part, :, pair_cap:] = total[:HALF_ROWS]
+            given[part, :, pair_cap:] = total[HALF_ROWS:LAG_ROWS].astype(jnp.bfloat16)
             return carry
 
         lax.fori_loop(0, regions, finish, 0)
 
-    shape = (regions, share, pair_cap + slots)
+    shape = (regions, HALF_ROWS, pair_cap + slots)
     index_rows = 8 * -(-(2 * cols + 2) // 8)
     width = (pair_cap + slots) // LANES
-    used = regions * (tiles * rows + 2 * LAG_ROWS * width + 2 * LANES + index_rows + 4 * tiles + slots)
-    used += (2 * per_block + 2 * events + batch * pair_cap) * rows + events * nch + 2 * NFFT
+    used = regions * (tiles * rows + LAG_ROWS * width + 2 * LANES + index_rows + 4 * tiles + slots)
+    used += (2 * per_block * batch + 2 * events + batch * pair_cap) * rows + events * nch + 3 * NFFT
     return pl.pallas_call(
         kernel,
         out_shape=(jax.ShapeDtypeStruct(shape, jnp.float32), jax.ShapeDtypeStruct(shape, jnp.bfloat16)),
@@ -324,12 +352,11 @@
         out_specs=(VMEM_ONLY, VMEM_ONLY),
         scratch_shapes=[
             pltpu.VMEM((regions, tiles, rows, LANES), jnp.float32),
-            pltpu.VMEM((2, per_block * rows, LANES), jnp.float32),
+            pltpu.VMEM((batch, 2, per_block * rows, LANES), jnp.float32),
             pltpu.VMEM((2 * events * rows, LANES), jnp.float32),
             pltpu.VMEM((batch * pair_cap * rows, LANES), jnp.float32),
             pltpu.VMEM((regions, index_rows, LANES), jnp.int32),
             pltpu.SMEM((regions, index_rows, LANES), jnp.int32),
-            pltpu.VMEM((regions, LAG_ROWS, pair_cap + slots), jnp.float32),
             pltpu.VMEM((2, regions, LANES, slots), jnp.float32),
             pltpu.SemaphoreType.DMA(()),
         ],
@@ -369,7 +396,10 @@
     swap = [(0, 1), (1, 0)]
     kept = kept + lax.ppermute(given, "chan", swap).astype(jnp.float32)
     spread = lax.all_to_all(kept.astype(jnp.bfloat16), "region", split_axis=0, concat_axis=0, tiled=True)
-    whole = jnp.sum(spread.astype(jnp.float32), axis=0)
+    here = lax.axis_index("region")
+    whole = lax.optimization_barrier(lax.dynamic_index_in_dim(kept, here, keepdims=False))
+    others = jnp.arange(regions, dtype=jnp.int32) != here
+    whole = whole + jnp.sum(jnp.where(others[:, None, None], spread.astype(jnp.float32), 0.0), axis=0)
     count = lax.axis_size("stn")
     step = 1
     while step < count:

time: 53 us -> 51.7 us (0.975)
  blocking collectives: 12.3 us -> 0 us
  waiting for transfers between devices: 12 us -> 22.3 us
  starting transfers between devices: 8.17 us -> 11.6 us
  local copies, waits for them, and re-layouts: 3.81 us -> 0.58 us
  other arithmetic: 1.98 us -> 2.79 us
    all_to_all x1 -> x0, blocking collectives: 12.3 us -> none  [on_device(): lax.all_to_all(kept.astype(jnp.bfloat16), 'region', split_axis=0, concat_...]
    all_to_all x0 -> x1, waiting for transfers between devices: none -> 9.9 us  [on_device(): lax.all_to_all(kept.astype(jnp.bfloat16), 'region', split_axis=0, concat_...]
    all_to_all x0 -> x1, starting transfers between devices: none -> 3.45 us  [on_device(): lax.all_to_all(kept.astype(jnp.bfloat16), 'region', split_axis=0, concat_...]
    unnamed x18 -> x8, local copies, waits for them, and re-layouts: 3.49 us -> 0.24 us
    pallas_call x1, Pallas kernels: 10.4 us -> 8.94 us  [on_device(): correlate(regions, per_block, pair_cap, segment, slots, nch)]
    pallas_call x1, Pallas kernels: 1.03 us -> 2.13 us  [pack(): pl.pallas_call(kernel, out_shape=jax.ShapeDtypeStruct((regions, nch, segm...]
    convert_element_type x1, other arithmetic: 0.07 us -> 0.78 us  [on_device(): kept.astype(jnp.bfloat16)]
  transfers between devices with their start and end apart: 4 -> 5, of which waited for: 4 -> 5; matrix products, arithmetic and copies ran while one was open for 2% -> 2% of each run, Pallas kernels for 3% -> 3%
where the time goes in v4:
time: 51.7 us; the launch traced here: 51.3 us
  waiting for transfers between devices  22.3 us (43%)
  Pallas kernels  12.6 us (24%)
  starting transfers between devices  11.6 us (22%)
  other arithmetic  2.79 us (5%)
  between operations  1.4 us (3%)
  local copies, waits for them, and re-layouts  0.58 us (1%)
    all_to_all x1, waiting for transfers between devices, on_device(): lax.all_to_all(kept.astype(jnp.bfloat16), 'region', split_axis=0, concat_...  9.9 us
    pallas_call x1, Pallas kernels, on_device(): correlate(regions, per_block, pair_cap, segment, slots, nch)  8.94 us
    all_to_all x1, waiting for transfers between devices, on_device(): lax.all_to_all(payload, 'region', split_axis=0, concat_axis=0, tiled=True)  6.69 us
    all_to_all x1, starting transfers between devices, on_device(): lax.all_to_all(payload, 'region', split_axis=0, concat_axis=0, tiled=True)  6.48 us
    all_to_all x1, starting transfers between devices, on_device(): lax.all_to_all(kept.astype(jnp.bfloat16), 'region', split_axis=0, concat_...  3.45 us
    ppermute x1, waiting for transfers between devices, on_device(): other = lax.ppermute(sent, 'stn', [(i, i ^ step) for i in range(count)])  2.85 us
    pallas_call x1, Pallas kernels, pack(): pl.pallas_call(kernel, out_shape=jax.ShapeDtypeStruct((regions, nch, segm...  2.13 us
    ppermute x1, waiting for transfers between devices, on_device(): kept = kept + lax.ppermute(given, 'chan', swap).astype(jnp.float32)  1.56 us
  transfers between devices with their start and end apart: 5, of which 5 were waited for; matrix products, arithmetic and copies ran while one was open for 2% of the time, Pallas kernels for 3%

profile of v4, /device:TPU:0, one launch (start us, length us, event | category | flops | bytes accessed | tf_op | source)
XLA Modules:
  0.0 51.3 jit_solution(3052171286330837221)
XLA Ops:
  1.3 0.0 copy-start.3
  1.3 2.1 %pack.1 = bf16[4,4,8704]{2,1,0:T(4,128)(2,1)} custom-call(bf16[10,3,8192]{2,1,0:T(4,128)(2,1)} %archive.1, s32[1,64]{1,0:T(1,128)} %bitcast.12, s32[20,256]{1,0:T(8,128)} %bitcast.7, s32[1,512]{1,0:T(1,128)} %bitcast.10, s32[1,512]{1,0:T(1,128)} %bitcast.11, s32[1]{0:T(128)S(6)} %copy.11.count), custom_call_target="tpu_custom_call" | custom-call | tf_op jit(solution)/shard_map/pack/pallas_call | solution.py:124
  3.4 0.0 copy-start
  3.4 0.0 copy-start.1
  3.4 6.5 %all-to-all-start = ((bf16[4,4,8704]{2,1,0:T(4,128)(2,1)}), bf16[4,4,8704]{2,1,0:T(4,128)(2,1)S(1)}, u32[]{:S(2)}, u32[]{:S(2)}) async-start(bf16[4,4,8704]{2,1,0:T(4,128)(2,1)} %pack.1), calls=%async_computation | async-start | bytes 557056 | tf_op jit(solution)/shard_map/all_to_all | solution.py:384
  9.9 0.0 copy-done.3
  9.9 0.1 eq.20
  10.0 0.1 fusion.1
  10.1 0.1 reduce_window_sum.11
  10.2 0.0 copy-start.2
  10.2 0.2 select_reduce_fusion.1
  10.5 0.1 reduce_sum.21
  10.6 0.1 add.57
  10.6 0.1 add.58
  10.8 0.2 copy-done.2
  11.0 1.5 %describe.1 = (f32[512,128]{1,0:T(8,128)S(1)}, f32[1024,128]{1,0:T(8,128)S(1)}) custom-call(s32[20,256]{1,0:T(8,128)S(1)} %bitcast.8, s32[4]{0:T(128)S(1)} %and_select_fusion.station, s32[1,256]{1,0:T(1,128)S(1)} %bitcast.9), custom_call_target="tpu_custom_call" | custom-call | tf_op jit(solution)/shard_map/describe/pallas_call | solution.py:158
  12.5 6.7 %all-to-all-done.recv = bf16[4,4,8704]{2,1,0:T(4,128)(2,1)S(1)} async-done(((bf16[4,4,8704]{2,1,0:T(4,128)(2,1)}), bf16[4,4,8704]{2,1,0:T(4,128)(2,1)S(1)}, u32[]{:S(2)}, u32[]{:S(2)}) %all-to-all-start) | async-done | bytes 278560 | tf_op jit(solution)/shard_map/all_to_all | solution.py:384
  19.2 0.0 copy-done
  19.2 0.0 copy-done.1
  19.2 8.9 %correlate.1 = (f32[4,56,640]{2,1,0:T(8,128)S(1)}, bf16[4,56,640]{2,1,0:T(8,128)(2,1)S(1)}) custom-call(bf16[4,4,8704]{2,1,0:T(4,128)(2,1)S(1)} %all-to-all-done.recv, f32[512,128]{1,0:T(8,128)S(1)} %get-tuple-element.6.slot_event, f32[1024,128]{1,0:T(8,128)S(1)} %get-tuple-element.7.weight_rows, bf16[512,512]{1,0:T(8,128)(2,1)S(1)} %copy-done, ...), custom_call_target="tpu_custom_call" | custom-call | tf_op jit(solution)/shard_map/correlate/pallas_call | solution.py:393
  28.1 0.1 collective-permute-start
  28.2 1.6 %collective-permute-done = bf16[4,56,640]{2,1,0:T(8,128)(2,1)S(1)} collective-permute-done((bf16[4,56,640]{2,1,0:T(8,128)(2,1)S(1)}, bf16[4,56,640]{2,1,0:T(8,128)(2,1)S(1)}, u32[]{:S(2)}, u32[]{:S(2)}) %collective-permute-start) | collective-permute-done | bytes 286752 | tf_op jit(solution)/shard_map/ppermute | solution.py:397
  29.8 0.8 %fusion.2 = (bf16[4,56,640]{2,1,0:T(8,128)(2,1)}, f32[4,56,640]{2,1,0:T(8,128)S(1)}) fusion(f32[4,56,640]{2,1,0:T(8,128)S(1)} %get-tuple-element.8, bf16[4,56,640]{2,1,0:T(8,128)(2,1)S(1)} %collective-permute-done), kind=kLoop, calls=%fused_computation.19 | loop fusion | flops 430080 | bytes 1720320 | tf_op jit(solution)/shard_map/convert_element_type | solution.py:398
  30.5 3.4 %all-to-all-start.1 = ((bf16[4,56,640]{2,1,0:T(8,128)(2,1)}), bf16[4,56,640]{2,1,0:T(8,128)(2,1)S(1)}, u32[]{:S(2)}, u32[]{:S(2)}) async-start(bf16[4,56,640]{2,1,0:T(8,128)(2,1)} %get-tuple-element.10), calls=%async_computation.1 | async-start | bytes 573440 | tf_op jit(solution)/shard_map/all_to_all | solution.py:398
  34.0 9.9 %all-to-all-done.1 = bf16[4,56,640]{2,1,0:T(8,128)(2,1)S(1)} async-done(((bf16[4,56,640]{2,1,0:T(8,128)(2,1)}), bf16[4,56,640]{2,1,0:T(8,128)(2,1)S(1)}, u32[]{:S(2)}, u32[]{:S(2)}) %all-to-all-start.1) | async-done | bytes 286752 | tf_op jit(solution)/shard_map/all_to_all | solution.py:398
  43.9 0.1 select_reduce_fusion
  44.1 1.5 %collective-permute-start.1 = (bf16[56,640]{1,0:T(8,128)(2,1)S(1)}, bf16[56,640]{1,0:T(8,128)(2,1)S(1)}, u32[]{:S(2)}, u32[]{:S(2)}) collective-permute-start(bf16[56,640]{1,0:T(8,128)(2,1)S(1)} %add_convert_fusion), channel_id=1, source_target_pairs={{0,2},{2,0},{1,3},{3,1},{4,6},{6,4},{5,7},{7,5},{8,10},{10,8},{9,1... | collective-permute-start | bytes 215048 | tf_op jit(solution)/shard_map/ppermute | solution.py:407
  45.6 2.9 %collective-permute-done.1 = bf16[56,640]{1,0:T(8,128)(2,1)S(1)} collective-permute-done((bf16[56,640]{1,0:T(8,128)(2,1)S(1)}, bf16[56,640]{1,0:T(8,128)(2,1)S(1)}, u32[]{:S(2)}, u32[]{:S(2)}) %collective-permute-start.1) | collective-permute-done | bytes 71712 | tf_op jit(solution)/shard_map/ppermute | solution.py:407
  48.5 0.1 collective-permute-start.2
  48.6 1.3 %collective-permute-done.2 = f32[56,640]{1,0:T(8,128)S(1)} collective-permute-done((f32[56,640]{1,0:T(8,128)S(1)}, f32[56,640]{1,0:T(8,128)S(1)}, u32[]{:S(2)}, u32[]{:S(2)}) %collective-permute-start.2) | collective-permute-done | bytes 143392 | tf_op jit(solution)/shard_map/ppermute | solution.py:410
  50.0 0.6 %pad_maximum_fusion = f32[101,128]{1,0:T(8,128)} fusion(f32[56,640]{1,0:T(8,128)S(1)} %get-tuple-element.12, f32[56,640]{1,0:T(8,128)S(1)} %get-tuple-element.13), kind=kLoop, calls=%fused_computation.13 | loop fusion | flops 12928 | bytes 338432 | tf_op jit(solution)/shard_map/concatenate | solution.py:413
  50.6 0.7 %fusion = f32[101,512]{1,0:T(8,128)} fusion(f32[56,640]{1,0:T(8,128)S(1)} %get-tuple-element.13, f32[56,640]{1,0:T(8,128)S(1)} %get-tuple-element.12), kind=kLoop, calls=%fused_computation.4 | loop fusion | flops 51712 | bytes 493568 | tf_op jit(solution)/shard_map/concatenate | solution.py:413
  (8 shorter events, 0.1 us)
Async XLA Ops:
  1.3 8.6 %copy-start.3 = (s32[256]{0:T(256)S(1)}, s32[256]{0:T(256)}, u32[]{:S(2)}) copy-start(s32[256]{0:T(256)} %param.11) | copy-start | bytes 3076
  3.4 15.7 %copy-start = (bf16[512,512]{1,0:T(8,128)(2,1)S(1)}, bf16[512,512]{1,0:T(8,128)(2,1)}, u32[]{:S(2)}) copy-start(bf16[512,512]{1,0:T(8,128)(2,1)} %constant.53.table) | copy-start | bytes 1572868
  3.4 15.7 %copy-start.1 = (bf16[2,256,512]{2,1,0:T(8,128)(2,1)S(1)}, bf16[2,256,512]{2,1,0:T(8,128)(2,1)}, u32[]{:S(2)}) copy-start(bf16[2,256,512]{2,1,0:T(8,128)(2,1)} %constant.58.weights) | copy-start | bytes 1572868
  3.4 15.7 %all-to-all-start = ((bf16[4,4,8704]{2,1,0:T(4,128)(2,1)}), bf16[4,4,8704]{2,1,0:T(4,128)(2,1)S(1)}, u32[]{:S(2)}, u32[]{:S(2)}) async-start(bf16[4,4,8704]{2,1,0:T(4,128)(2,1)} %pack.1), calls=%async_computation | async-start | bytes 557056 | tf_op jit(solution)/shard_map/all_to_all | solution.py:384
  10.2 0.7 %copy-start.2 = (s32[256,20]{0,1:T(8,128)S(1)}, s32[256,20]{0,1:T(8,128)}, u32[]{:S(2)}) copy-start(s32[256,20]{0,1:T(8,128)} %param.12) | copy-start | bytes 61444
  28.1 1.6 %collective-permute-start = (bf16[4,56,640]{2,1,0:T(8,128)(2,1)S(1)}, bf16[4,56,640]{2,1,0:T(8,128)(2,1)S(1)}, u32[]{:S(2)}, u32[]{:S(2)}) collective-permute-start(bf16[4,56,640]{2,1,0:T(8,128)(2,1)S(1)} %get-tuple-element.9), channel_id=1, source_target_pairs={{0,1},{1,0},{2,3},{3,2},{4,5},{5,4},{6,7},{7,6},{8,9},{9,8},{10,11... | collective-permute-start | bytes 860168 | tf_op jit(solution)/shard_map/ppermute | solution.py:397
  30.5 13.4 %all-to-all-start.1 = ((bf16[4,56,640]{2,1,0:T(8,128)(2,1)}), bf16[4,56,640]{2,1,0:T(8,128)(2,1)S(1)}, u32[]{:S(2)}, u32[]{:S(2)}) async-start(bf16[4,56,640]{2,1,0:T(8,128)(2,1)} %get-tuple-element.10), calls=%async_computation.1 | async-start | bytes 573440 | tf_op jit(solution)/shard_map/all_to_all | solution.py:398
  44.1 4.4 %collective-permute-start.1 = (bf16[56,640]{1,0:T(8,128)(2,1)S(1)}, bf16[56,640]{1,0:T(8,128)(2,1)S(1)}, u32[]{:S(2)}, u32[]{:S(2)}) collective-permute-start(bf16[56,640]{1,0:T(8,128)(2,1)S(1)} %add_convert_fusion), channel_id=1, source_target_pairs={{0,2},{2,0},{1,3},{3,1},{4,6},{6,4},{5,7},{7,5},{8,10},{10,8},{9,1... | collective-permute-start | bytes 215048 | tf_op jit(solution)/shard_map/ppermute | solution.py:407
  48.5 1.4 %collective-permute-start.2 = (f32[56,640]{1,0:T(8,128)S(1)}, f32[56,640]{1,0:T(8,128)S(1)}, u32[]{:S(2)}, u32[]{:S(2)}) collective-permute-start(f32[56,640]{1,0:T(8,128)S(1)} %convert_add_fusion.1), channel_id=1, source_target_pairs={{0,1},{1,0},{2,3},{3,2},{4,5},{5,4},{6,7},{7,6},{8,9},{9,8},{10,11... | collective-permute-start | bytes 430088 | tf_op jit(solution)/shard_map/ppermute | solution.py:410

commit v5 on v4

--- a/solution.py
+++ b/solution.py
@@ -78,6 +78,26 @@
     return -(-(2 * digit_count(events) + 2) // 4) * pair_cap
 
 
+def separate(regions):
+    return regions <= 4
+
+
+def block_shapes(regions, shape, dtype):
+    if separate(regions):
+        return [jax.ShapeDtypeStruct(shape, dtype)] * regions
+    return [jax.ShapeDtypeStruct((regions,) + shape, dtype)]
+
+
+def exchange(blocks, regions):
+    if separate(regions):
+        masks = range(regions - 1, 0, -1)
+        moved = {m: lax.ppermute(blocks[m], "region", [(i, i ^ m) for i in range(regions)]) for m in masks}
+        return [blocks[0]] + [moved[m] for m in range(1, regions)]
+    order = jnp.arange(regions, dtype=jnp.int32) ^ lax.axis_index("region")
+    moved = lax.all_to_all(jnp.take(blocks[0], order, axis=0), "region", split_axis=0, concat_axis=0, tiled=True)
+    return [jnp.take(moved, order, axis=0)]
+
+
 def station_share(stations, chans):
     return -(-stations // chans)
 
@@ -88,16 +108,21 @@
     per_block = starts.shape[1]
     pair_cap = pair_first.shape[1]
     share = station_share(stations, chans)
-    total = regions * nch
-
-    def kernel(archive, starts, mask, first, second, count, out, flat):
+
+    def kernel(archive, starts, mask, first, second, count, *rest):
+        outs, flat = rest[:-1], rest[-1]
+        region = lax.axis_index("region")
         chan = lax.axis_index("chan")
         base = jnp.minimum(chan * share, stations - share)
-        flat[pl.ds(total - nch, nch), :] = jnp.zeros((nch, segment), jnp.float32)
+        for block in range(share * COMP // nch, regions):
+            flat[block] = jnp.zeros((nch, segment), jnp.float32)
         for station in range(share):
-            flat[pl.ds(station * COMP, COMP), :] = archive[base + station].astype(jnp.float32)
-        if share * COMP < total - nch:
-            flat[share * COMP : total - nch, :] = jnp.zeros((total - nch - share * COMP, segment), jnp.float32)
+            data = archive[base + station].astype(jnp.float32)
+            row = station * COMP
+            while row < (station + 1) * COMP:
+                end = min((row // nch + 1) * nch, (station + 1) * COMP)
+                flat[row // nch, row % nch : row % nch + end - row, :] = data[row - station * COMP : end - station * COMP]
+                row = end
         names = lax.broadcasted_iota(jnp.int32, (events, pair_cap), 0)
         usable = mask[...].astype(jnp.float32).astype(jnp.bfloat16)
         chosen = [jnp.dot(usable, as_bf16(names == ref[...]), preferred_element_type=jnp.float32)
@@ -105,7 +130,7 @@
         common = jnp.sum(chosen[0] * chosen[1], axis=0, keepdims=True)
         position = lax.broadcasted_iota(jnp.int32, (1, pair_cap), 1)
         code = jnp.where(position < count[0], common + 1.0, 0.0).astype(jnp.bfloat16)
-        offset = digits_of(starts[...] - lax.axis_index("region") * segment)
+        offset = digits_of(starts[...] - region * segment)
         used = [jnp.full((1, per_block), digit, jnp.int32) for digit in (count[0] >> 7, count[0] & 127)]
         used = [digit.astype(jnp.float32).astype(jnp.bfloat16) for digit in used]
         rest = jnp.zeros((1, pair_cap - 4 * per_block), jnp.bfloat16)
@@ -115,18 +140,19 @@
         else:
             fields = list(digits_of(first[...]) + digits_of(second[...]))
         fields += [code, scalars]
-        for part in range(regions):
-            out[part, :, :segment] = flat[pl.ds(part * nch, nch), :].astype(jnp.bfloat16)
+        for m in range(regions):
+            out = outs[m] if separate(regions) else outs[0].at[m]
+            out[:, :segment] = flat[region ^ m].astype(jnp.bfloat16)
             for k, field in enumerate(fields):
                 lane = segment + k // 4 * pair_cap
-                out[part, k % 4 : k % 4 + 1, lane : lane + pair_cap] = field
+                out[k % 4 : k % 4 + 1, lane : lane + pair_cap] = field
 
     return pl.pallas_call(
         kernel,
-        out_shape=jax.ShapeDtypeStruct((regions, nch, segment + field_width(events, pair_cap)), jnp.bfloat16),
+        out_shape=block_shapes(regions, (nch, segment + field_width(events, pair_cap)), jnp.bfloat16),
         in_specs=[VMEM_ONLY] * 5 + [SMEM_ONLY],
-        out_specs=VMEM_ONLY,
-        scratch_shapes=[pltpu.VMEM((total, segment), jnp.float32)],
+        out_specs=[VMEM_ONLY] * (regions if separate(regions) else 1),
+        scratch_shapes=[pltpu.VMEM((regions, nch, segment), jnp.float32)],
         name="pack",
     )(archive, starts, station_mask, pair_first, pair_second, pair_count)
 
@@ -177,14 +203,23 @@
     half = 2 * LANES
     cols = pair_cap // LANES
     per_row = min(per_block, LANES)
-    batch = regions if regions <= 4 else 1
+    batch = regions if separate(regions) else 1
     digits = digit_count(events)
-
-    def kernel(recv, slot_event, weight_rows, table, weights, kept, given, shifted, windows, spec, prod,
-               index_vmem, index, profile, sem):
+    static = separate(regions)
+    sources = regions if static else 1
+
+    def kernel(*refs):
+        received, refs = refs[:sources], refs[sources:]
+        (slot_event, weight_rows, table, weights, kept, given, shifted, windows, spec, prod, index_vmem, index, profile,
+         sem) = refs
+        region = lax.axis_index("region")
+
+        def recv(m):
+            return received[m] if static else received[0].at[m]
+
         def field(part, k):
             lane = segment + k // 4 * pair_cap
-            return recv[part, :, lane : lane + pair_cap].astype(jnp.float32)[k % 4 : k % 4 + 1]
+            return recv(part)[:, lane : lane + pair_cap].astype(jnp.float32)[k % 4 : k % 4 + 1]
 
         def listed(part, k):
             if digits == 1:
@@ -203,17 +238,20 @@
         copy = pltpu.make_async_copy(index_vmem, index, sem)
         copy.start()
 
-        def widen(part, carry):
+        def widen(part, carry=0):
             for k in range(tiles + 2):
-                data = recv[part, :, k * LANES : (k + 1) * LANES].astype(jnp.float32)
+                data = recv(part)[:, k * LANES : (k + 1) * LANES].astype(jnp.float32)
                 if k < tiles:
                     shifted[part, k, pl.ds(0, nch, stride=2), :] = data
                 if k >= 2:
                     shifted[part, k - 2, pl.ds(1, nch, stride=2), :] = data
             return carry
 
-        lax.fori_loop(0, regions, widen, 0)
-
+        if static:
+            for m in range(regions):
+                widen(m)
+        else:
+            lax.fori_loop(0, regions, widen, 0)
         copy.wait()
 
         lane = lax.broadcasted_iota(jnp.int32, (rows, LANES), 1)
@@ -239,21 +277,21 @@
             early, late = (jnp.concatenate(piece, axis=1).astype(jnp.bfloat16) for piece in pieces)
             coefs = jnp.dot(early, table[:half, :], preferred_element_type=jnp.float32)
             coefs += jnp.dot(late, table[half:, :], preferred_element_type=jnp.float32)
-            place = part * count if batch == regions else pl.multiple_of(part * count, count)
+            place = pl.multiple_of((part ^ region) * count, count)
             factor = weight_rows[pl.ds(place, count), :] * lax.rsqrt(energy + WIN * 1e-05)
             for s in range(2):
                 for k in range(2):
                     column = s * BINS + k * LANES
                     piece = (coefs[:, column : column + LANES] * factor).astype(jnp.bfloat16).astype(jnp.float32)
                     for c in range(nch):
-                        row = 2 * rows * per_block * part + s * rows + 2 * c + k
+                        row = pl.multiple_of((part ^ region) * (2 * rows * per_block), 2 * rows) + s * rows + 2 * c + k
                         spec[pl.ds(row, per_block, stride=2 * rows), :] = piece[c * per_block : (c + 1) * per_block]
 
         def looped_segment(part, carry):
             one_segment(part, 0)
             return carry
 
-        if batch == regions:
+        if static:
             for part in range(regions):
                 one_segment(part, part)
         else:
@@ -314,13 +352,17 @@
                     hot = as_bf16(jnp.concatenate([column] * cols, axis=1) == event)
                     return lax.dot_general(stack, hot, NT, preferred_element_type=jnp.float32)
 
-                profile[0, part] += gathered(part, first)
-                profile[1, part] += gathered(part, second)
-                after = (part + 1) % regions
-                profile[1, after] += gathered(after, second)
+                owner = part ^ region
+                after = (owner + 1) & (regions - 1)
+                profile[0, part] += gathered(owner, first)
+                profile[1, part] += gathered(owner, second)
+                profile[1, after ^ region] += gathered(after, second)
             return carry
 
-        lax.fori_loop(0, regions // batch, one_group, 0)
+        if static:
+            one_group(0, 0)
+        else:
+            lax.fori_loop(0, regions, one_group, 0)
         def lag_of(axis):
             row = lax.broadcasted_iota(jnp.int32, (LANES, LANES), axis)
             return jnp.where(row < HALF_ROWS, row + chan * HALF_ROWS, row - chan * HALF_ROWS)
@@ -348,7 +390,7 @@
     return pl.pallas_call(
         kernel,
         out_shape=(jax.ShapeDtypeStruct(shape, jnp.float32), jax.ShapeDtypeStruct(shape, jnp.bfloat16)),
-        in_specs=[VMEM_ONLY] * 5,
+        in_specs=[VMEM_ONLY] * (sources + 4),
         out_specs=(VMEM_ONLY, VMEM_ONLY),
         scratch_shapes=[
             pltpu.VMEM((regions, tiles, rows, LANES), jnp.float32),
@@ -379,9 +421,9 @@
     nch = 4 * -(-share * COMP // (4 * regions))
 
     mask = station_mask.T
-    payload = pack(archive, starts.reshape(1, -1), mask, pair_first.reshape(1, -1),
-                   pair_second.reshape(1, -1), pair_count, regions, chans, nch)
-    received = lax.all_to_all(payload, "region", split_axis=0, concat_axis=0, tiled=True)
+    blocks = pack(archive, starts.reshape(1, -1), mask, pair_first.reshape(1, -1),
+                  pair_second.reshape(1, -1), pair_count, regions, chans, nch)
+    received = exchange(blocks, regions)
 
     slot_of = slot_table(event_owner, regions, per_block, bucket, slots).reshape(1, -1)
     channel = lax.axis_index("region") * nch + jnp.arange(nch, dtype=jnp.int32)
@@ -391,15 +433,19 @@
 
     slot_event, weight_rows = describe(mask, station, slot_of, regions, slots, nch)
     kept, given = correlate(regions, per_block, pair_cap, segment, slots, nch)(
-        received, slot_event, weight_rows, forward_table(), lag_table())
+        *received, slot_event, weight_rows, forward_table(), lag_table())
 
     swap = [(0, 1), (1, 0)]
-    kept = kept + lax.ppermute(given, "chan", swap).astype(jnp.float32)
-    spread = lax.all_to_all(kept.astype(jnp.bfloat16), "region", split_axis=0, concat_axis=0, tiled=True)
-    here = lax.axis_index("region")
-    whole = lax.optimization_barrier(lax.dynamic_index_in_dim(kept, here, keepdims=False))
-    others = jnp.arange(regions, dtype=jnp.int32) != here
-    whole = whole + jnp.sum(jnp.where(others[:, None, None], spread.astype(jnp.float32), 0.0), axis=0)
+    swapped = lax.ppermute(given, "chan", swap)
+    if separate(regions):
+        sums = [kept[m] + swapped[m].astype(jnp.float32) for m in range(regions)]
+        moved = exchange([term.astype(jnp.bfloat16) for term in sums], regions)
+        whole = sums[0]
+        for term in moved[1:]:
+            whole = whole + term.astype(jnp.float32)
+    else:
+        moved = exchange([(kept + swapped.astype(jnp.float32)).astype(jnp.bfloat16)], regions)
+        whole = jnp.sum(moved[0].astype(jnp.float32), axis=0)
     count = lax.axis_size("stn")
     step = 1
     while step < count:

time: 51.7 us -> 44.1 us (0.85)
  waiting for transfers between devices: 22.3 us -> 16.3 us
  other arithmetic: 2.79 us -> 1.98 us
  starting transfers between devices: 11.6 us -> 10.9 us
    all_to_all x2 -> x0, waiting for transfers between devices: 16.6 us -> none  [the longest x1 9.9 us: on_device(): lax.all_to_all(kept.astype(jnp.bfloat16), 'region', split_axis=0, concat_...]
    ppermute x1 -> x7, waiting for transfers between devices: 1.56 us -> 12.1 us  [the longest x6 10.6 us: exchange(): lax.ppermute(blocks[m], 'region', [(i, i ^ m) for i in range(regions)])]
    all_to_all x2 -> x0, starting transfers between devices: 9.93 us -> none  [the longest x1 6.48 us: on_device(): lax.all_to_all(payload, 'region', split_axis=0, concat_axis=0, tiled=True)]
    ppermute x1 -> x7, starting transfers between devices: 0.07 us -> 9.27 us  [the longest x6 9.2 us: exchange(): lax.ppermute(blocks[m], 'region', [(i, i ^ m) for i in range(regions)])]
    convert_element_type x1, other arithmetic: 0.78 us -> 0.05 us  [on_device(): moved = exchange([term.astype(jnp.bfloat16) for term in sums], regions)]
  transfers between devices with their start and end apart: 5 -> 9, of which waited for: 5 -> 8; matrix products, arithmetic and copies ran while one was open for 2% -> 2% of each run, Pallas kernels for 3% -> 3%
where the time goes in v5:
time: 44.1 us; the launch traced here: 43.9 us
  waiting for transfers between devices  16.3 us (37%)
  Pallas kernels  12.6 us (29%)
  starting transfers between devices  10.9 us (25%)
  other arithmetic  1.98 us (4%)
  between operations  1.41 us (3%)
  local copies, waits for them, and re-layouts  0.73 us (2%)
    ppermute x6, waiting for transfers between devices, exchange(): lax.ppermute(blocks[m], 'region', [(i, i ^ m) for i in range(regions)])  10.6 us
    ppermute x6, starting transfers between devices, exchange(): lax.ppermute(blocks[m], 'region', [(i, i ^ m) for i in range(regions)])  9.2 us
    pallas_call x1, Pallas kernels, on_device(): correlate(regions, per_block, pair_cap, segment, slots, nch)  8.98 us
    ppermute x1, waiting for transfers between devices, on_device(): other = lax.ppermute(sent, 'stn', [(i, i ^ step) for i in range(count)])  2.84 us
    pallas_call x1, Pallas kernels, pack(): pl.pallas_call(kernel, out_shape=block_shapes(regions, (nch, segment + fi...  2.14 us
    ppermute x1, waiting for transfers between devices, on_device(): swapped = lax.ppermute(given, 'chan', swap)  1.56 us
    ppermute x1, starting transfers between devices, on_device(): other = lax.ppermute(sent, 'stn', [(i, i ^ step) for i in range(count)])  1.55 us
    pallas_call x1, Pallas kernels, describe(): pl.pallas_call(kernel, out_shape=(jax.ShapeDtypeStruct((regions * slots,...  1.49 us
  transfers between devices with their start and end apart: 9, of which 8 were waited for; matrix products, arithmetic and copies ran while one was open for 2% of the time, Pallas kernels for 3%

profile of v5, /device:TPU:0, one launch (start us, length us, event | category | flops | bytes accessed | tf_op | source)
XLA Modules:
  0.0 43.9 jit_solution(4478367732858687907)
XLA Ops:
  1.3 0.0 copy-start.4
  1.3 0.0 copy-start
  1.3 0.0 copy-start.1
  1.3 2.1 %pack.1 = (bf16[4,8704]{1,0:T(4,128)(2,1)}, bf16[4,8704]{1,0:T(4,128)(2,1)}, bf16[4,8704]{1,0:T(4,128)(2,1)}, bf16[4,8704]{1,0:T(4,128)(2,1)}) custom-call(bf16[10,3,8192]{2,1,0:T(4,128)(2,1)} %archive.1, s32[1,64]{1,0:T(1,128)} %bitcast.24, s32[20,256]{1,0:T(8,128)} %bitcast.19, s32[1,512]{1,0:T(1,128)} %bitcast.22, s32[1,512]{1,0:T(1,128)} %bitcast.23, ...), custom_call_target="tpu_custom_call" | custom-call | tf_op jit(solution)/shard_map/pack/pallas_call | solution.py:150
  3.5 3.1 %collective-permute-start = (bf16[4,8704]{1,0:T(4,128)(2,1)}, bf16[4,8704]{1,0:T(4,128)(2,1)S(1)}, u32[]{:S(2)}, u32[]{:S(2)}) collective-permute-start(bf16[4,8704]{1,0:T(4,128)(2,1)} %get-tuple-element.11), channel_id=1, source_target_pairs={{0,4},{4,0},{8,12},{12,8},{1,5},{5,1},{9,13},{13,9},{2,6},{6,2},{1... | collective-permute-start | bytes 208904 | tf_op jit(solution)/shard_map/ppermute | solution.py:94
  6.5 2.6 %collective-permute-start.1 = (bf16[4,8704]{1,0:T(4,128)(2,1)}, bf16[4,8704]{1,0:T(4,128)(2,1)S(1)}, u32[]{:S(2)}, u32[]{:S(2)}) collective-permute-start(bf16[4,8704]{1,0:T(4,128)(2,1)} %get-tuple-element.12), channel_id=1, source_target_pairs={{0,8},{4,12},{8,0},{12,4},{1,9},{5,13},{9,1},{13,5},{2,10},{6,14},... | collective-permute-start | bytes 208904 | tf_op jit(solution)/shard_map/ppermute | solution.py:94
  9.1 0.0 collective-permute-start.2
  9.1 0.1 add.74
  9.2 0.1 add.75
  9.3 0.0 copy-done.4
  9.3 0.1 eq.20
  9.3 0.1 fusion.4
  9.5 0.1 reduce_window_sum.11
  9.6 0.0 copy-start.2
  9.6 0.0 copy-start.3
  9.6 0.2 select_reduce_fusion
  9.8 0.1 reduce_sum.12
  10.0 0.4 copy-done.2
  10.3 1.5 %describe.1 = (f32[512,128]{1,0:T(8,128)S(1)}, f32[1024,128]{1,0:T(8,128)S(1)}) custom-call(s32[20,256]{1,0:T(8,128)S(1)} %bitcast.20, s32[4]{0:T(128)S(1)} %and_select_fusion.station, s32[1,256]{1,0:T(1,128)S(1)} %bitcast.21), custom_call_target="tpu_custom_call" | custom-call | tf_op jit(solution)/shard_map/describe/pallas_call | solution.py:184
  11.8 0.0 collective-permute-done.refs_1_
  11.8 2.4 %collective-permute-done.1.refs_2_ = bf16[4,8704]{1,0:T(4,128)(2,1)S(1)} collective-permute-done((bf16[4,8704]{1,0:T(4,128)(2,1)}, bf16[4,8704]{1,0:T(4,128)(2,1)S(1)}, u32[]{:S(2)}, u32[]{:S(2)}) %collective-permute-start.1) | collective-permute-done | bytes 69664 | tf_op jit(solution)/shard_map/ppermute | solution.py:94
  14.2 1.3 %collective-permute-done.2.refs_3_ = bf16[4,8704]{1,0:T(4,128)(2,1)S(1)} collective-permute-done((bf16[4,8704]{1,0:T(4,128)(2,1)}, bf16[4,8704]{1,0:T(4,128)(2,1)S(1)}, u32[]{:S(2)}, u32[]{:S(2)}) %collective-permute-start.2) | collective-permute-done | bytes 69664 | tf_op jit(solution)/shard_map/ppermute | solution.py:94
  15.5 0.0 copy-done
  15.5 0.0 copy-done.1
  15.5 0.0 copy-done.3
  15.5 9.0 %correlate.1 = (f32[4,56,640]{2,1,0:T(8,128)S(1)}, bf16[4,56,640]{2,1,0:T(8,128)(2,1)S(1)}) custom-call(bf16[4,8704]{1,0:T(4,128)(2,1)S(1)} %copy-done.3, bf16[4,8704]{1,0:T(4,128)(2,1)S(1)} %collective-permute-done.refs_1_, bf16[4,8704]{1,0:T(4,128)(2,1)S(1)} %collective-permute-done.1.refs_2_, bf16[4,8704]{1,0:T(4,128)(2,1)S(1)} %collective-permute-done.2.refs_3_, ...), custom_call_target="tpu_custom_call" | custom-call | tf_op jit(solution)/shard_map/correlate/pallas_call | solution.py:435
  24.5 0.1 collective-permute-start.3
  24.6 1.6 %collective-permute-done.3 = bf16[4,56,640]{2,1,0:T(8,128)(2,1)S(1)} collective-permute-done((bf16[4,56,640]{2,1,0:T(8,128)(2,1)S(1)}, bf16[4,56,640]{2,1,0:T(8,128)(2,1)S(1)}, u32[]{:S(2)}, u32[]{:S(2)}) %collective-permute-start.3) | collective-permute-done | bytes 286752 | tf_op jit(solution)/shard_map/ppermute | solution.py:439
  26.1 0.1 fusion.5
  26.2 0.9 %collective-permute-start.4 = (bf16[56,640]{1,0:T(8,128)(2,1)S(1)}, bf16[56,640]{1,0:T(8,128)(2,1)S(1)}, u32[]{:S(2)}, u32[]{:S(2)}) collective-permute-start(bf16[56,640]{1,0:T(8,128)(2,1)S(1)} %get-tuple-element.18), channel_id=1, source_target_pairs={{0,4},{4,0},{8,12},{12,8},{1,5},{5,1},{9,13},{13,9},{2,6},{6,2},{1... | collective-permute-start | bytes 215048 | tf_op jit(solution)/shard_map/ppermute | solution.py:94
  27.1 2.5 %collective-permute-start.6 = (bf16[56,640]{1,0:T(8,128)(2,1)S(1)}, bf16[56,640]{1,0:T(8,128)(2,1)S(1)}, u32[]{:S(2)}, u32[]{:S(2)}) collective-permute-start(bf16[56,640]{1,0:T(8,128)(2,1)S(1)} %get-tuple-element.19), channel_id=1, source_target_pairs={{0,12},{4,8},{8,4},{12,0},{1,13},{5,9},{9,5},{13,1},{2,14},{6,10},... | collective-permute-start | bytes 215048 | tf_op jit(solution)/shard_map/ppermute | solution.py:94
  29.5 0.2 collective-permute-start.5
  29.8 0.8 %collective-permute-done.4 = bf16[56,640]{1,0:T(8,128)(2,1)S(1)} collective-permute-done((bf16[56,640]{1,0:T(8,128)(2,1)S(1)}, bf16[56,640]{1,0:T(8,128)(2,1)S(1)}, u32[]{:S(2)}, u32[]{:S(2)}) %collective-permute-start.4) | collective-permute-done | bytes 71712 | tf_op jit(solution)/shard_map/ppermute | solution.py:94
  30.6 3.5 %collective-permute-done.6 = bf16[56,640]{1,0:T(8,128)(2,1)S(1)} collective-permute-done((bf16[56,640]{1,0:T(8,128)(2,1)S(1)}, bf16[56,640]{1,0:T(8,128)(2,1)S(1)}, u32[]{:S(2)}, u32[]{:S(2)}) %collective-permute-start.6) | collective-permute-done | bytes 71712 | tf_op jit(solution)/shard_map/ppermute | solution.py:94
  34.1 2.6 %collective-permute-done.5 = bf16[56,640]{1,0:T(8,128)(2,1)S(1)} collective-permute-done((bf16[56,640]{1,0:T(8,128)(2,1)S(1)}, bf16[56,640]{1,0:T(8,128)(2,1)S(1)}, u32[]{:S(2)}, u32[]{:S(2)}) %collective-permute-start.5) | collective-permute-done | bytes 71712 | tf_op jit(solution)/shard_map/ppermute | solution.py:94
  36.7 0.1 fusion.3
  36.7 1.6 %collective-permute-start.7 = (bf16[56,640]{1,0:T(8,128)(2,1)S(1)}, bf16[56,640]{1,0:T(8,128)(2,1)S(1)}, u32[]{:S(2)}, u32[]{:S(2)}) collective-permute-start(bf16[56,640]{1,0:T(8,128)(2,1)S(1)} %fusion.3), channel_id=1, source_target_pairs={{0,2},{2,0},{1,3},{3,1},{4,6},{6,4},{5,7},{7,5},{8,10},{10,8},{9,1... | collective-permute-start | bytes 215048 | tf_op jit(solution)/shard_map/ppermute | solution.py:453
  38.3 2.8 %collective-permute-done.7 = bf16[56,640]{1,0:T(8,128)(2,1)S(1)} collective-permute-done((bf16[56,640]{1,0:T(8,128)(2,1)S(1)}, bf16[56,640]{1,0:T(8,128)(2,1)S(1)}, u32[]{:S(2)}, u32[]{:S(2)}) %collective-permute-start.7) | collective-permute-done | bytes 71712 | tf_op jit(solution)/shard_map/ppermute | solution.py:453
  41.1 0.1 collective-permute-start.8
  41.2 1.3 %collective-permute-done.8 = f32[56,640]{1,0:T(8,128)S(1)} collective-permute-done((f32[56,640]{1,0:T(8,128)S(1)}, f32[56,640]{1,0:T(8,128)S(1)}, u32[]{:S(2)}, u32[]{:S(2)}) %collective-permute-start.8) | collective-permute-done | bytes 143392 | tf_op jit(solution)/shard_map/ppermute | solution.py:456
  42.6 0.6 %pad_maximum_fusion = f32[101,128]{1,0:T(8,128)} fusion(f32[56,640]{1,0:T(8,128)S(1)} %get-tuple-element.21, f32[56,640]{1,0:T(8,128)S(1)} %get-tuple-element.22), kind=kLoop, calls=%fused_computation.19 | loop fusion | flops 12928 | bytes 338432 | tf_op jit(solution)/shard_map/concatenate | solution.py:459
  43.2 0.7 %fusion = f32[101,512]{1,0:T(8,128)} fusion(f32[56,640]{1,0:T(8,128)S(1)} %get-tuple-element.22, f32[56,640]{1,0:T(8,128)S(1)} %get-tuple-element.21), kind=kLoop, calls=%fused_computation.2 | loop fusion | flops 51712 | bytes 493568 | tf_op jit(solution)/shard_map/concatenate | solution.py:459
  (5 shorter events, 0.1 us)
Async XLA Ops:
  1.3 8.0 %copy-start.4 = (s32[256]{0:T(256)S(1)}, s32[256]{0:T(256)}, u32[]{:S(2)}) copy-start(s32[256]{0:T(256)} %param.11) | copy-start | bytes 3076
  1.3 14.2 %copy-start = (bf16[2,256,512]{2,1,0:T(8,128)(2,1)S(1)}, bf16[2,256,512]{2,1,0:T(8,128)(2,1)}, u32[]{:S(2)}) copy-start(bf16[2,256,512]{2,1,0:T(8,128)(2,1)} %constant.52.refs_7_) | copy-start | bytes 1572868
  1.3 14.2 %copy-start.1 = (bf16[512,512]{1,0:T(8,128)(2,1)S(1)}, bf16[512,512]{1,0:T(8,128)(2,1)}, u32[]{:S(2)}) copy-start(bf16[512,512]{1,0:T(8,128)(2,1)} %constant.47.refs_6_) | copy-start | bytes 1572868
  3.5 8.4 %collective-permute-start = (bf16[4,8704]{1,0:T(4,128)(2,1)}, bf16[4,8704]{1,0:T(4,128)(2,1)S(1)}, u32[]{:S(2)}, u32[]{:S(2)}) collective-permute-start(bf16[4,8704]{1,0:T(4,128)(2,1)} %get-tuple-element.11), channel_id=1, source_target_pairs={{0,4},{4,0},{8,12},{12,8},{1,5},{5,1},{9,13},{13,9},{2,6},{6,2},{1... | collective-permute-start | bytes 208904 | tf_op jit(solution)/shard_map/ppermute | solution.py:94
  6.5 7.7 %collective-permute-start.1 = (bf16[4,8704]{1,0:T(4,128)(2,1)}, bf16[4,8704]{1,0:T(4,128)(2,1)S(1)}, u32[]{:S(2)}, u32[]{:S(2)}) collective-permute-start(bf16[4,8704]{1,0:T(4,128)(2,1)} %get-tuple-element.12), channel_id=1, source_target_pairs={{0,8},{4,12},{8,0},{12,4},{1,9},{5,13},{9,1},{13,5},{2,10},{6,14},... | collective-permute-start | bytes 208904 | tf_op jit(solution)/shard_map/ppermute | solution.py:94
  9.1 6.4 %collective-permute-start.2 = (bf16[4,8704]{1,0:T(4,128)(2,1)}, bf16[4,8704]{1,0:T(4,128)(2,1)S(1)}, u32[]{:S(2)}, u32[]{:S(2)}) collective-permute-start(bf16[4,8704]{1,0:T(4,128)(2,1)} %get-tuple-element.13), channel_id=1, source_target_pairs={{0,12},{4,8},{8,4},{12,0},{1,13},{5,9},{9,5},{13,1},{2,14},{6,10},... | collective-permute-start | bytes 208904 | tf_op jit(solution)/shard_map/ppermute | solution.py:94
  9.6 0.7 %copy-start.2 = (s32[256,20]{0,1:T(8,128)S(1)}, s32[256,20]{0,1:T(8,128)}, u32[]{:S(2)}) copy-start(s32[256,20]{0,1:T(8,128)} %param.12) | copy-start | bytes 61444
  9.6 5.9 %copy-start.3 = (bf16[4,8704]{1,0:T(4,128)(2,1)S(1)}, bf16[4,8704]{1,0:T(4,128)(2,1)}, u32[]{:S(2)}) copy-start(bf16[4,8704]{1,0:T(4,128)(2,1)} %get-tuple-element.10.refs_0_) | copy-start | bytes 208900
  24.5 1.6 %collective-permute-start.3 = (bf16[4,56,640]{2,1,0:T(8,128)(2,1)S(1)}, bf16[4,56,640]{2,1,0:T(8,128)(2,1)S(1)}, u32[]{:S(2)}, u32[]{:S(2)}) collective-permute-start(bf16[4,56,640]{2,1,0:T(8,128)(2,1)S(1)} %get-tuple-element.17), channel_id=1, source_target_pairs={{0,1},{1,0},{2,3},{3,2},{4,5},{5,4},{6,7},{7,6},{8,9},{9,8},{10,11... | collective-permute-start | bytes 860168 | tf_op jit(solution)/shard_map/ppermute | solution.py:439
  26.2 4.4 %collective-permute-start.4 = (bf16[56,640]{1,0:T(8,128)(2,1)S(1)}, bf16[56,640]{1,0:T(8,128)(2,1)S(1)}, u32[]{:S(2)}, u32[]{:S(2)}) collective-permute-start(bf16[56,640]{1,0:T(8,128)(2,1)S(1)} %get-tuple-element.18), channel_id=1, source_target_pairs={{0,4},{4,0},{8,12},{12,8},{1,5},{5,1},{9,13},{13,9},{2,6},{6,2},{1... | collective-permute-start | bytes 215048 | tf_op jit(solution)/shard_map/ppermute | solution.py:94
  27.1 7.0 %collective-permute-start.6 = (bf16[56,640]{1,0:T(8,128)(2,1)S(1)}, bf16[56,640]{1,0:T(8,128)(2,1)S(1)}, u32[]{:S(2)}, u32[]{:S(2)}) collective-permute-start(bf16[56,640]{1,0:T(8,128)(2,1)S(1)} %get-tuple-element.19), channel_id=1, source_target_pairs={{0,12},{4,8},{8,4},{12,0},{1,13},{5,9},{9,5},{13,1},{2,14},{6,10},... | collective-permute-start | bytes 215048 | tf_op jit(solution)/shard_map/ppermute | solution.py:94
  29.5 7.1 %collective-permute-start.5 = (bf16[56,640]{1,0:T(8,128)(2,1)S(1)}, bf16[56,640]{1,0:T(8,128)(2,1)S(1)}, u32[]{:S(2)}, u32[]{:S(2)}) collective-permute-start(bf16[56,640]{1,0:T(8,128)(2,1)S(1)} %get-tuple-element.20), channel_id=1, source_target_pairs={{0,8},{4,12},{8,0},{12,4},{1,9},{5,13},{9,1},{13,5},{2,10},{6,14},... | collective-permute-start | bytes 215048 | tf_op jit(solution)/shard_map/ppermute | solution.py:94
  36.7 4.4 %collective-permute-start.7 = (bf16[56,640]{1,0:T(8,128)(2,1)S(1)}, bf16[56,640]{1,0:T(8,128)(2,1)S(1)}, u32[]{:S(2)}, u32[]{:S(2)}) collective-permute-start(bf16[56,640]{1,0:T(8,128)(2,1)S(1)} %fusion.3), channel_id=1, source_target_pairs={{0,2},{2,0},{1,3},{3,1},{4,6},{6,4},{5,7},{7,5},{8,10},{10,8},{9,1... | collective-permute-start | bytes 215048 | tf_op jit(solution)/shard_map/ppermute | solution.py:453
  41.1 1.4 %collective-permute-start.8 = (f32[56,640]{1,0:T(8,128)S(1)}, f32[56,640]{1,0:T(8,128)S(1)}, u32[]{:S(2)}, u32[]{:S(2)}) collective-permute-start(f32[56,640]{1,0:T(8,128)S(1)} %convert_add_fusion), channel_id=1, source_target_pairs={{0,1},{1,0},{2,3},{3,2},{4,5},{5,4},{6,7},{7,6},{8,9},{9,8},{10,11... | collective-permute-start | bytes 430088 | tf_op jit(solution)/shard_map/ppermute | solution.py:456

commit v6 on v5

--- a/solution.py
+++ b/solution.py
@@ -162,13 +162,14 @@
     per_block = events // regions
 
     def kernel(mask, station, slot_of, slot_event, weight_rows):
+        region = lax.axis_index("region")
         listed = lax.broadcasted_iota(jnp.int32, (mask.shape[0], LANES), 0)
         usable = mask[...].astype(jnp.float32).astype(jnp.bfloat16)
         for c in range(nch):
             value = lax.dot_general(usable, as_bf16(listed == station[c]), TN, preferred_element_type=jnp.float32)
             for part in range(regions):
-                row = (part * nch + c) * per_block
-                weight_rows[row : row + per_block, :] = value[part * per_block : (part + 1) * per_block]
+                row = pl.multiple_of(((part ^ region) * nch + c) * per_block, per_block)
+                weight_rows[pl.ds(row, per_block), :] = value[part * per_block : (part + 1) * per_block]
         names = digits_of(lax.broadcasted_iota(jnp.int32, (events, LANES), 0) + 1)
         place = lax.broadcasted_iota(jnp.int32, (slots, events), 0)
         slot_lane = slot_of[...]
@@ -196,22 +197,131 @@
     return min(rows * LANES * 4 * 5 // 4 + (4 << 20), 60 * 1024 * 1024)
 
 
-def correlate(regions, per_block, pair_cap, segment, slots, nch):
-    rows = 2 * nch
-    tiles = segment // LANES + 2
+class Cutter:
+    def __init__(self, per_block, segment, nch):
+        self.per_block, self.nch = per_block, nch
+        self.rows = 2 * nch
+        self.tiles = segment // LANES + 2
+        self.count = per_block * nch
+        self.spec_rows = 2 * self.rows * per_block
+
+    def words(self, scalars, slot):
+        tile, lane = scalars[:, : self.per_block], scalars[:, self.per_block : 2 * self.per_block]
+        return ((tile + slot * self.tiles) * (256.0 * self.rows) + (LANES - lane)).astype(jnp.int32)
+
+    def widen(self, source, shifted, slot):
+        rows, nch = self.rows, self.nch
+        first = slot * (self.tiles * rows)
+        if not isinstance(slot, int):
+            first = pl.multiple_of(first, rows)
+        for k in range(self.tiles + 2):
+            data = source[:, k * LANES : (k + 1) * LANES].astype(jnp.float32)
+            if k < self.tiles:
+                shifted[pl.ds(first + k * rows, nch, stride=2), :] = data
+            if k >= 2:
+                shifted[pl.ds(first + (k - 2) * rows + 1, nch, stride=2), :] = data
+
+    def cut(self, word_of, shifted, windows, slot):
+        rows = self.rows
+        from_right = LANES - 1 - lax.broadcasted_iota(jnp.int32, (rows, LANES), 1)
+        for event in range(self.per_block):
+            word = word_of(event)
+            first = pl.multiple_of(word >> 8, rows)
+            turn = word & (2 * LANES - 1)
+            data = [shifted[pl.ds(first + k * rows, rows), :] for k in range(3)]
+            later = from_right < turn
+            turn = turn & (LANES - 1)
+            row = event * rows
+            windows[slot, 0, row : row + rows, :] = pltpu.roll(jnp.where(later, data[0], data[1]), turn, 1)
+            windows[slot, 1, row : row + rows, :] = pltpu.roll(jnp.where(later, data[1], data[2]), turn, 1)
+
+    def transform(self, windows, slot, weight_rows, block, table, spec, place):
+        per_block, nch, rows, count = self.per_block, self.nch, self.rows, self.count
+        half = 2 * LANES
+        inside = lax.broadcasted_iota(jnp.int32, (count, LANES), 1) < WIN - half - LANES
+        pieces = [[jnp.concatenate([windows[slot, t, pl.ds(2 * c + k, per_block, stride=rows), :] for c in range(nch)])
+                   for t in range(2)] for k in range(2)]
+        squares = pieces[0][0] * pieces[0][0] + pieces[0][1] * pieces[0][1] + pieces[1][0] * pieces[1][0]
+        squares += jnp.where(inside, pieces[1][1] * pieces[1][1], 0.0)
+        energy = jnp.sum(squares, axis=1, keepdims=True)
+        early, late = (jnp.concatenate(piece, axis=1).astype(jnp.bfloat16) for piece in pieces)
+        coefs = jnp.dot(early, table[:half, :], preferred_element_type=jnp.float32)
+        coefs += jnp.dot(late, table[half:, :], preferred_element_type=jnp.float32)
+        first = block * count if isinstance(block, int) else pl.multiple_of(block * count, count)
+        factor = weight_rows[pl.ds(first, count), :] * lax.rsqrt(energy + WIN * 1e-05)
+        for s in range(2):
+            for k in range(2):
+                column = s * BINS + k * LANES
+                piece = (coefs[:, column : column + LANES] * factor).astype(jnp.bfloat16).astype(jnp.float32)
+                for c in range(nch):
+                    row = place + s * rows + 2 * c + k
+                    spec[pl.ds(row, per_block, stride=2 * rows), :] = piece[c * per_block : (c + 1) * per_block]
+
+
+def scalar_field(events):
+    return 2 * digit_count(events) + 1
+
+
+def early_spectra(blocks, weight_rows, table, regions, per_block, pair_cap, segment, nch):
+    cutter = Cutter(per_block, segment, nch)
+    number = len(blocks)
+    k = scalar_field(regions * per_block)
+
+    def kernel(*refs):
+        sources, refs = refs[:number], refs[number:]
+        weight_rows, table, spec, shifted, windows, index_vmem, index, sem = refs
+        for slot in range(number):
+            lane = segment + k // 4 * pair_cap
+            scalars = sources[slot][:, lane : lane + LANES].astype(jnp.float32)[k % 4 : k % 4 + 1]
+            index_vmem[slot : slot + 1, :per_block] = cutter.words(scalars, slot)
+        copy = pltpu.make_async_copy(index_vmem, index, sem)
+        copy.start()
+        for slot in range(number):
+            cutter.widen(sources[slot], shifted, slot)
+        copy.wait()
+
+        def cut(slot, carry):
+            cutter.cut(lambda event: index[slot, event], shifted, windows, slot)
+            return carry
+
+        lax.fori_loop(0, number, cut, 0)
+        for slot in range(number):
+            cutter.transform(windows, slot, weight_rows, slot, table, spec, slot * cutter.spec_rows)
+
+    used = number * (cutter.spec_rows + (cutter.tiles + 2 * per_block) * cutter.rows + 2 * segment * nch // LANES)
+    return pl.pallas_call(
+        kernel,
+        out_shape=jax.ShapeDtypeStruct((number * cutter.spec_rows, LANES), jnp.float32),
+        in_specs=[VMEM_ONLY] * (number + 2),
+        out_specs=VMEM_ONLY,
+        scratch_shapes=[
+            pltpu.VMEM((number * cutter.tiles * cutter.rows, LANES), jnp.float32),
+            pltpu.VMEM((number, 2, per_block * cutter.rows, LANES), jnp.float32),
+            pltpu.VMEM((8, LANES), jnp.int32),
+            pltpu.SMEM((8, LANES), jnp.int32),
+            pltpu.SemaphoreType.DMA(()),
+        ],
+        compiler_params=pltpu.CompilerParams(vmem_limit_bytes=grant(used + weight_rows.shape[0] + 2 * NFFT)),
+        name="early_spectra",
+    )(*blocks, weight_rows, table)
+
+
+def correlate(regions, per_block, pair_cap, segment, slots, nch, ready):
+    cutter = Cutter(per_block, segment, nch)
+    rows, tiles = cutter.rows, cutter.tiles
     events = regions * per_block
-    half = 2 * LANES
     cols = pair_cap // LANES
-    per_row = min(per_block, LANES)
     batch = regions if separate(regions) else 1
     digits = digit_count(events)
     static = separate(regions)
     sources = regions if static else 1
+    shift = per_block.bit_length() - 1
+    assert per_block == 1 << shift
 
     def kernel(*refs):
         received, refs = refs[:sources], refs[sources:]
-        (slot_event, weight_rows, table, weights, kept, given, shifted, windows, spec, prod, index_vmem, index, profile,
-         sem) = refs
+        (ready_spec, slot_event, weight_rows, table, weights, kept, given, shifted, windows, spec, prod, index_vmem, index,
+         profile, sem) = refs if ready else (None,) + refs
         region = lax.axis_index("region")
 
         def recv(m):
@@ -229,78 +339,52 @@
         for part in range(regions):
             rows_out = []
             for k in range(2):
-                event = listed(part, k).astype(jnp.int32) * (2 * rows)
+                event = (listed(part, k).astype(jnp.int32) ^ (region << shift)) * (2 * rows)
                 rows_out += [event[:, c * LANES : (c + 1) * LANES] for c in range(cols)]
-            scalars = field(part, 2 * digits + 1).astype(jnp.int32)
-            rows_out += [scalars[:, c * LANES : (c + 1) * LANES] for c in range(2)]
+            scalars = field(part, scalar_field(events))
+            rows_out += [scalars[:, LANES : 2 * LANES].astype(jnp.int32)]
             for row, value in enumerate(rows_out):
                 index_vmem[part, row : row + 1, :] = value
+            slot = part - ready if static else part
+            index_vmem[part, 2 * cols + 1 : 2 * cols + 2, :per_block] = cutter.words(scalars, slot)
         copy = pltpu.make_async_copy(index_vmem, index, sem)
         copy.start()
-
-        def widen(part, carry=0):
-            for k in range(tiles + 2):
-                data = recv(part)[:, k * LANES : (k + 1) * LANES].astype(jnp.float32)
-                if k < tiles:
-                    shifted[part, k, pl.ds(0, nch, stride=2), :] = data
-                if k >= 2:
-                    shifted[part, k - 2, pl.ds(1, nch, stride=2), :] = data
+        if static:
+            if ready:
+                spec[: ready * cutter.spec_rows, :] = ready_spec[...]
+            for part in range(ready, regions):
+                cutter.widen(recv(part), shifted, part - ready)
+        else:
+            def widen(part, carry):
+                cutter.widen(recv(part), shifted, part)
+                return carry
+
+            lax.fori_loop(0, regions, widen, 0)
+        profile[...] = jnp.zeros_like(profile)
+        copy.wait()
+
+        def cut(slot, carry):
+            cutter.cut(lambda event: index[slot + ready, 2 * cols + 1, event], shifted, windows, slot)
             return carry
 
+        def cut_and_transform(part, carry):
+            cutter.cut(lambda event: index[part, 2 * cols + 1, event], shifted, windows, 0)
+            place = pl.multiple_of(part * cutter.spec_rows, cutter.spec_rows)
+            cutter.transform(windows, 0, weight_rows, part, table, spec, place)
+            return carry
+
         if static:
-            for m in range(regions):
-                widen(m)
+            lax.fori_loop(0, regions - ready, cut, 0)
+            for part in range(ready, regions):
+                cutter.transform(windows, part - ready, weight_rows, part, table, spec, part * cutter.spec_rows)
         else:
-            lax.fori_loop(0, regions, widen, 0)
-        copy.wait()
+            lax.fori_loop(0, regions, cut_and_transform, 0)
 
         lane = lax.broadcasted_iota(jnp.int32, (rows, LANES), 1)
         sublane = lax.broadcasted_iota(jnp.int32, (rows, LANES), 0)
-        count = per_block * nch
-        inside = lax.broadcasted_iota(jnp.int32, (count, LANES), 1) < WIN - half - LANES
-
-        def one_segment(part, slot):
-            for event in range(per_block):
-                base = index[part, 2 * cols, event]
-                off = index[part, 2 * cols, per_block + event]
-                turn = (LANES - off) & (LANES - 1)
-                data = [shifted[part, base + k] for k in range(3)]
-                later = lane >= off
-                row = event * rows
-                windows[slot, 0, row : row + rows, :] = pltpu.roll(jnp.where(later, data[0], data[1]), turn, 1)
-                windows[slot, 1, row : row + rows, :] = pltpu.roll(jnp.where(later, data[1], data[2]), turn, 1)
-            pieces = [[jnp.concatenate([windows[slot, t, pl.ds(2 * c + k, per_block, stride=rows), :] for c in range(nch)])
-                       for t in range(2)] for k in range(2)]
-            squares = pieces[0][0] * pieces[0][0] + pieces[0][1] * pieces[0][1] + pieces[1][0] * pieces[1][0]
-            squares += jnp.where(inside, pieces[1][1] * pieces[1][1], 0.0)
-            energy = jnp.sum(squares, axis=1, keepdims=True)
-            early, late = (jnp.concatenate(piece, axis=1).astype(jnp.bfloat16) for piece in pieces)
-            coefs = jnp.dot(early, table[:half, :], preferred_element_type=jnp.float32)
-            coefs += jnp.dot(late, table[half:, :], preferred_element_type=jnp.float32)
-            place = pl.multiple_of((part ^ region) * count, count)
-            factor = weight_rows[pl.ds(place, count), :] * lax.rsqrt(energy + WIN * 1e-05)
-            for s in range(2):
-                for k in range(2):
-                    column = s * BINS + k * LANES
-                    piece = (coefs[:, column : column + LANES] * factor).astype(jnp.bfloat16).astype(jnp.float32)
-                    for c in range(nch):
-                        row = pl.multiple_of((part ^ region) * (2 * rows * per_block), 2 * rows) + s * rows + 2 * c + k
-                        spec[pl.ds(row, per_block, stride=2 * rows), :] = piece[c * per_block : (c + 1) * per_block]
-
-        def looped_segment(part, carry):
-            one_segment(part, 0)
-            return carry
-
-        if static:
-            for part in range(regions):
-                one_segment(part, part)
-        else:
-            lax.fori_loop(0, regions, looped_segment, 0)
-
         chan = lax.axis_index("chan")
         special = (sublane % 2 == 0) & (lane == 0)
         upper = sublane < nch
-        profile[...] = jnp.zeros_like(profile)
 
         def one_group(group, carry):
             def some_pairs(member, row):
@@ -321,7 +405,7 @@
 
             def pairs_of(member, inner):
                 part = group * batch + member
-                pairs = index[part, 2 * cols + 1, 0] * LANES + index[part, 2 * cols + 1, per_block]
+                pairs = index[part, 2 * cols, 0] * LANES + index[part, 2 * cols, per_block]
                 lax.fori_loop(0, jnp.minimum((pairs + LANES - 1) // LANES, cols), lambda row, m: some_pairs(m, row),
                               member)
                 return inner
@@ -385,15 +469,15 @@
     shape = (regions, HALF_ROWS, pair_cap + slots)
     index_rows = 8 * -(-(2 * cols + 2) // 8)
     width = (pair_cap + slots) // LANES
-    used = regions * (tiles * rows + LAG_ROWS * width + 2 * LANES + index_rows + 4 * tiles + slots)
+    used = regions * (tiles * rows + LAG_ROWS * width + 2 * LANES + index_rows + 4 * tiles + slots) + ready * cutter.spec_rows
     used += (2 * per_block * batch + 2 * events + batch * pair_cap) * rows + events * nch + 3 * NFFT
     return pl.pallas_call(
         kernel,
         out_shape=(jax.ShapeDtypeStruct(shape, jnp.float32), jax.ShapeDtypeStruct(shape, jnp.bfloat16)),
-        in_specs=[VMEM_ONLY] * (sources + 4),
+        in_specs=[VMEM_ONLY] * (sources + 4 + (ready > 0)),
         out_specs=(VMEM_ONLY, VMEM_ONLY),
         scratch_shapes=[
-            pltpu.VMEM((regions, tiles, rows, LANES), jnp.float32),
+            pltpu.VMEM(((regions - ready) * tiles * rows, LANES), jnp.float32),
             pltpu.VMEM((batch, 2, per_block * rows, LANES), jnp.float32),
             pltpu.VMEM((2 * events * rows, LANES), jnp.float32),
             pltpu.VMEM((batch * pair_cap * rows, LANES), jnp.float32),
@@ -405,6 +489,30 @@
         compiler_params=pltpu.CompilerParams(vmem_limit_bytes=grant(used)),
         name="correlate",
     )
+
+
+def assemble(whole, other, pair_cap):
+    rest = LAGS - HALF_ROWS
+
+    def kernel(whole, other, stack, profile):
+        first = lax.axis_index("chan") == 0
+        low = jnp.where(first, whole[...], other[...])
+        high = jnp.where(first, other[...], whole[...])
+        stack[:HALF_ROWS, :] = low[:, :pair_cap]
+        stack[HALF_ROWS:, :] = high[:rest, :pair_cap]
+        profile[:HALF_ROWS, :] = low[:, pair_cap:]
+        profile[HALF_ROWS:, :] = high[:rest, pair_cap:]
+
+    width = whole.shape[1]
+    return pl.pallas_call(
+        kernel,
+        out_shape=(jax.ShapeDtypeStruct((LAGS, pair_cap), jnp.float32),
+                   jax.ShapeDtypeStruct((LAGS, width - pair_cap), jnp.float32)),
+        in_specs=[VMEM_ONLY] * 2,
+        out_specs=(VMEM_ONLY, VMEM_ONLY),
+        compiler_params=pltpu.CompilerParams(vmem_limit_bytes=grant(4 * LAG_ROWS * width // LANES)),
+        name="assemble",
+    )(whole, other)
 
 
 def on_device(archive, starts, event_owner, station_mask, pair_first, pair_second, pair_count):
@@ -432,8 +540,13 @@
     station = jnp.where(used, lax.axis_index("stn") * stations + local, -1)
 
     slot_event, weight_rows = describe(mask, station, slot_of, regions, slots, nch)
-    kept, given = correlate(regions, per_block, pair_cap, segment, slots, nch)(
-        *received, slot_event, weight_rows, forward_table(), lag_table())
+    table = forward_table()
+    ready = 2 if regions == 4 else 0
+    spectra = []
+    if ready:
+        spectra = [early_spectra(received[:ready], weight_rows, table, regions, per_block, pair_cap, segment, nch)]
+    kept, given = correlate(regions, per_block, pair_cap, segment, slots, nch, ready)(
+        *received, *spectra, slot_event, weight_rows, table, lag_table())
 
     swap = [(0, 1), (1, 0)]
     swapped = lax.ppermute(given, "chan", swap)
@@ -454,10 +567,7 @@
         whole = sent.astype(jnp.float32) + other.astype(jnp.float32)
         step *= 2
     other = lax.ppermute(whole, "chan", swap)
-    low = jnp.where(chan_index == 0, whole, other)
-    high = jnp.where(chan_index == 0, other, whole)
-    full = jnp.concatenate([low, high], axis=0)[:LAGS]
-    return full[:, :pair_cap], full[:, pair_cap:]
+    return assemble(whole, other, pair_cap)
 
 
 def solution(mesh):

time: 44.1 us -> 42.8 us (0.971)
  waiting for transfers between devices: 16.3 us -> 13.9 us
  Pallas kernels: 12.6 us -> 14.5 us
  other arithmetic: 1.98 us -> 0.61 us
  local copies, waits for them, and re-layouts: 0.73 us -> 1.32 us
    ppermute x6, waiting for transfers between devices: 10.6 us -> 8.11 us  [exchange(): lax.ppermute(blocks[m], 'region', [(i, i ^ m) for i in range(regions)])]
    pallas_call x1 -> x3, Pallas kernels: 8.98 us -> 10.8 us  [the longest x1 8.3 us: on_device(): correlate(regions, per_block, pair_cap, segment, slots, nch, ready)]
    concatenate x2 -> x0, other arithmetic: 1.33 us -> none  [on_device(): full = jnp.concatenate([low, high], axis=0)[:LAGS]]
    unnamed x10, local copies, waits for them, and re-layouts: 0.4 us -> 1 us
  transfers between devices with their start and end apart: 9 -> 9, of which waited for: 8 -> 7; matrix products, arithmetic and copies ran while one was open for 2% -> 2% of each run, Pallas kernels for 3% -> 8%
where the time goes in v6:
time: 42.8 us; the launch traced here: 42.5 us
  Pallas kernels  14.5 us (34%)
  waiting for transfers between devices  13.9 us (32%)
  starting transfers between devices  10.9 us (25%)
  between operations  1.42 us (3%)
  local copies, waits for them, and re-layouts  1.32 us (3%)
  other arithmetic  0.61 us (1%)
    ppermute x6, starting transfers between devices, exchange(): lax.ppermute(blocks[m], 'region', [(i, i ^ m) for i in range(regions)])  9.2 us
    pallas_call x1, Pallas kernels, on_device(): correlate(regions, per_block, pair_cap, segment, slots, nch, ready)  8.3 us
    ppermute x6, waiting for transfers between devices, exchange(): lax.ppermute(blocks[m], 'region', [(i, i ^ m) for i in range(regions)])  8.11 us
    ppermute x1, waiting for transfers between devices, on_device(): other = lax.ppermute(sent, 'stn', [(i, i ^ step) for i in range(count)])  2.83 us
    pallas_call x1, Pallas kernels, pack(): pl.pallas_call(kernel, out_shape=block_shapes(regions, (nch, segment + fi...  2.11 us
    pallas_call x1, Pallas kernels, early_spectra(): pl.pallas_call(kernel, out_shape=jax.ShapeDtypeStruct((number * cutter.sp...  1.82 us
    ppermute x1, starting transfers between devices, on_device(): other = lax.ppermute(sent, 'stn', [(i, i ^ step) for i in range(count)])  1.56 us
    ppermute x1, waiting for transfers between devices, on_device(): swapped = lax.ppermute(given, 'chan', swap)  1.56 us
  transfers between devices with their start and end apart: 9, of which 7 were waited for; matrix products, arithmetic and copies ran while one was open for 2% of the time, Pallas kernels for 8%

profile of v6, /device:TPU:0, one launch (start us, length us, event | category | flops | bytes accessed | tf_op | source)
XLA Modules:
  0.0 42.5 jit_solution(7415143934972982998)
XLA Ops:
  1.3 0.0 copy-start
  1.3 2.1 %pack.1 = (bf16[4,8704]{1,0:T(4,128)(2,1)}, bf16[4,8704]{1,0:T(4,128)(2,1)}, bf16[4,8704]{1,0:T(4,128)(2,1)}, bf16[4,8704]{1,0:T(4,128)(2,1)}) custom-call(bf16[10,3,8192]{2,1,0:T(4,128)(2,1)} %archive.1, s32[1,64]{1,0:T(1,128)} %bitcast.24, s32[20,256]{1,0:T(8,128)} %bitcast.19, s32[1,512]{1,0:T(1,128)} %bitcast.22, s32[1,512]{1,0:T(1,128)} %bitcast.23, ...), custom_call_target="tpu_custom_call" | custom-call | tf_op jit(solution)/shard_map/pack/pallas_call | solution.py:150
  3.4 3.1 %collective-permute-start = (bf16[4,8704]{1,0:T(4,128)(2,1)}, bf16[4,8704]{1,0:T(4,128)(2,1)S(1)}, u32[]{:S(2)}, u32[]{:S(2)}) collective-permute-start(bf16[4,8704]{1,0:T(4,128)(2,1)} %get-tuple-element.11), channel_id=1, source_target_pairs={{0,4},{4,0},{8,12},{12,8},{1,5},{5,1},{9,13},{13,9},{2,6},{6,2},{1... | collective-permute-start | bytes 208904 | tf_op jit(solution)/shard_map/ppermute | solution.py:94
  6.5 2.6 %collective-permute-start.1 = (bf16[4,8704]{1,0:T(4,128)(2,1)}, bf16[4,8704]{1,0:T(4,128)(2,1)S(1)}, u32[]{:S(2)}, u32[]{:S(2)}) collective-permute-start(bf16[4,8704]{1,0:T(4,128)(2,1)} %get-tuple-element.12), channel_id=1, source_target_pairs={{0,8},{4,12},{8,0},{12,4},{1,9},{5,13},{9,1},{13,5},{2,10},{6,14},... | collective-permute-start | bytes 208904 | tf_op jit(solution)/shard_map/ppermute | solution.py:94
  9.0 0.0 collective-permute-start.2
  9.1 0.1 add.74
  9.1 0.0 copy-start.4
  9.1 0.1 add.75
  9.2 0.6 %copy-done.4 = s32[256]{0:T(256)S(1)} copy-done((s32[256]{0:T(256)S(1)}, s32[256]{0:T(256)}, u32[]{:S(2)}) %copy-start.4) | copy-done | bytes 1048
  9.8 0.1 eq.15
  9.9 0.1 fusion.3
  10.0 0.1 reduce_window_sum.11
  10.1 0.0 copy-start.3
  10.1 0.0 copy-start.2
  10.2 0.2 select_reduce_fusion
  10.4 0.1 reduce_sum.12
  10.5 0.4 copy-done.3
  10.9 1.5 %describe.1 = (f32[512,128]{1,0:T(8,128)S(1)}, f32[1024,128]{1,0:T(8,128)S(1)}) custom-call(s32[20,256]{1,0:T(8,128)S(1)} %bitcast.20, s32[4]{0:T(128)S(1)} %and_select_fusion.station, s32[1,256]{1,0:T(1,128)S(1)} %bitcast.21), custom_call_target="tpu_custom_call" | custom-call | tf_op jit(solution)/shard_map/describe/pallas_call | solution.py:185
  12.4 0.0 collective-permute-done.refs_1_
  12.4 0.0 copy-done
  12.4 0.0 copy-done.2
  12.4 0.0 copy-start.1
  12.4 1.8 %early_spectra.1.refs_4_ = f32[2048,128]{1,0:T(8,128)S(1)} custom-call(bf16[4,8704]{1,0:T(4,128)(2,1)S(1)} %copy-done.2, bf16[4,8704]{1,0:T(4,128)(2,1)S(1)} %collective-permute-done.refs_1_, f32[1024,128]{1,0:T(8,128)S(1)} %get-tuple-element.14.refs_2_.refs_6_, bf16[512,512]{1,0:T(8,128)(2,1)S(1)} %copy-done), custom_call_target="tpu_custom_call" | custom-call | tf_op jit(solution)/shard_map/early_spectra/pallas_call | solution.py:292
  14.3 0.0 collective-permute-done.1.refs_2_
  14.3 1.2 %collective-permute-done.2.refs_3_ = bf16[4,8704]{1,0:T(4,128)(2,1)S(1)} collective-permute-done((bf16[4,8704]{1,0:T(4,128)(2,1)}, bf16[4,8704]{1,0:T(4,128)(2,1)S(1)}, u32[]{:S(2)}, u32[]{:S(2)}) %collective-permute-start.2) | collective-permute-done | bytes 69664 | tf_op jit(solution)/shard_map/ppermute | solution.py:94
  15.5 0.0 copy-done.1
  15.5 8.3 %correlate.1 = (f32[4,56,640]{2,1,0:T(8,128)S(1)}, bf16[4,56,640]{2,1,0:T(8,128)(2,1)S(1)}) custom-call(bf16[4,8704]{1,0:T(4,128)(2,1)S(1)} %copy-done.2, bf16[4,8704]{1,0:T(4,128)(2,1)S(1)} %collective-permute-done.refs_1_, bf16[4,8704]{1,0:T(4,128)(2,1)S(1)} %collective-permute-done.1.refs_2_, bf16[4,8704]{1,0:T(4,128)(2,1)S(1)} %collective-permute-done.2.refs_3_, ...), custom_call_target="tpu_custom_call" | custom-call | tf_op jit(solution)/shard_map/correlate/pallas_call | solution.py:548
  23.8 0.1 collective-permute-start.3
  23.9 1.6 %collective-permute-done.3 = bf16[4,56,640]{2,1,0:T(8,128)(2,1)S(1)} collective-permute-done((bf16[4,56,640]{2,1,0:T(8,128)(2,1)S(1)}, bf16[4,56,640]{2,1,0:T(8,128)(2,1)S(1)}, u32[]{:S(2)}, u32[]{:S(2)}) %collective-permute-start.3) | collective-permute-done | bytes 286752 | tf_op jit(solution)/shard_map/ppermute | solution.py:552
  25.5 0.9 %collective-permute-start.4 = (bf16[56,640]{1,0:T(8,128)(2,1)S(1)}, bf16[56,640]{1,0:T(8,128)(2,1)S(1)}, u32[]{:S(2)}, u32[]{:S(2)}) collective-permute-start(bf16[56,640]{1,0:T(8,128)(2,1)S(1)} %get-tuple-element.18), channel_id=1, source_target_pairs={{0,4},{4,0},{8,12},{12,8},{1,5},{5,1},{9,13},{13,9},{2,6},{6,2},{1... | collective-permute-start | bytes 215048 | tf_op jit(solution)/shard_map/ppermute | solution.py:94
  26.3 2.5 %collective-permute-start.6 = (bf16[56,640]{1,0:T(8,128)(2,1)S(1)}, bf16[56,640]{1,0:T(8,128)(2,1)S(1)}, u32[]{:S(2)}, u32[]{:S(2)}) collective-permute-start(bf16[56,640]{1,0:T(8,128)(2,1)S(1)} %get-tuple-element.19), channel_id=1, source_target_pairs={{0,12},{4,8},{8,4},{12,0},{1,13},{5,9},{9,5},{13,1},{2,14},{6,10},... | collective-permute-start | bytes 215048 | tf_op jit(solution)/shard_map/ppermute | solution.py:94
  28.8 0.2 collective-permute-start.5
  29.0 0.8 %collective-permute-done.4 = bf16[56,640]{1,0:T(8,128)(2,1)S(1)} collective-permute-done((bf16[56,640]{1,0:T(8,128)(2,1)S(1)}, bf16[56,640]{1,0:T(8,128)(2,1)S(1)}, u32[]{:S(2)}, u32[]{:S(2)}) %collective-permute-start.4) | collective-permute-done | bytes 71712 | tf_op jit(solution)/shard_map/ppermute | solution.py:94
  29.8 3.4 %collective-permute-done.6 = bf16[56,640]{1,0:T(8,128)(2,1)S(1)} collective-permute-done((bf16[56,640]{1,0:T(8,128)(2,1)S(1)}, bf16[56,640]{1,0:T(8,128)(2,1)S(1)}, u32[]{:S(2)}, u32[]{:S(2)}) %collective-permute-start.6) | collective-permute-done | bytes 71712 | tf_op jit(solution)/shard_map/ppermute | solution.py:94
  33.3 2.6 %collective-permute-done.5 = bf16[56,640]{1,0:T(8,128)(2,1)S(1)} collective-permute-done((bf16[56,640]{1,0:T(8,128)(2,1)S(1)}, bf16[56,640]{1,0:T(8,128)(2,1)S(1)}, u32[]{:S(2)}, u32[]{:S(2)}) %collective-permute-start.5) | collective-permute-done | bytes 71712 | tf_op jit(solution)/shard_map/ppermute | solution.py:94
  35.9 0.1 fusion.2
  36.0 1.6 %collective-permute-start.7 = (bf16[56,640]{1,0:T(8,128)(2,1)S(1)}, bf16[56,640]{1,0:T(8,128)(2,1)S(1)}, u32[]{:S(2)}, u32[]{:S(2)}) collective-permute-start(bf16[56,640]{1,0:T(8,128)(2,1)S(1)} %fusion.2), channel_id=1, source_target_pairs={{0,2},{2,0},{1,3},{3,1},{4,6},{6,4},{5,7},{7,5},{8,10},{10,8},{9,1... | collective-permute-start | bytes 215048 | tf_op jit(solution)/shard_map/ppermute | solution.py:566
  37.5 2.8 %collective-permute-done.7 = bf16[56,640]{1,0:T(8,128)(2,1)S(1)} collective-permute-done((bf16[56,640]{1,0:T(8,128)(2,1)S(1)}, bf16[56,640]{1,0:T(8,128)(2,1)S(1)}, u32[]{:S(2)}, u32[]{:S(2)}) %collective-permute-start.7) | collective-permute-done | bytes 71712 | tf_op jit(solution)/shard_map/ppermute | solution.py:566
  40.4 0.1 collective-permute-start.8
  40.5 1.4 %collective-permute-done.8.other = f32[56,640]{1,0:T(8,128)S(1)} collective-permute-done((f32[56,640]{1,0:T(8,128)S(1)}, f32[56,640]{1,0:T(8,128)S(1)}, u32[]{:S(2)}, u32[]{:S(2)}) %collective-permute-start.8) | collective-permute-done | bytes 143392 | tf_op jit(solution)/shard_map/ppermute | solution.py:569
  41.8 0.7 %assemble.1 = (f32[101,512]{1,0:T(8,128)}, f32[101,128]{1,0:T(8,128)}) custom-call(f32[56,640]{1,0:T(8,128)S(1)} %convert_add_fusion.whole, f32[56,640]{1,0:T(8,128)S(1)} %collective-permute-done.8.other), custom_call_target="tpu_custom_call" | custom-call | tf_op jit(solution)/shard_map/assemble/pallas_call | solution.py:507
  (5 shorter events, 0.1 us)
Async XLA Ops:
  1.3 11.1 %copy-start = (bf16[512,512]{1,0:T(8,128)(2,1)S(1)}, bf16[512,512]{1,0:T(8,128)(2,1)}, u32[]{:S(2)}) copy-start(bf16[512,512]{1,0:T(8,128)(2,1)} %constant.47.refs_3_.refs_7_) | copy-start | bytes 1572868
  3.4 9.0 %collective-permute-start = (bf16[4,8704]{1,0:T(4,128)(2,1)}, bf16[4,8704]{1,0:T(4,128)(2,1)S(1)}, u32[]{:S(2)}, u32[]{:S(2)}) collective-permute-start(bf16[4,8704]{1,0:T(4,128)(2,1)} %get-tuple-element.11), channel_id=1, source_target_pairs={{0,4},{4,0},{8,12},{12,8},{1,5},{5,1},{9,13},{13,9},{2,6},{6,2},{1... | collective-permute-start | bytes 208904 | tf_op jit(solution)/shard_map/ppermute | solution.py:94
  6.5 7.8 %collective-permute-start.1 = (bf16[4,8704]{1,0:T(4,128)(2,1)}, bf16[4,8704]{1,0:T(4,128)(2,1)S(1)}, u32[]{:S(2)}, u32[]{:S(2)}) collective-permute-start(bf16[4,8704]{1,0:T(4,128)(2,1)} %get-tuple-element.12), channel_id=1, source_target_pairs={{0,8},{4,12},{8,0},{12,4},{1,9},{5,13},{9,1},{13,5},{2,10},{6,14},... | collective-permute-start | bytes 208904 | tf_op jit(solution)/shard_map/ppermute | solution.py:94
  9.0 6.4 %collective-permute-start.2 = (bf16[4,8704]{1,0:T(4,128)(2,1)}, bf16[4,8704]{1,0:T(4,128)(2,1)S(1)}, u32[]{:S(2)}, u32[]{:S(2)}) collective-permute-start(bf16[4,8704]{1,0:T(4,128)(2,1)} %get-tuple-element.13), channel_id=1, source_target_pairs={{0,12},{4,8},{8,4},{12,0},{1,13},{5,9},{9,5},{13,1},{2,14},{6,10},... | collective-permute-start | bytes 208904 | tf_op jit(solution)/shard_map/ppermute | solution.py:94
  9.1 0.7 %copy-start.4 = (s32[256]{0:T(256)S(1)}, s32[256]{0:T(256)}, u32[]{:S(2)}) copy-start(s32[256]{0:T(256)} %param.11) | copy-start | bytes 3076
  10.1 0.7 %copy-start.3 = (s32[256,20]{0,1:T(8,128)S(1)}, s32[256,20]{0,1:T(8,128)}, u32[]{:S(2)}) copy-start(s32[256,20]{0,1:T(8,128)} %param.12) | copy-start | bytes 61444
  10.1 2.3 %copy-start.2 = (bf16[4,8704]{1,0:T(4,128)(2,1)S(1)}, bf16[4,8704]{1,0:T(4,128)(2,1)}, u32[]{:S(2)}) copy-start(bf16[4,8704]{1,0:T(4,128)(2,1)} %get-tuple-element.10.refs_0_) | copy-start | bytes 208900
  12.4 3.1 %copy-start.1 = (bf16[2,256,512]{2,1,0:T(8,128)(2,1)S(1)}, bf16[2,256,512]{2,1,0:T(8,128)(2,1)}, u32[]{:S(2)}) copy-start(bf16[2,256,512]{2,1,0:T(8,128)(2,1)} %constant.52.refs_8_) | copy-start | bytes 1572868
  23.8 1.6 %collective-permute-start.3 = (bf16[4,56,640]{2,1,0:T(8,128)(2,1)S(1)}, bf16[4,56,640]{2,1,0:T(8,128)(2,1)S(1)}, u32[]{:S(2)}, u32[]{:S(2)}) collective-permute-start(bf16[4,56,640]{2,1,0:T(8,128)(2,1)S(1)} %get-tuple-element.17), channel_id=1, source_target_pairs={{0,1},{1,0},{2,3},{3,2},{4,5},{5,4},{6,7},{7,6},{8,9},{9,8},{10,11... | collective-permute-start | bytes 860168 | tf_op jit(solution)/shard_map/ppermute | solution.py:552
  25.5 4.4 %collective-permute-start.4 = (bf16[56,640]{1,0:T(8,128)(2,1)S(1)}, bf16[56,640]{1,0:T(8,128)(2,1)S(1)}, u32[]{:S(2)}, u32[]{:S(2)}) collective-permute-start(bf16[56,640]{1,0:T(8,128)(2,1)S(1)} %get-tuple-element.18), channel_id=1, source_target_pairs={{0,4},{4,0},{8,12},{12,8},{1,5},{5,1},{9,13},{13,9},{2,6},{6,2},{1... | collective-permute-start | bytes 215048 | tf_op jit(solution)/shard_map/ppermute | solution.py:94
  26.3 7.0 %collective-permute-start.6 = (bf16[56,640]{1,0:T(8,128)(2,1)S(1)}, bf16[56,640]{1,0:T(8,128)(2,1)S(1)}, u32[]{:S(2)}, u32[]{:S(2)}) collective-permute-start(bf16[56,640]{1,0:T(8,128)(2,1)S(1)} %get-tuple-element.19), channel_id=1, source_target_pairs={{0,12},{4,8},{8,4},{12,0},{1,13},{5,9},{9,5},{13,1},{2,14},{6,10},... | collective-permute-start | bytes 215048 | tf_op jit(solution)/shard_map/ppermute | solution.py:94
  28.8 7.1 %collective-permute-start.5 = (bf16[56,640]{1,0:T(8,128)(2,1)S(1)}, bf16[56,640]{1,0:T(8,128)(2,1)S(1)}, u32[]{:S(2)}, u32[]{:S(2)}) collective-permute-start(bf16[56,640]{1,0:T(8,128)(2,1)S(1)} %get-tuple-element.20), channel_id=1, source_target_pairs={{0,8},{4,12},{8,0},{12,4},{1,9},{5,13},{9,1},{13,5},{2,10},{6,14},... | collective-permute-start | bytes 215048 | tf_op jit(solution)/shard_map/ppermute | solution.py:94
  36.0 4.4 %collective-permute-start.7 = (bf16[56,640]{1,0:T(8,128)(2,1)S(1)}, bf16[56,640]{1,0:T(8,128)(2,1)S(1)}, u32[]{:S(2)}, u32[]{:S(2)}) collective-permute-start(bf16[56,640]{1,0:T(8,128)(2,1)S(1)} %fusion.2), channel_id=1, source_target_pairs={{0,2},{2,0},{1,3},{3,1},{4,6},{6,4},{5,7},{7,5},{8,10},{10,8},{9,1... | collective-permute-start | bytes 215048 | tf_op jit(solution)/shard_map/ppermute | solution.py:566
  40.4 1.4 %collective-permute-start.8 = (f32[56,640]{1,0:T(8,128)S(1)}, f32[56,640]{1,0:T(8,128)S(1)}, u32[]{:S(2)}, u32[]{:S(2)}) collective-permute-start(f32[56,640]{1,0:T(8,128)S(1)} %convert_add_fusion.whole), channel_id=1, source_target_pairs={{0,1},{1,0},{2,3},{3,2},{4,5},{5,4},{6,7},{7,6},{8,9},{9,8},{10,11... | collective-permute-start | bytes 430088 | tf_op jit(solution)/shard_map/ppermute | solution.py:569

commit v7 on v6

--- a/solution.py
+++ b/solution.py
@@ -15,8 +15,9 @@
 LAGS = 101
 BINS = NFFT // 2
 LANES = 128
-LAG_ROWS = 112
-HALF_ROWS = LAG_ROWS // 2
+HALF_LAGS = 51
+HALF_ROWS = 56
+TILE_ROWS = 48
 VMEM_ONLY = pl.BlockSpec(memory_space=pltpu.VMEM)
 SMEM_ONLY = pl.BlockSpec(memory_space=pltpu.SMEM)
 NT = (((1,), (1,)), ((), ()))
@@ -35,7 +36,7 @@
 
 
 def lag_table():
-    shift = np.arange(LAG_ROWS)[:, None] - MAXLAG
+    shift = np.arange(2 * HALF_LAGS)[:, None] - MAXLAG
     freq = np.arange(BINS)[None, :]
     angle = (freq * shift % NFFT) * (2.0 * math.pi / NFFT)
     weight = np.where(freq == 0, 1.0 / NFFT, 2.0 / NFFT)
@@ -44,8 +45,9 @@
     odd[:, 0] = (np.cos(math.pi * (shift[:, 0] % 2)) - 1.0) / NFFT
     table = np.concatenate([even, odd], axis=1) * math.sqrt(WIN)
     table[LAGS:] = 0.0
-    filler = np.zeros((LANES - LAG_ROWS, NFFT))
-    halves = table[:HALF_ROWS], table[HALF_ROWS:]
+    gap = np.zeros((HALF_ROWS - HALF_LAGS, NFFT))
+    filler = np.zeros((LANES - 2 * HALF_ROWS, NFFT))
+    halves = [np.concatenate([table[:HALF_LAGS], gap]), np.concatenate([table[HALF_LAGS:], gap])]
     table = np.stack([np.concatenate([halves[c], halves[1 - c], filler]) for c in range(2)])
     table = jnp.asarray(table, jnp.float32)
     high = table.astype(jnp.bfloat16)
@@ -70,6 +72,20 @@
     return (value >> 7).astype(jnp.float32).astype(jnp.bfloat16), (value & 127).astype(jnp.float32).astype(jnp.bfloat16)
 
 
+def folded_rows(width):
+    tiles = width // LANES
+    return -(-HALF_LAGS * tiles // 16) * 16
+
+
+def fold(value, store, first, tiles):
+    for k in range(value.shape[1] // LANES):
+        piece = value[:HALF_LAGS, k * LANES : (k + 1) * LANES]
+        t = first + k
+        store[t * TILE_ROWS : (t + 1) * TILE_ROWS, :] = piece[:TILE_ROWS]
+        row = tiles * TILE_ROWS + t * (HALF_LAGS - TILE_ROWS)
+        store[row : row + HALF_LAGS - TILE_ROWS, :] = piece[TILE_ROWS:]
+
+
 def digit_count(events):
     return 1 if events <= 256 else 2
 
@@ -108,21 +124,21 @@
     per_block = starts.shape[1]
     pair_cap = pair_first.shape[1]
     share = station_share(stations, chans)
-
-    def kernel(archive, starts, mask, first, second, count, *rest):
-        outs, flat = rest[:-1], rest[-1]
+    number = regions if separate(regions) else 1
+
+    def kernel(*refs):
+        sources, count, outs, refs = refs[:5], refs[5], refs[6 : 6 + number], refs[6 + number :]
+        flat, archive, starts, mask, first, second, sems = refs
         region = lax.axis_index("region")
         chan = lax.axis_index("chan")
         base = jnp.minimum(chan * share, stations - share)
-        for block in range(share * COMP // nch, regions):
-            flat[block] = jnp.zeros((nch, segment), jnp.float32)
-        for station in range(share):
-            data = archive[base + station].astype(jnp.float32)
-            row = station * COMP
-            while row < (station + 1) * COMP:
-                end = min((row // nch + 1) * nch, (station + 1) * COMP)
-                flat[row // nch, row % nch : row % nch + end - row, :] = data[row - station * COMP : end - station * COMP]
-                row = end
+        sources = (sources[0].at[pl.ds(base, share)],) + sources[1:]
+        copies = [pltpu.make_async_copy(source, target, sems.at[k])
+                  for k, (source, target) in enumerate(zip(sources, (archive, starts, mask, first, second)))]
+        for copy in copies:
+            copy.start()
+        for copy in copies[1:]:
+            copy.wait()
         names = lax.broadcasted_iota(jnp.int32, (events, pair_cap), 0)
         usable = mask[...].astype(jnp.float32).astype(jnp.bfloat16)
         chosen = [jnp.dot(usable, as_bf16(names == ref[...]), preferred_element_type=jnp.float32)
@@ -140,6 +156,16 @@
         else:
             fields = list(digits_of(first[...]) + digits_of(second[...]))
         fields += [code, scalars]
+        copies[0].wait()
+        for block in range(share * COMP // nch, regions):
+            flat[block] = jnp.zeros((nch, segment), jnp.float32)
+        for station in range(share):
+            data = archive[station].astype(jnp.float32)
+            row = station * COMP
+            while row < (station + 1) * COMP:
+                end = min((row // nch + 1) * nch, (station + 1) * COMP)
+                flat[row // nch, row % nch : row % nch + end - row, :] = data[row - station * COMP : end - station * COMP]
+                row = end
         for m in range(regions):
             out = outs[m] if separate(regions) else outs[0].at[m]
             out[:, :segment] = flat[region ^ m].astype(jnp.bfloat16)
@@ -150,9 +176,17 @@
     return pl.pallas_call(
         kernel,
         out_shape=block_shapes(regions, (nch, segment + field_width(events, pair_cap)), jnp.bfloat16),
-        in_specs=[VMEM_ONLY] * 5 + [SMEM_ONLY],
-        out_specs=[VMEM_ONLY] * (regions if separate(regions) else 1),
-        scratch_shapes=[pltpu.VMEM((regions, nch, segment), jnp.float32)],
+        in_specs=[pl.BlockSpec(memory_space=pltpu.HBM)] * 5 + [SMEM_ONLY],
+        out_specs=[VMEM_ONLY] * number,
+        scratch_shapes=[
+            pltpu.VMEM((regions, nch, segment), jnp.float32),
+            pltpu.VMEM((share, COMP, segment), archive.dtype),
+            pltpu.VMEM(starts.shape, jnp.int32),
+            pltpu.VMEM(station_mask.shape, jnp.int32),
+            pltpu.VMEM(pair_first.shape, jnp.int32),
+            pltpu.VMEM(pair_first.shape, jnp.int32),
+            pltpu.SemaphoreType.DMA((5,)),
+        ],
         name="pack",
     )(archive, starts, station_mask, pair_first, pair_second, pair_count)
 
@@ -177,14 +211,15 @@
         def one_region(part, carry):
             hit = as_bf16(place + part * slots == slot_lane)
             high, low = (jnp.dot(hit, digit, preferred_element_type=jnp.float32) for digit in names)
-            slot_event[pl.ds(pl.multiple_of(part * slots, slots), slots), :] = high * 128.0 + low - 1.0
+            event = high * 128.0 + low - 1.0
+            slot_event[pl.ds(pl.multiple_of(part * slots, slots), slots), :] = event.astype(slot_event.dtype)
             return carry
 
         lax.fori_loop(0, regions, one_region, 0)
 
     return pl.pallas_call(
         kernel,
-        out_shape=(jax.ShapeDtypeStruct((regions * slots, LANES), jnp.float32),
+        out_shape=(jax.ShapeDtypeStruct((regions * slots, LANES), jnp.bfloat16 if digit_count(events) == 1 else jnp.float32),
                    jax.ShapeDtypeStruct((events * nch, LANES), jnp.float32)),
         in_specs=[VMEM_ONLY, SMEM_ONLY, VMEM_ONLY],
         out_specs=(VMEM_ONLY, VMEM_ONLY),
@@ -311,6 +346,7 @@
     rows, tiles = cutter.rows, cutter.tiles
     events = regions * per_block
     cols = pair_cap // LANES
+    width = cols + slots // LANES
     batch = regions if separate(regions) else 1
     digits = digit_count(events)
     static = separate(regions)
@@ -321,7 +357,7 @@
     def kernel(*refs):
         received, refs = refs[:sources], refs[sources:]
         (ready_spec, slot_event, weight_rows, table, weights, kept, given, shifted, windows, spec, prod, index_vmem, index,
-         profile, sem) = refs if ready else (None,) + refs
+         profile, folded, sem) = refs if ready else (None,) + refs
         region = lax.axis_index("region")
 
         def recv(m):
@@ -360,7 +396,6 @@
                 return carry
 
             lax.fori_loop(0, regions, widen, 0)
-        profile[...] = jnp.zeros_like(profile)
         copy.wait()
 
         def cut(slot, carry):
@@ -426,21 +461,26 @@
                 code = field(part, 2 * digits)
                 live = jnp.maximum((code - 1.0) * COMP, 1.0)
                 stack = jnp.where(code > 0.0, cross * lax.rsqrt(live), 0.0)
-                kept[part, :, :pair_cap] = stack[:HALF_ROWS]
-                given[part, :, :pair_cap] = stack[HALF_ROWS:LAG_ROWS].astype(jnp.bfloat16)
+                fold(stack[:HALF_ROWS], kept.at[part], 0, width)
+                fold(stack[HALF_ROWS:], folded.at[part], 0, width)
                 first, second = listed(part, 0), listed(part, 1)
                 stack = stack.astype(jnp.bfloat16)
 
-                def gathered(owner, event):
+                def hot(owner, event):
                     column = slot_event[pl.ds(pl.multiple_of(owner * slots, slots), slots), :]
-                    hot = as_bf16(jnp.concatenate([column] * cols, axis=1) == event)
-                    return lax.dot_general(stack, hot, NT, preferred_element_type=jnp.float32)
+                    column = jnp.concatenate([column] * cols, axis=1)
+                    if digits > 1:
+                        return as_bf16(column == event)
+                    event = jnp.broadcast_to(event.astype(jnp.bfloat16), column.shape)
+                    return jnp.where(column == event, jnp.ones((), jnp.bfloat16), jnp.zeros((), jnp.bfloat16))
 
                 owner = part ^ region
                 after = (owner + 1) & (regions - 1)
-                profile[0, part] += gathered(owner, first)
-                profile[1, part] += gathered(owner, second)
-                profile[1, after ^ region] += gathered(after, second)
+                hots = jnp.concatenate([hot(owner, first), hot(owner, second), hot(after, second)], axis=0)
+                terms = lax.dot_general(stack, hots, NT, preferred_element_type=jnp.float32)
+                profile[0, part] = terms[:, :slots]
+                profile[1, part] = terms[:, slots : 2 * slots]
+                profile[2, after ^ region] = terms[:, 2 * slots :]
             return carry
 
         if static:
@@ -449,27 +489,27 @@
             lax.fori_loop(0, regions, one_group, 0)
         def lag_of(axis):
             row = lax.broadcasted_iota(jnp.int32, (LANES, LANES), axis)
-            return jnp.where(row < HALF_ROWS, row + chan * HALF_ROWS, row - chan * HALF_ROWS)
+            return jnp.where(row < HALF_ROWS, row + chan * HALF_LAGS, row - HALF_ROWS + (1 - chan) * HALF_LAGS)
 
         mirror = as_bf16(lag_of(0) + lag_of(1) == LAGS - 1)
 
         def finish(part, carry):
-            value = profile[1, part]
+            value = profile[1, part] + profile[2, part]
             high = value.astype(jnp.bfloat16)
             low = (value - high.astype(jnp.float32)).astype(jnp.bfloat16)
             flipped = jnp.dot(mirror, high, preferred_element_type=jnp.float32) + jnp.dot(
                 mirror, low, preferred_element_type=jnp.float32)
             total = profile[0, part] + flipped
-            kept[part, :, pair_cap:] = total[:HALF_ROWS]
-            given[part, :, pair_cap:] = total[HALF_ROWS:LAG_ROWS].astype(jnp.bfloat16)
+            fold(total[:HALF_ROWS], kept.at[part], cols, width)
+            fold(total[HALF_ROWS:], folded.at[part], cols, width)
+            given[part] = folded[part].astype(jnp.bfloat16)
             return carry
 
         lax.fori_loop(0, regions, finish, 0)
 
-    shape = (regions, HALF_ROWS, pair_cap + slots)
+    shape = (regions, folded_rows(pair_cap + slots), LANES)
     index_rows = 8 * -(-(2 * cols + 2) // 8)
-    width = (pair_cap + slots) // LANES
-    used = regions * (tiles * rows + LAG_ROWS * width + 2 * LANES + index_rows + 4 * tiles + slots) + ready * cutter.spec_rows
+    used = regions * (tiles * rows + 3 * HALF_ROWS * width + 3 * LANES + index_rows + 4 * tiles + slots) + ready * cutter.spec_rows
     used += (2 * per_block * batch + 2 * events + batch * pair_cap) * rows + events * nch + 3 * NFFT
     return pl.pallas_call(
         kernel,
@@ -483,7 +523,8 @@
             pltpu.VMEM((batch * pair_cap * rows, LANES), jnp.float32),
             pltpu.VMEM((regions, index_rows, LANES), jnp.int32),
             pltpu.SMEM((regions, index_rows, LANES), jnp.int32),
-            pltpu.VMEM((2, regions, LANES, slots), jnp.float32),
+            pltpu.VMEM((3, regions, LANES, slots), jnp.float32),
+            pltpu.VMEM(shape, jnp.float32),
             pltpu.SemaphoreType.DMA(()),
         ],
         compiler_params=pltpu.CompilerParams(vmem_limit_bytes=grant(used)),
@@ -491,26 +532,29 @@
     )
 
 
-def assemble(whole, other, pair_cap):
-    rest = LAGS - HALF_ROWS
+def assemble(whole, other, pair_cap, slots):
+    tiles = pair_cap // LANES + slots // LANES
 
     def kernel(whole, other, stack, profile):
         first = lax.axis_index("chan") == 0
-        low = jnp.where(first, whole[...], other[...])
-        high = jnp.where(first, other[...], whole[...])
-        stack[:HALF_ROWS, :] = low[:, :pair_cap]
-        stack[HALF_ROWS:, :] = high[:rest, :pair_cap]
-        profile[:HALF_ROWS, :] = low[:, pair_cap:]
-        profile[HALF_ROWS:, :] = high[:rest, pair_cap:]
-
-    width = whole.shape[1]
+        halves = jnp.where(first, whole[...], other[...]), jnp.where(first, other[...], whole[...])
+        for t in range(tiles):
+            out, column = (stack, t * LANES) if t * LANES < pair_cap else (profile, t * LANES - pair_cap)
+            lanes = pl.ds(column, LANES)
+            for h, half in enumerate(halves):
+                lag = h * HALF_LAGS
+                out[lag : lag + TILE_ROWS, lanes] = half[t * TILE_ROWS : (t + 1) * TILE_ROWS]
+                row = tiles * TILE_ROWS + t * (HALF_LAGS - TILE_ROWS)
+                count = min(HALF_LAGS, LAGS - lag) - TILE_ROWS
+                out[lag + TILE_ROWS : lag + TILE_ROWS + count, lanes] = half[row : row + count]
+
     return pl.pallas_call(
         kernel,
         out_shape=(jax.ShapeDtypeStruct((LAGS, pair_cap), jnp.float32),
-                   jax.ShapeDtypeStruct((LAGS, width - pair_cap), jnp.float32)),
+                   jax.ShapeDtypeStruct((LAGS, slots), jnp.float32)),
         in_specs=[VMEM_ONLY] * 2,
         out_specs=(VMEM_ONLY, VMEM_ONLY),
-        compiler_params=pltpu.CompilerParams(vmem_limit_bytes=grant(4 * LAG_ROWS * width // LANES)),
+        compiler_params=pltpu.CompilerParams(vmem_limit_bytes=grant(8 * HALF_ROWS * tiles)),
         name="assemble",
     )(whole, other)
 
@@ -567,7 +611,7 @@
         whole = sent.astype(jnp.float32) + other.astype(jnp.float32)
         step *= 2
     other = lax.ppermute(whole, "chan", swap)
-    return assemble(whole, other, pair_cap)
+    return assemble(whole, other, pair_cap, slots)
 
 
 def solution(mesh):

time: 42.8 us -> 41.8 us (0.977)
  waiting for transfers between devices: 13.9 us -> 13.3 us
  Pallas kernels: 14.5 us -> 14 us
    ppermute x6, waiting for transfers between devices: 8.11 us -> 7.64 us  [exchange(): lax.ppermute(blocks[m], 'region', [(i, i ^ m) for i in range(regions)])]
where the time goes in v7:
time: 41.8 us; the launch traced here: 41.6 us
  Pallas kernels  14 us (33%)
  waiting for transfers between devices  13.3 us (32%)
  starting transfers between devices  11 us (26%)
  between operations  1.42 us (3%)
  local copies, waits for them, and re-layouts  1.32 us (3%)
  other arithmetic  0.6 us (1%)
    ppermute x6, starting transfers between devices, exchange(): lax.ppermute(blocks[m], 'region', [(i, i ^ m) for i in range(regions)])  9.26 us
    pallas_call x1, Pallas kernels, on_device(): correlate(regions, per_block, pair_cap, segment, slots, nch, ready)  7.98 us
    ppermute x6, waiting for transfers between devices, exchange(): lax.ppermute(blocks[m], 'region', [(i, i ^ m) for i in range(regions)])  7.64 us
    ppermute x1, waiting for transfers between devices, on_device(): other = lax.ppermute(sent, 'stn', [(i, i ^ step) for i in range(count)])  2.78 us
    pallas_call x1, Pallas kernels, pack(): pl.pallas_call(kernel, out_shape=block_shapes(regions, (nch, segment + fi...  1.97 us
    pallas_call x1, Pallas kernels, early_spectra(): pl.pallas_call(kernel, out_shape=jax.ShapeDtypeStruct((number * cutter.sp...  1.82 us
    ppermute x1, starting transfers between devices, on_device(): other = lax.ppermute(sent, 'stn', [(i, i ^ step) for i in range(count)])  1.55 us
    ppermute x1, waiting for transfers between devices, on_device(): swapped = lax.ppermute(given, 'chan', swap)  1.52 us
  transfers between devices with their start and end apart: 9, of which 7 were waited for; matrix products, arithmetic and copies ran while one was open for 2% of the time, Pallas kernels for 8%

profile of v7, /device:TPU:0, one launch (start us, length us, event | category | flops | bytes accessed | tf_op | source)
XLA Modules:
  0.0 41.6 jit_solution(17876062571609605116)
XLA Ops:
  1.3 0.0 copy-start
  1.3 2.0 %pack.1 = (bf16[4,8704]{1,0:T(4,128)(2,1)}, bf16[4,8704]{1,0:T(4,128)(2,1)}, bf16[4,8704]{1,0:T(4,128)(2,1)}, bf16[4,8704]{1,0:T(4,128)(2,1)}) custom-call(bf16[10,3,8192]{2,1,0:T(4,128)(2,1)} %refs_0_.1, s32[1,64]{1,0:T(1,128)} %bitcast.24, s32[20,256]{1,0:T(8,128)} %bitcast.19, s32[1,512]{1,0:T(1,128)} %bitcast.22, s32[1,512]{1,0:T(1,128)} %bitcast.23, ...), custom_call_target="tpu_custom_call" | custom-call | tf_op jit(solution)/shard_map/pack/pallas_call | solution.py:176
  3.3 3.1 %collective-permute-start = (bf16[4,8704]{1,0:T(4,128)(2,1)}, bf16[4,8704]{1,0:T(4,128)(2,1)S(1)}, u32[]{:S(2)}, u32[]{:S(2)}) collective-permute-start(bf16[4,8704]{1,0:T(4,128)(2,1)} %get-tuple-element.11), channel_id=1, source_target_pairs={{0,4},{4,0},{8,12},{12,8},{1,5},{5,1},{9,13},{13,9},{2,6},{6,2},{1... | collective-permute-start | bytes 208904 | tf_op jit(solution)/shard_map/ppermute | solution.py:110
  6.4 2.6 %collective-permute-start.1 = (bf16[4,8704]{1,0:T(4,128)(2,1)}, bf16[4,8704]{1,0:T(4,128)(2,1)S(1)}, u32[]{:S(2)}, u32[]{:S(2)}) collective-permute-start(bf16[4,8704]{1,0:T(4,128)(2,1)} %get-tuple-element.12), channel_id=1, source_target_pairs={{0,8},{4,12},{8,0},{12,4},{1,9},{5,13},{9,1},{13,5},{2,10},{6,14},... | collective-permute-start | bytes 208904 | tf_op jit(solution)/shard_map/ppermute | solution.py:110
  9.0 0.0 collective-permute-start.2
  9.0 0.1 add.74
  9.1 0.0 copy-start.4
  9.1 0.1 add.75
  9.1 0.6 %copy-done.4 = s32[256]{0:T(256)S(1)} copy-done((s32[256]{0:T(256)S(1)}, s32[256]{0:T(256)}, u32[]{:S(2)}) %copy-start.4) | copy-done | bytes 1048
  9.7 0.1 eq.15
  9.8 0.1 fusion.3
  9.9 0.1 reduce_window_sum.11
  10.1 0.0 copy-start.3
  10.1 0.0 copy-start.2
  10.1 0.2 select_reduce_fusion
  10.3 0.1 reduce_sum.12
  10.4 0.4 copy-done.3
  10.8 1.5 %describe.1 = (bf16[512,128]{1,0:T(8,128)(2,1)S(1)}, f32[1024,128]{1,0:T(8,128)S(1)}) custom-call(s32[20,256]{1,0:T(8,128)S(1)} %bitcast.20, s32[4]{0:T(128)S(1)} %and_select_fusion.station, s32[1,256]{1,0:T(1,128)S(1)} %bitcast.21), custom_call_target="tpu_custom_call" | custom-call | tf_op jit(solution)/shard_map/describe/pallas_call | solution.py:220
  12.3 0.0 collective-permute-done.refs_1_
  12.3 0.0 copy-done
  12.3 0.0 copy-done.2
  12.3 0.0 copy-start.1
  12.4 1.8 %early_spectra.1.refs_4_ = f32[2048,128]{1,0:T(8,128)S(1)} custom-call(bf16[4,8704]{1,0:T(4,128)(2,1)S(1)} %copy-done.2, bf16[4,8704]{1,0:T(4,128)(2,1)S(1)} %collective-permute-done.refs_1_, f32[1024,128]{1,0:T(8,128)S(1)} %get-tuple-element.14.refs_2_.refs_6_, bf16[512,512]{1,0:T(8,128)(2,1)S(1)} %copy-done), custom_call_target="tpu_custom_call" | custom-call | tf_op jit(solution)/shard_map/early_spectra/pallas_call | solution.py:327
  14.2 0.0 collective-permute-done.1.refs_2_
  14.2 1.2 %collective-permute-done.2.refs_3_ = bf16[4,8704]{1,0:T(4,128)(2,1)S(1)} collective-permute-done((bf16[4,8704]{1,0:T(4,128)(2,1)}, bf16[4,8704]{1,0:T(4,128)(2,1)S(1)}, u32[]{:S(2)}, u32[]{:S(2)}) %collective-permute-start.2) | collective-permute-done | bytes 69664 | tf_op jit(solution)/shard_map/ppermute | solution.py:110
  15.4 0.0 copy-done.1
  15.4 8.0 %correlate.1 = (f32[4,256,128]{2,1,0:T(8,128)S(1)}, bf16[4,256,128]{2,1,0:T(8,128)(2,1)S(1)}) custom-call(bf16[4,8704]{1,0:T(4,128)(2,1)S(1)} %copy-done.2, bf16[4,8704]{1,0:T(4,128)(2,1)S(1)} %collective-permute-done.refs_1_, bf16[4,8704]{1,0:T(4,128)(2,1)S(1)} %collective-permute-done.1.refs_2_, bf16[4,8704]{1,0:T(4,128)(2,1)S(1)} %collective-permute-done.2.refs_3_, ...), custom_call_target="tpu_custom_call" | custom-call | tf_op jit(solution)/shard_map/correlate/pallas_call | solution.py:592
  23.4 0.1 collective-permute-start.3
  23.5 1.5 %collective-permute-done.3 = bf16[4,256,128]{2,1,0:T(8,128)(2,1)S(1)} collective-permute-done((bf16[4,256,128]{2,1,0:T(8,128)(2,1)S(1)}, bf16[4,256,128]{2,1,0:T(8,128)(2,1)S(1)}, u32[]{:S(2)}, u32[]{:S(2)}) %collective-permute-start.3) | collective-permute-done | bytes 262176 | tf_op jit(solution)/shard_map/ppermute | solution.py:596
  25.0 0.9 %collective-permute-start.4 = (bf16[256,128]{1,0:T(8,128)(2,1)S(1)}, bf16[256,128]{1,0:T(8,128)(2,1)S(1)}, u32[]{:S(2)}, u32[]{:S(2)}) collective-permute-start(bf16[256,128]{1,0:T(8,128)(2,1)S(1)} %get-tuple-element.18), channel_id=1, source_target_pairs={{0,4},{4,0},{8,12},{12,8},{1,5},{5,1},{9,13},{13,9},{2,6},{6,2},{1... | collective-permute-start | bytes 196616 | tf_op jit(solution)/shard_map/ppermute | solution.py:110
  25.9 2.5 %collective-permute-start.6 = (bf16[256,128]{1,0:T(8,128)(2,1)S(1)}, bf16[256,128]{1,0:T(8,128)(2,1)S(1)}, u32[]{:S(2)}, u32[]{:S(2)}) collective-permute-start(bf16[256,128]{1,0:T(8,128)(2,1)S(1)} %get-tuple-element.19), channel_id=1, source_target_pairs={{0,12},{4,8},{8,4},{12,0},{1,13},{5,9},{9,5},{13,1},{2,14},{6,10},... | collective-permute-start | bytes 196616 | tf_op jit(solution)/shard_map/ppermute | solution.py:110
  28.4 0.2 collective-permute-start.5
  28.6 0.8 %collective-permute-done.4 = bf16[256,128]{1,0:T(8,128)(2,1)S(1)} collective-permute-done((bf16[256,128]{1,0:T(8,128)(2,1)S(1)}, bf16[256,128]{1,0:T(8,128)(2,1)S(1)}, u32[]{:S(2)}, u32[]{:S(2)}) %collective-permute-start.4) | collective-permute-done | bytes 65568 | tf_op jit(solution)/shard_map/ppermute | solution.py:110
  29.4 3.3 %collective-permute-done.6 = bf16[256,128]{1,0:T(8,128)(2,1)S(1)} collective-permute-done((bf16[256,128]{1,0:T(8,128)(2,1)S(1)}, bf16[256,128]{1,0:T(8,128)(2,1)S(1)}, u32[]{:S(2)}, u32[]{:S(2)}) %collective-permute-start.6) | collective-permute-done | bytes 65568 | tf_op jit(solution)/shard_map/ppermute | solution.py:110
  32.7 2.3 %collective-permute-done.5 = bf16[256,128]{1,0:T(8,128)(2,1)S(1)} collective-permute-done((bf16[256,128]{1,0:T(8,128)(2,1)S(1)}, bf16[256,128]{1,0:T(8,128)(2,1)S(1)}, u32[]{:S(2)}, u32[]{:S(2)}) %collective-permute-start.5) | collective-permute-done | bytes 65568 | tf_op jit(solution)/shard_map/ppermute | solution.py:110
  35.1 1.6 %collective-permute-start.7 = (bf16[256,128]{1,0:T(8,128)(2,1)S(1)}, bf16[256,128]{1,0:T(8,128)(2,1)S(1)}, u32[]{:S(2)}, u32[]{:S(2)}) collective-permute-start(bf16[256,128]{1,0:T(8,128)(2,1)S(1)} %fusion.2), channel_id=1, source_target_pairs={{0,2},{2,0},{1,3},{3,1},{4,6},{6,4},{5,7},{7,5},{8,10},{10,8},{9,1... | collective-permute-start | bytes 196616 | tf_op jit(solution)/shard_map/ppermute | solution.py:610
  36.6 2.8 %collective-permute-done.7 = bf16[256,128]{1,0:T(8,128)(2,1)S(1)} collective-permute-done((bf16[256,128]{1,0:T(8,128)(2,1)S(1)}, bf16[256,128]{1,0:T(8,128)(2,1)S(1)}, u32[]{:S(2)}, u32[]{:S(2)}) %collective-permute-start.7) | collective-permute-done | bytes 65568 | tf_op jit(solution)/shard_map/ppermute | solution.py:610
  39.4 0.1 collective-permute-start.8
  39.5 1.3 %collective-permute-done.8.other = f32[256,128]{1,0:T(8,128)S(1)} collective-permute-done((f32[256,128]{1,0:T(8,128)S(1)}, f32[256,128]{1,0:T(8,128)S(1)}, u32[]{:S(2)}, u32[]{:S(2)}) %collective-permute-start.8) | collective-permute-done | bytes 131104 | tf_op jit(solution)/shard_map/ppermute | solution.py:613
  40.9 0.7 %assemble.1 = (f32[101,512]{1,0:T(8,128)}, f32[101,128]{1,0:T(8,128)}) custom-call(f32[256,128]{1,0:T(8,128)S(1)} %convert_add_fusion.whole, f32[256,128]{1,0:T(8,128)S(1)} %collective-permute-done.8.other), custom_call_target="tpu_custom_call" | custom-call | tf_op jit(solution)/shard_map/assemble/pallas_call | solution.py:551
  (6 shorter events, 0.1 us)
Async XLA Ops:
  1.3 11.1 %copy-start = (bf16[512,512]{1,0:T(8,128)(2,1)S(1)}, bf16[512,512]{1,0:T(8,128)(2,1)}, u32[]{:S(2)}) copy-start(bf16[512,512]{1,0:T(8,128)(2,1)} %constant.47.refs_3_.refs_7_) | copy-start | bytes 1572868
  3.3 9.1 %collective-permute-start = (bf16[4,8704]{1,0:T(4,128)(2,1)}, bf16[4,8704]{1,0:T(4,128)(2,1)S(1)}, u32[]{:S(2)}, u32[]{:S(2)}) collective-permute-start(bf16[4,8704]{1,0:T(4,128)(2,1)} %get-tuple-element.11), channel_id=1, source_target_pairs={{0,4},{4,0},{8,12},{12,8},{1,5},{5,1},{9,13},{13,9},{2,6},{6,2},{1... | collective-permute-start | bytes 208904 | tf_op jit(solution)/shard_map/ppermute | solution.py:110
  6.4 7.8 %collective-permute-start.1 = (bf16[4,8704]{1,0:T(4,128)(2,1)}, bf16[4,8704]{1,0:T(4,128)(2,1)S(1)}, u32[]{:S(2)}, u32[]{:S(2)}) collective-permute-start(bf16[4,8704]{1,0:T(4,128)(2,1)} %get-tuple-element.12), channel_id=1, source_target_pairs={{0,8},{4,12},{8,0},{12,4},{1,9},{5,13},{9,1},{13,5},{2,10},{6,14},... | collective-permute-start | bytes 208904 | tf_op jit(solution)/shard_map/ppermute | solution.py:110
  9.0 6.4 %collective-permute-start.2 = (bf16[4,8704]{1,0:T(4,128)(2,1)}, bf16[4,8704]{1,0:T(4,128)(2,1)S(1)}, u32[]{:S(2)}, u32[]{:S(2)}) collective-permute-start(bf16[4,8704]{1,0:T(4,128)(2,1)} %get-tuple-element.13), channel_id=1, source_target_pairs={{0,12},{4,8},{8,4},{12,0},{1,13},{5,9},{9,5},{13,1},{2,14},{6,10},... | collective-permute-start | bytes 208904 | tf_op jit(solution)/shard_map/ppermute | solution.py:110
  9.1 0.7 %copy-start.4 = (s32[256]{0:T(256)S(1)}, s32[256]{0:T(256)}, u32[]{:S(2)}) copy-start(s32[256]{0:T(256)} %param.11) | copy-start | bytes 3076
  10.1 0.7 %copy-start.3 = (s32[256,20]{0,1:T(8,128)S(1)}, s32[256,20]{0,1:T(8,128)}, u32[]{:S(2)}) copy-start(s32[256,20]{0,1:T(8,128)} %param.12) | copy-start | bytes 61444
  10.1 2.3 %copy-start.2 = (bf16[4,8704]{1,0:T(4,128)(2,1)S(1)}, bf16[4,8704]{1,0:T(4,128)(2,1)}, u32[]{:S(2)}) copy-start(bf16[4,8704]{1,0:T(4,128)(2,1)} %get-tuple-element.10.refs_0_) | copy-start | bytes 208900
  12.3 3.0 %copy-start.1 = (bf16[2,256,512]{2,1,0:T(8,128)(2,1)S(1)}, bf16[2,256,512]{2,1,0:T(8,128)(2,1)}, u32[]{:S(2)}) copy-start(bf16[2,256,512]{2,1,0:T(8,128)(2,1)} %constant.52.refs_8_) | copy-start | bytes 1572868
  23.4 1.6 %collective-permute-start.3 = (bf16[4,256,128]{2,1,0:T(8,128)(2,1)S(1)}, bf16[4,256,128]{2,1,0:T(8,128)(2,1)S(1)}, u32[]{:S(2)}, u32[]{:S(2)}) collective-permute-start(bf16[4,256,128]{2,1,0:T(8,128)(2,1)S(1)} %get-tuple-element.17), channel_id=1, source_target_pairs={{0,1},{1,0},{2,3},{3,2},{4,5},{5,4},{6,7},{7,6},{8,9},{9,8},{10,11... | collective-permute-start | bytes 786440 | tf_op jit(solution)/shard_map/ppermute | solution.py:596
  25.0 4.3 %collective-permute-start.4 = (bf16[256,128]{1,0:T(8,128)(2,1)S(1)}, bf16[256,128]{1,0:T(8,128)(2,1)S(1)}, u32[]{:S(2)}, u32[]{:S(2)}) collective-permute-start(bf16[256,128]{1,0:T(8,128)(2,1)S(1)} %get-tuple-element.18), channel_id=1, source_target_pairs={{0,4},{4,0},{8,12},{12,8},{1,5},{5,1},{9,13},{13,9},{2,6},{6,2},{1... | collective-permute-start | bytes 196616 | tf_op jit(solution)/shard_map/ppermute | solution.py:110
  25.9 6.8 %collective-permute-start.6 = (bf16[256,128]{1,0:T(8,128)(2,1)S(1)}, bf16[256,128]{1,0:T(8,128)(2,1)S(1)}, u32[]{:S(2)}, u32[]{:S(2)}) collective-permute-start(bf16[256,128]{1,0:T(8,128)(2,1)S(1)} %get-tuple-element.19), channel_id=1, source_target_pairs={{0,12},{4,8},{8,4},{12,0},{1,13},{5,9},{9,5},{13,1},{2,14},{6,10},... | collective-permute-start | bytes 196616 | tf_op jit(solution)/shard_map/ppermute | solution.py:110
  28.4 6.7 %collective-permute-start.5 = (bf16[256,128]{1,0:T(8,128)(2,1)S(1)}, bf16[256,128]{1,0:T(8,128)(2,1)S(1)}, u32[]{:S(2)}, u32[]{:S(2)}) collective-permute-start(bf16[256,128]{1,0:T(8,128)(2,1)S(1)} %get-tuple-element.20), channel_id=1, source_target_pairs={{0,8},{4,12},{8,0},{12,4},{1,9},{5,13},{9,1},{13,5},{2,10},{6,14},... | collective-permute-start | bytes 196616 | tf_op jit(solution)/shard_map/ppermute | solution.py:110
  35.1 4.3 %collective-permute-start.7 = (bf16[256,128]{1,0:T(8,128)(2,1)S(1)}, bf16[256,128]{1,0:T(8,128)(2,1)S(1)}, u32[]{:S(2)}, u32[]{:S(2)}) collective-permute-start(bf16[256,128]{1,0:T(8,128)(2,1)S(1)} %fusion.2), channel_id=1, source_target_pairs={{0,2},{2,0},{1,3},{3,1},{4,6},{6,4},{5,7},{7,5},{8,10},{10,8},{9,1... | collective-permute-start | bytes 196616 | tf_op jit(solution)/shard_map/ppermute | solution.py:610
  39.4 1.4 %collective-permute-start.8 = (f32[256,128]{1,0:T(8,128)S(1)}, f32[256,128]{1,0:T(8,128)S(1)}, u32[]{:S(2)}, u32[]{:S(2)}) collective-permute-start(f32[256,128]{1,0:T(8,128)S(1)} %convert_add_fusion.whole), channel_id=1, source_target_pairs={{0,1},{1,0},{2,3},{3,2},{4,5},{5,4},{6,7},{7,6},{8,9},{9,8},{10,11... | collective-permute-start | bytes 393224 | tf_op jit(solution)/shard_map/ppermute | solution.py:613

commit v8 on v7

--- a/solution.py
+++ b/solution.py
@@ -7,6 +7,7 @@
 from jax.experimental import pallas as pl
 from jax.experimental.pallas import tpu as pltpu
 from jax.sharding import PartitionSpec as P
+
 
 COMP = 3
 WIN = 400
@@ -106,8 +107,9 @@
 
 def exchange(blocks, regions):
     if separate(regions):
-        masks = range(regions - 1, 0, -1)
-        moved = {m: lax.ppermute(blocks[m], "region", [(i, i ^ m) for i in range(regions)]) for m in masks}
+        moved = {}
+        for m in range(regions - 1, 0, -1):
+            moved[m] = lax.ppermute(blocks[m], "region", [(i, i ^ m) for i in range(regions)])
         return [blocks[0]] + [moved[m] for m in range(1, regions)]
     order = jnp.arange(regions, dtype=jnp.int32) ^ lax.axis_index("region")
     moved = lax.all_to_all(jnp.take(blocks[0], order, axis=0), "region", split_axis=0, concat_axis=0, tiled=True)
@@ -487,6 +489,7 @@
             one_group(0, 0)
         else:
             lax.fori_loop(0, regions, one_group, 0)
+
         def lag_of(axis):
             row = lax.broadcasted_iota(jnp.int32, (LANES, LANES), axis)
             return jnp.where(row < HALF_ROWS, row + chan * HALF_LAGS, row - HALF_ROWS + (1 - chan) * HALF_LAGS)
@@ -559,7 +562,7 @@
     )(whole, other)
 
 
-def on_device(archive, starts, event_owner, station_mask, pair_first, pair_second, pair_count):
+def locate(archive, starts, event_owner, station_mask, pair_first, pair_second, pair_count):
     regions = lax.axis_size("region")
     chans = lax.axis_size("chan")
     chan_index = lax.axis_index("chan")
@@ -585,7 +588,7 @@
 
     slot_event, weight_rows = describe(mask, station, slot_of, regions, slots, nch)
     table = forward_table()
-    ready = 2 if regions == 4 else 0
+    ready = 1 if separate(regions) else 0
     spectra = []
     if ready:
         spectra = [early_spectra(received[:ready], weight_rows, table, regions, per_block, pair_cap, segment, nch)]
@@ -625,7 +628,7 @@
         P(("groups", "region")),
     )
     return jax.shard_map(
-        on_device,
+        locate,
         mesh=mesh,
         in_specs=placed,
         out_specs=(P(None, ("groups", "region")), P(None, ("groups", "region"))),

time: 41.8 us -> 42.4 us (1.014)
  waiting for transfers between devices: 13.3 us -> 13.8 us
    pallas_call x1, Pallas kernels: 7.98 us -> 8.56 us  [locate(): correlate(regions, per_block, pair_cap, segment, slots, nch, ready)]
    ppermute x6, waiting for transfers between devices: 7.64 us -> 8.16 us  [exchange(): lax.ppermute(blocks[m], 'region', [(i, i ^ m) for i in range(regions)])]
    pallas_call x1, Pallas kernels: 1.82 us -> 1.31 us  [early_spectra(): pl.pallas_call(kernel, out_shape=jax.ShapeDtypeStruct((number * cutter.sp...]
  transfers between devices with their start and end apart: 9 -> 9, of which waited for: 7 -> 8; matrix products, arithmetic and copies ran while one was open for 2% -> 2% of each run, Pallas kernels for 8% -> 7%
where the time goes in v8:
time: 42.4 us; the launch traced here: 42.2 us
  Pallas kernels  14.1 us (33%)
  waiting for transfers between devices  13.8 us (33%)
  starting transfers between devices  11 us (26%)
  between operations  1.42 us (3%)
  local copies, waits for them, and re-layouts  1.32 us (3%)
  other arithmetic  0.61 us (1%)
    ppermute x6, starting transfers between devices, exchange(): lax.ppermute(blocks[m], 'region', [(i, i ^ m) for i in range(regions)])  9.26 us
    pallas_call x1, Pallas kernels, locate(): correlate(regions, per_block, pair_cap, segment, slots, nch, ready)  8.56 us
    ppermute x6, waiting for transfers between devices, exchange(): lax.ppermute(blocks[m], 'region', [(i, i ^ m) for i in range(regions)])  8.16 us
    ppermute x1, waiting for transfers between devices, locate(): other = lax.ppermute(sent, 'stn', [(i, i ^ step) for i in range(count)])  2.77 us
    pallas_call x1, Pallas kernels, pack(): pl.pallas_call(kernel, out_shape=block_shapes(regions, (nch, segment + fi...  1.97 us
    ppermute x1, starting transfers between devices, locate(): other = lax.ppermute(sent, 'stn', [(i, i ^ step) for i in range(count)])  1.56 us
    ppermute x1, waiting for transfers between devices, locate(): swapped = lax.ppermute(given, 'chan', swap)  1.52 us
    pallas_call x1, Pallas kernels, describe(): pl.pallas_call(kernel, out_shape=(jax.ShapeDtypeStruct((regions * slots,...  1.51 us
  transfers between devices with their start and end apart: 9, of which 8 were waited for; matrix products, arithmetic and copies ran while one was open for 2% of the time, Pallas kernels for 7%

profile of v8, /device:TPU:0, one launch (start us, length us, event | category | flops | bytes accessed | tf_op | source)
XLA Modules:
  0.0 42.2 jit_solution(16913256912069844372)
XLA Ops:
  1.3 0.0 copy-start
  1.3 2.0 %pack.1 = (bf16[4,8704]{1,0:T(4,128)(2,1)}, bf16[4,8704]{1,0:T(4,128)(2,1)}, bf16[4,8704]{1,0:T(4,128)(2,1)}, bf16[4,8704]{1,0:T(4,128)(2,1)}) custom-call(bf16[10,3,8192]{2,1,0:T(4,128)(2,1)} %refs_0_.1, s32[1,64]{1,0:T(1,128)} %bitcast.24, s32[20,256]{1,0:T(8,128)} %bitcast.19, s32[1,512]{1,0:T(1,128)} %bitcast.22, s32[1,512]{1,0:T(1,128)} %bitcast.23, ...), custom_call_target="tpu_custom_call" | custom-call | tf_op jit(solution)/shard_map/pack/pallas_call | solution.py:178
  3.3 3.1 %collective-permute-start = (bf16[4,8704]{1,0:T(4,128)(2,1)}, bf16[4,8704]{1,0:T(4,128)(2,1)S(1)}, u32[]{:S(2)}, u32[]{:S(2)}) collective-permute-start(bf16[4,8704]{1,0:T(4,128)(2,1)} %get-tuple-element.11), channel_id=1, source_target_pairs={{0,4},{4,0},{8,12},{12,8},{1,5},{5,1},{9,13},{13,9},{2,6},{6,2},{1... | collective-permute-start | bytes 208904 | tf_op jit(solution)/shard_map/ppermute | solution.py:112
  6.4 2.6 %collective-permute-start.1 = (bf16[4,8704]{1,0:T(4,128)(2,1)}, bf16[4,8704]{1,0:T(4,128)(2,1)S(1)}, u32[]{:S(2)}, u32[]{:S(2)}) collective-permute-start(bf16[4,8704]{1,0:T(4,128)(2,1)} %get-tuple-element.12), channel_id=1, source_target_pairs={{0,8},{4,12},{8,0},{12,4},{1,9},{5,13},{9,1},{13,5},{2,10},{6,14},... | collective-permute-start | bytes 208904 | tf_op jit(solution)/shard_map/ppermute | solution.py:112
  9.0 0.0 collective-permute-start.2
  9.0 0.1 add.74
  9.1 0.0 copy-start.4
  9.1 0.1 add.75
  9.1 0.6 %copy-done.4 = s32[256]{0:T(256)S(1)} copy-done((s32[256]{0:T(256)S(1)}, s32[256]{0:T(256)}, u32[]{:S(2)}) %copy-start.4) | copy-done | bytes 1048
  9.7 0.1 eq.15
  9.8 0.1 fusion.3
  9.9 0.1 reduce_window_sum.11
  10.1 0.0 copy-start.3
  10.1 0.0 copy-start.2
  10.1 0.2 select_reduce_fusion
  10.3 0.1 reduce_sum.12
  10.4 0.4 copy-done.3
  10.8 1.5 %describe.1 = (bf16[512,128]{1,0:T(8,128)(2,1)S(1)}, f32[1024,128]{1,0:T(8,128)S(1)}) custom-call(s32[20,256]{1,0:T(8,128)S(1)} %bitcast.20, s32[4]{0:T(128)S(1)} %and_select_fusion.station, s32[1,256]{1,0:T(1,128)S(1)} %bitcast.21), custom_call_target="tpu_custom_call" | custom-call | tf_op jit(solution)/shard_map/describe/pallas_call | solution.py:222
  12.3 0.0 copy-done
  12.3 0.0 copy-done.2
  12.3 0.0 copy-start.1
  12.3 1.3 %early_spectra.1.refs_4_ = f32[1024,128]{1,0:T(8,128)S(1)} custom-call(bf16[4,8704]{1,0:T(4,128)(2,1)S(1)} %copy-done.2, f32[1024,128]{1,0:T(8,128)S(1)} %get-tuple-element.14.refs_1_.refs_6_, bf16[512,512]{1,0:T(8,128)(2,1)S(1)} %copy-done), custom_call_target="tpu_custom_call" | custom-call | tf_op jit(solution)/shard_map/early_spectra/pallas_call | solution.py:329
  13.7 0.0 collective-permute-done.refs_1_
  13.7 0.4 %collective-permute-done.1.refs_2_ = bf16[4,8704]{1,0:T(4,128)(2,1)S(1)} collective-permute-done((bf16[4,8704]{1,0:T(4,128)(2,1)}, bf16[4,8704]{1,0:T(4,128)(2,1)S(1)}, u32[]{:S(2)}, u32[]{:S(2)}) %collective-permute-start.1) | collective-permute-done | bytes 69664 | tf_op jit(solution)/shard_map/ppermute | solution.py:112
  14.1 1.3 %collective-permute-done.2.refs_3_ = bf16[4,8704]{1,0:T(4,128)(2,1)S(1)} collective-permute-done((bf16[4,8704]{1,0:T(4,128)(2,1)}, bf16[4,8704]{1,0:T(4,128)(2,1)S(1)}, u32[]{:S(2)}, u32[]{:S(2)}) %collective-permute-start.2) | collective-permute-done | bytes 69664 | tf_op jit(solution)/shard_map/ppermute | solution.py:112
  15.4 0.0 copy-done.1
  15.4 8.6 %correlate.1 = (f32[4,256,128]{2,1,0:T(8,128)S(1)}, bf16[4,256,128]{2,1,0:T(8,128)(2,1)S(1)}) custom-call(bf16[4,8704]{1,0:T(4,128)(2,1)S(1)} %copy-done.2, bf16[4,8704]{1,0:T(4,128)(2,1)S(1)} %collective-permute-done.refs_1_, bf16[4,8704]{1,0:T(4,128)(2,1)S(1)} %collective-permute-done.1.refs_2_, bf16[4,8704]{1,0:T(4,128)(2,1)S(1)} %collective-permute-done.2.refs_3_, ...), custom_call_target="tpu_custom_call" | custom-call | tf_op jit(solution)/shard_map/correlate/pallas_call | solution.py:595
  24.0 0.1 collective-permute-start.3
  24.0 1.5 %collective-permute-done.3 = bf16[4,256,128]{2,1,0:T(8,128)(2,1)S(1)} collective-permute-done((bf16[4,256,128]{2,1,0:T(8,128)(2,1)S(1)}, bf16[4,256,128]{2,1,0:T(8,128)(2,1)S(1)}, u32[]{:S(2)}, u32[]{:S(2)}) %collective-permute-start.3) | collective-permute-done | bytes 262176 | tf_op jit(solution)/shard_map/ppermute | solution.py:599
  25.6 0.1 fusion.4
  25.6 0.9 %collective-permute-start.4 = (bf16[256,128]{1,0:T(8,128)(2,1)S(1)}, bf16[256,128]{1,0:T(8,128)(2,1)S(1)}, u32[]{:S(2)}, u32[]{:S(2)}) collective-permute-start(bf16[256,128]{1,0:T(8,128)(2,1)S(1)} %get-tuple-element.18), channel_id=1, source_target_pairs={{0,4},{4,0},{8,12},{12,8},{1,5},{5,1},{9,13},{13,9},{2,6},{6,2},{1... | collective-permute-start | bytes 196616 | tf_op jit(solution)/shard_map/ppermute | solution.py:112
  26.5 2.5 %collective-permute-start.6 = (bf16[256,128]{1,0:T(8,128)(2,1)S(1)}, bf16[256,128]{1,0:T(8,128)(2,1)S(1)}, u32[]{:S(2)}, u32[]{:S(2)}) collective-permute-start(bf16[256,128]{1,0:T(8,128)(2,1)S(1)} %get-tuple-element.19), channel_id=1, source_target_pairs={{0,12},{4,8},{8,4},{12,0},{1,13},{5,9},{9,5},{13,1},{2,14},{6,10},... | collective-permute-start | bytes 196616 | tf_op jit(solution)/shard_map/ppermute | solution.py:112
  28.9 0.2 collective-permute-start.5
  29.2 0.8 %collective-permute-done.4 = bf16[256,128]{1,0:T(8,128)(2,1)S(1)} collective-permute-done((bf16[256,128]{1,0:T(8,128)(2,1)S(1)}, bf16[256,128]{1,0:T(8,128)(2,1)S(1)}, u32[]{:S(2)}, u32[]{:S(2)}) %collective-permute-start.4) | collective-permute-done | bytes 65568 | tf_op jit(solution)/shard_map/ppermute | solution.py:112
  30.0 3.4 %collective-permute-done.6 = bf16[256,128]{1,0:T(8,128)(2,1)S(1)} collective-permute-done((bf16[256,128]{1,0:T(8,128)(2,1)S(1)}, bf16[256,128]{1,0:T(8,128)(2,1)S(1)}, u32[]{:S(2)}, u32[]{:S(2)}) %collective-permute-start.6) | collective-permute-done | bytes 65568 | tf_op jit(solution)/shard_map/ppermute | solution.py:112
  33.3 2.3 %collective-permute-done.5 = bf16[256,128]{1,0:T(8,128)(2,1)S(1)} collective-permute-done((bf16[256,128]{1,0:T(8,128)(2,1)S(1)}, bf16[256,128]{1,0:T(8,128)(2,1)S(1)}, u32[]{:S(2)}, u32[]{:S(2)}) %collective-permute-start.5) | collective-permute-done | bytes 65568 | tf_op jit(solution)/shard_map/ppermute | solution.py:112
  35.7 1.6 %collective-permute-start.7 = (bf16[256,128]{1,0:T(8,128)(2,1)S(1)}, bf16[256,128]{1,0:T(8,128)(2,1)S(1)}, u32[]{:S(2)}, u32[]{:S(2)}) collective-permute-start(bf16[256,128]{1,0:T(8,128)(2,1)S(1)} %fusion.2), channel_id=1, source_target_pairs={{0,2},{2,0},{1,3},{3,1},{4,6},{6,4},{5,7},{7,5},{8,10},{10,8},{9,1... | collective-permute-start | bytes 196616 | tf_op jit(solution)/shard_map/ppermute | solution.py:613
  37.2 2.8 %collective-permute-done.7 = bf16[256,128]{1,0:T(8,128)(2,1)S(1)} collective-permute-done((bf16[256,128]{1,0:T(8,128)(2,1)S(1)}, bf16[256,128]{1,0:T(8,128)(2,1)S(1)}, u32[]{:S(2)}, u32[]{:S(2)}) %collective-permute-start.7) | collective-permute-done | bytes 65568 | tf_op jit(solution)/shard_map/ppermute | solution.py:613
  40.0 0.1 collective-permute-start.8
  40.1 1.3 %collective-permute-done.8.other = f32[256,128]{1,0:T(8,128)S(1)} collective-permute-done((f32[256,128]{1,0:T(8,128)S(1)}, f32[256,128]{1,0:T(8,128)S(1)}, u32[]{:S(2)}, u32[]{:S(2)}) %collective-permute-start.8) | collective-permute-done | bytes 131104 | tf_op jit(solution)/shard_map/ppermute | solution.py:616
  41.4 0.7 %assemble.1 = (f32[101,512]{1,0:T(8,128)}, f32[101,128]{1,0:T(8,128)}) custom-call(f32[256,128]{1,0:T(8,128)S(1)} %convert_add_fusion.whole, f32[256,128]{1,0:T(8,128)S(1)} %collective-permute-done.8.other), custom_call_target="tpu_custom_call" | custom-call | tf_op jit(solution)/shard_map/assemble/pallas_call | solution.py:554
  (5 shorter events, 0.1 us)
Async XLA Ops:
  1.3 11.0 %copy-start = (bf16[512,512]{1,0:T(8,128)(2,1)S(1)}, bf16[512,512]{1,0:T(8,128)(2,1)}, u32[]{:S(2)}) copy-start(bf16[512,512]{1,0:T(8,128)(2,1)} %constant.47.refs_2_.refs_7_) | copy-start | bytes 1572868
  3.3 10.4 %collective-permute-start = (bf16[4,8704]{1,0:T(4,128)(2,1)}, bf16[4,8704]{1,0:T(4,128)(2,1)S(1)}, u32[]{:S(2)}, u32[]{:S(2)}) collective-permute-start(bf16[4,8704]{1,0:T(4,128)(2,1)} %get-tuple-element.11), channel_id=1, source_target_pairs={{0,4},{4,0},{8,12},{12,8},{1,5},{5,1},{9,13},{13,9},{2,6},{6,2},{1... | collective-permute-start | bytes 208904 | tf_op jit(solution)/shard_map/ppermute | solution.py:112
  6.4 7.7 %collective-permute-start.1 = (bf16[4,8704]{1,0:T(4,128)(2,1)}, bf16[4,8704]{1,0:T(4,128)(2,1)S(1)}, u32[]{:S(2)}, u32[]{:S(2)}) collective-permute-start(bf16[4,8704]{1,0:T(4,128)(2,1)} %get-tuple-element.12), channel_id=1, source_target_pairs={{0,8},{4,12},{8,0},{12,4},{1,9},{5,13},{9,1},{13,5},{2,10},{6,14},... | collective-permute-start | bytes 208904 | tf_op jit(solution)/shard_map/ppermute | solution.py:112
  9.0 6.4 %collective-permute-start.2 = (bf16[4,8704]{1,0:T(4,128)(2,1)}, bf16[4,8704]{1,0:T(4,128)(2,1)S(1)}, u32[]{:S(2)}, u32[]{:S(2)}) collective-permute-start(bf16[4,8704]{1,0:T(4,128)(2,1)} %get-tuple-element.13), channel_id=1, source_target_pairs={{0,12},{4,8},{8,4},{12,0},{1,13},{5,9},{9,5},{13,1},{2,14},{6,10},... | collective-permute-start | bytes 208904 | tf_op jit(solution)/shard_map/ppermute | solution.py:112
  9.1 0.7 %copy-start.4 = (s32[256]{0:T(256)S(1)}, s32[256]{0:T(256)}, u32[]{:S(2)}) copy-start(s32[256]{0:T(256)} %param.11) | copy-start | bytes 3076
  10.1 0.7 %copy-start.3 = (s32[256,20]{0,1:T(8,128)S(1)}, s32[256,20]{0,1:T(8,128)}, u32[]{:S(2)}) copy-start(s32[256,20]{0,1:T(8,128)} %param.12) | copy-start | bytes 61444
  10.1 2.3 %copy-start.2 = (bf16[4,8704]{1,0:T(4,128)(2,1)S(1)}, bf16[4,8704]{1,0:T(4,128)(2,1)}, u32[]{:S(2)}) copy-start(bf16[4,8704]{1,0:T(4,128)(2,1)} %get-tuple-element.10.refs_0_) | copy-start | bytes 208900
  12.3 3.1 %copy-start.1 = (bf16[2,256,512]{2,1,0:T(8,128)(2,1)S(1)}, bf16[2,256,512]{2,1,0:T(8,128)(2,1)}, u32[]{:S(2)}) copy-start(bf16[2,256,512]{2,1,0:T(8,128)(2,1)} %constant.52.refs_8_) | copy-start | bytes 1572868
  24.0 1.6 %collective-permute-start.3 = (bf16[4,256,128]{2,1,0:T(8,128)(2,1)S(1)}, bf16[4,256,128]{2,1,0:T(8,128)(2,1)S(1)}, u32[]{:S(2)}, u32[]{:S(2)}) collective-permute-start(bf16[4,256,128]{2,1,0:T(8,128)(2,1)S(1)} %get-tuple-element.17), channel_id=1, source_target_pairs={{0,1},{1,0},{2,3},{3,2},{4,5},{5,4},{6,7},{7,6},{8,9},{9,8},{10,11... | collective-permute-start | bytes 786440 | tf_op jit(solution)/shard_map/ppermute | solution.py:599
  25.6 4.3 %collective-permute-start.4 = (bf16[256,128]{1,0:T(8,128)(2,1)S(1)}, bf16[256,128]{1,0:T(8,128)(2,1)S(1)}, u32[]{:S(2)}, u32[]{:S(2)}) collective-permute-start(bf16[256,128]{1,0:T(8,128)(2,1)S(1)} %get-tuple-element.18), channel_id=1, source_target_pairs={{0,4},{4,0},{8,12},{12,8},{1,5},{5,1},{9,13},{13,9},{2,6},{6,2},{1... | collective-permute-start | bytes 196616 | tf_op jit(solution)/shard_map/ppermute | solution.py:112
  26.5 6.9 %collective-permute-start.6 = (bf16[256,128]{1,0:T(8,128)(2,1)S(1)}, bf16[256,128]{1,0:T(8,128)(2,1)S(1)}, u32[]{:S(2)}, u32[]{:S(2)}) collective-permute-start(bf16[256,128]{1,0:T(8,128)(2,1)S(1)} %get-tuple-element.19), channel_id=1, source_target_pairs={{0,12},{4,8},{8,4},{12,0},{1,13},{5,9},{9,5},{13,1},{2,14},{6,10},... | collective-permute-start | bytes 196616 | tf_op jit(solution)/shard_map/ppermute | solution.py:112
  28.9 6.7 %collective-permute-start.5 = (bf16[256,128]{1,0:T(8,128)(2,1)S(1)}, bf16[256,128]{1,0:T(8,128)(2,1)S(1)}, u32[]{:S(2)}, u32[]{:S(2)}) collective-permute-start(bf16[256,128]{1,0:T(8,128)(2,1)S(1)} %get-tuple-element.20), channel_id=1, source_target_pairs={{0,8},{4,12},{8,0},{12,4},{1,9},{5,13},{9,1},{13,5},{2,10},{6,14},... | collective-permute-start | bytes 196616 | tf_op jit(solution)/shard_map/ppermute | solution.py:112
  35.7 4.3 %collective-permute-start.7 = (bf16[256,128]{1,0:T(8,128)(2,1)S(1)}, bf16[256,128]{1,0:T(8,128)(2,1)S(1)}, u32[]{:S(2)}, u32[]{:S(2)}) collective-permute-start(bf16[256,128]{1,0:T(8,128)(2,1)S(1)} %fusion.2), channel_id=1, source_target_pairs={{0,2},{2,0},{1,3},{3,1},{4,6},{6,4},{5,7},{7,5},{8,10},{10,8},{9,1... | collective-permute-start | bytes 196616 | tf_op jit(solution)/shard_map/ppermute | solution.py:613
  40.0 1.4 %collective-permute-start.8 = (f32[256,128]{1,0:T(8,128)S(1)}, f32[256,128]{1,0:T(8,128)S(1)}, u32[]{:S(2)}, u32[]{:S(2)}) collective-permute-start(f32[256,128]{1,0:T(8,128)S(1)} %convert_add_fusion.whole), channel_id=1, source_target_pairs={{0,1},{1,0},{2,3},{3,2},{4,5},{5,4},{6,7},{7,6},{8,9},{9,8},{10,11... | collective-permute-start | bytes 393224 | tf_op jit(solution)/shard_map/ppermute | solution.py:616

commit v9 on v8

--- a/solution.py
+++ b/solution.py
@@ -53,16 +53,6 @@
     table = jnp.asarray(table, jnp.float32)
     high = table.astype(jnp.bfloat16)
     return jnp.concatenate([high, (table - high.astype(jnp.float32)).astype(jnp.bfloat16)], axis=1)
-
-
-def slot_table(event_owner, regions, per_block, bucket, slots):
-    blocks = event_owner.reshape(regions, per_block)
-    owned = blocks[:, :, None] == jnp.arange(regions, dtype=jnp.int32)[None, None, :]
-    onehot = owned.astype(jnp.int32)
-    before = jnp.cumsum(onehot, axis=1) - onehot
-    ranking = jnp.sum(before * onehot, axis=2)
-    block_index = jnp.arange(regions, dtype=jnp.int32)[:, None]
-    return (blocks * slots + block_index * bucket + ranking).reshape(-1)
 
 
 def as_bf16(flags):
@@ -193,43 +183,6 @@
     )(archive, starts, station_mask, pair_first, pair_second, pair_count)
 
 
-def describe(station_mask, station, slot_of, regions, slots, nch):
-    events = station_mask.shape[1]
-    per_block = events // regions
-
-    def kernel(mask, station, slot_of, slot_event, weight_rows):
-        region = lax.axis_index("region")
-        listed = lax.broadcasted_iota(jnp.int32, (mask.shape[0], LANES), 0)
-        usable = mask[...].astype(jnp.float32).astype(jnp.bfloat16)
-        for c in range(nch):
-            value = lax.dot_general(usable, as_bf16(listed == station[c]), TN, preferred_element_type=jnp.float32)
-            for part in range(regions):
-                row = pl.multiple_of(((part ^ region) * nch + c) * per_block, per_block)
-                weight_rows[pl.ds(row, per_block), :] = value[part * per_block : (part + 1) * per_block]
-        names = digits_of(lax.broadcasted_iota(jnp.int32, (events, LANES), 0) + 1)
-        place = lax.broadcasted_iota(jnp.int32, (slots, events), 0)
-        slot_lane = slot_of[...]
-
-        def one_region(part, carry):
-            hit = as_bf16(place + part * slots == slot_lane)
-            high, low = (jnp.dot(hit, digit, preferred_element_type=jnp.float32) for digit in names)
-            event = high * 128.0 + low - 1.0
-            slot_event[pl.ds(pl.multiple_of(part * slots, slots), slots), :] = event.astype(slot_event.dtype)
-            return carry
-
-        lax.fori_loop(0, regions, one_region, 0)
-
-    return pl.pallas_call(
-        kernel,
-        out_shape=(jax.ShapeDtypeStruct((regions * slots, LANES), jnp.bfloat16 if digit_count(events) == 1 else jnp.float32),
-                   jax.ShapeDtypeStruct((events * nch, LANES), jnp.float32)),
-        in_specs=[VMEM_ONLY, SMEM_ONLY, VMEM_ONLY],
-        out_specs=(VMEM_ONLY, VMEM_ONLY),
-        compiler_params=pltpu.CompilerParams(vmem_limit_bytes=grant(regions * slots + 2 * events * nch)),
-        name="describe",
-    )(station_mask, station, slot_of)
-
-
 def grant(rows):
     return min(rows * LANES * 4 * 5 // 4 + (4 << 20), 60 * 1024 * 1024)
 
@@ -299,48 +252,98 @@
     return 2 * digit_count(events) + 1
 
 
-def early_spectra(blocks, weight_rows, table, regions, per_block, pair_cap, segment, nch):
+def prepare(blocks, station_mask, event_owner, table, regions, chans, stations, per_block, pair_cap, segment, bucket, nch):
     cutter = Cutter(per_block, segment, nch)
     number = len(blocks)
-    k = scalar_field(regions * per_block)
+    events = regions * per_block
+    slots = regions * bucket
+    share = station_share(stations, chans)
+    k = scalar_field(events)
 
     def kernel(*refs):
         sources, refs = refs[:number], refs[number:]
-        weight_rows, table, spec, shifted, windows, index_vmem, index, sem = refs
-        for slot in range(number):
-            lane = segment + k // 4 * pair_cap
-            scalars = sources[slot][:, lane : lane + LANES].astype(jnp.float32)[k % 4 : k % 4 + 1]
-            index_vmem[slot : slot + 1, :per_block] = cutter.words(scalars, slot)
-        copy = pltpu.make_async_copy(index_vmem, index, sem)
-        copy.start()
-        for slot in range(number):
-            cutter.widen(sources[slot], shifted, slot)
-        copy.wait()
-
-        def cut(slot, carry):
-            cutter.cut(lambda event: index[slot, event], shifted, windows, slot)
+        mask, owners, table, slot_event, weight_rows = refs[:5]
+        region = lax.axis_index("region")
+        if number:
+            spec, shifted, windows, index_vmem, index, sem = refs[5:]
+            for slot in range(number):
+                lane = segment + k // 4 * pair_cap
+                scalars = sources[slot][:, lane : lane + LANES].astype(jnp.float32)[k % 4 : k % 4 + 1]
+                index_vmem[slot : slot + 1, :per_block] = cutter.words(scalars, slot)
+            copy = pltpu.make_async_copy(index_vmem, index, sem)
+            copy.start()
+            for slot in range(number):
+                cutter.widen(sources[slot], shifted, slot)
+
+        listed = lax.broadcasted_iota(jnp.int32, (mask.shape[0], LANES), 0)
+        usable = mask[...].astype(jnp.float32).astype(jnp.bfloat16)
+        chan = lax.axis_index("chan")
+        for c in range(nch):
+            channel = region * nch + c
+            local = jnp.minimum(chan * share, stations - share) + channel // COMP
+            used = (channel < share * COMP) & (local >= chan * share)
+            station = jnp.where(used, lax.axis_index("stn") * stations + local, -1)
+            value = lax.dot_general(usable, as_bf16(listed == station), TN, preferred_element_type=jnp.float32)
+            for part in range(regions):
+                row = pl.multiple_of(((part ^ region) * nch + c) * per_block, per_block)
+                weight_rows[pl.ds(row, per_block), :] = value[part * per_block : (part + 1) * per_block]
+
+        owner = owners[...]
+        owner = jnp.concatenate([owner[:, s * per_block : (s + 1) * per_block] for s in range(regions)], axis=0)
+        earlier = as_bf16(lax.broadcasted_iota(jnp.int32, (per_block, per_block), 0)
+                          < lax.broadcasted_iota(jnp.int32, (per_block, per_block), 1))
+        rank = jnp.zeros((regions, per_block), jnp.float32)
+        for r in range(regions):
+            flags = (owner == r).astype(jnp.float32)
+            before = jnp.dot(flags.astype(jnp.bfloat16), earlier, preferred_element_type=jnp.float32)
+            rank += flags * before
+        in_segment = lax.broadcasted_iota(jnp.int32, (regions, per_block), 0) * bucket + rank.astype(jnp.int32)
+        slot_of = owner * slots + in_segment
+        slot_lane = jnp.concatenate([slot_of[s : s + 1] for s in range(regions)], axis=1)
+        names = digits_of(lax.broadcasted_iota(jnp.int32, (events, LANES), 0) + 1)
+        place = lax.broadcasted_iota(jnp.int32, (slots, events), 0)
+
+        def one_region(part, carry):
+            hit = as_bf16(place + part * slots == slot_lane)
+            high, low = (jnp.dot(hit, digit, preferred_element_type=jnp.float32) for digit in names)
+            event = high * 128.0 + low - 1.0
+            slot_event[pl.ds(pl.multiple_of(part * slots, slots), slots), :] = event.astype(slot_event.dtype)
             return carry
 
-        lax.fori_loop(0, number, cut, 0)
-        for slot in range(number):
-            cutter.transform(windows, slot, weight_rows, slot, table, spec, slot * cutter.spec_rows)
-
-    used = number * (cutter.spec_rows + (cutter.tiles + 2 * per_block) * cutter.rows + 2 * segment * nch // LANES)
-    return pl.pallas_call(
-        kernel,
-        out_shape=jax.ShapeDtypeStruct((number * cutter.spec_rows, LANES), jnp.float32),
-        in_specs=[VMEM_ONLY] * (number + 2),
-        out_specs=VMEM_ONLY,
-        scratch_shapes=[
+        if separate(regions):
+            for part in range(regions):
+                one_region(part, 0)
+        else:
+            lax.fori_loop(0, regions, one_region, 0)
+        if number:
+            copy.wait()
+            for slot in range(number):
+                cutter.cut(lambda event, slot=slot: index[slot, event], shifted, windows, slot)
+                cutter.transform(windows, slot, weight_rows, slot, table, spec, slot * cutter.spec_rows)
+
+    shapes = [jax.ShapeDtypeStruct((regions * slots, LANES), jnp.bfloat16 if digit_count(events) == 1 else jnp.float32),
+              jax.ShapeDtypeStruct((events * nch, LANES), jnp.float32)]
+    scratch = []
+    if number:
+        shapes.append(jax.ShapeDtypeStruct((number * cutter.spec_rows, LANES), jnp.float32))
+        scratch = [
             pltpu.VMEM((number * cutter.tiles * cutter.rows, LANES), jnp.float32),
             pltpu.VMEM((number, 2, per_block * cutter.rows, LANES), jnp.float32),
             pltpu.VMEM((8, LANES), jnp.int32),
             pltpu.SMEM((8, LANES), jnp.int32),
             pltpu.SemaphoreType.DMA(()),
-        ],
-        compiler_params=pltpu.CompilerParams(vmem_limit_bytes=grant(used + weight_rows.shape[0] + 2 * NFFT)),
-        name="early_spectra",
-    )(*blocks, weight_rows, table)
+        ]
+    used = number * (cutter.spec_rows + (cutter.tiles + 2 * per_block) * cutter.rows + 2 * segment * nch // LANES)
+    used += regions * slots + 2 * events * nch + 2 * NFFT + (1024 if separate(regions) else 0)
+    return pl.pallas_call(
+        kernel,
+        out_shape=shapes,
+        in_specs=[VMEM_ONLY] * (number + 3),
+        out_specs=[VMEM_ONLY] * len(shapes),
+        scratch_shapes=scratch,
+        compiler_params=pltpu.CompilerParams(vmem_limit_bytes=grant(used)),
+        name="prepare",
+    )(*blocks, station_mask, event_owner, table)
 
 
 def correlate(regions, per_block, pair_cap, segment, slots, nch, ready):
@@ -565,7 +568,6 @@
 def locate(archive, starts, event_owner, station_mask, pair_first, pair_second, pair_count):
     regions = lax.axis_size("region")
     chans = lax.axis_size("chan")
-    chan_index = lax.axis_index("chan")
     per_block = starts.shape[0]
     pair_cap = pair_first.shape[0]
     stations = archive.shape[0]
@@ -580,18 +582,11 @@
                   pair_second.reshape(1, -1), pair_count, regions, chans, nch)
     received = exchange(blocks, regions)
 
-    slot_of = slot_table(event_owner, regions, per_block, bucket, slots).reshape(1, -1)
-    channel = lax.axis_index("region") * nch + jnp.arange(nch, dtype=jnp.int32)
-    local = jnp.minimum(chan_index * share, stations - share) + channel // COMP
-    used = (channel < share * COMP) & (local >= chan_index * share)
-    station = jnp.where(used, lax.axis_index("stn") * stations + local, -1)
-
-    slot_event, weight_rows = describe(mask, station, slot_of, regions, slots, nch)
     table = forward_table()
     ready = 1 if separate(regions) else 0
-    spectra = []
-    if ready:
-        spectra = [early_spectra(received[:ready], weight_rows, table, regions, per_block, pair_cap, segment, nch)]
+    slot_event, weight_rows, *spectra = prepare(
+        received[:ready], mask, event_owner.reshape(1, -1), table, regions, chans, stations, per_block, pair_cap, segment,
+        bucket, nch)
     kept, given = correlate(regions, per_block, pair_cap, segment, slots, nch, ready)(
         *received, *spectra, slot_event, weight_rows, table, lag_table())
 

time: 42.4 us -> 42.5 us (level)
  Pallas kernels: 14.1 us -> 13.1 us
  local copies, waits for them, and re-layouts: 1.32 us -> 2.32 us
  waiting for transfers between devices: 13.8 us -> 14.4 us
  other arithmetic: 0.61 us -> 0.1 us
    unnamed x10 -> x12, local copies, waits for them, and re-layouts: 1 us -> 2.32 us
    pallas_call x2 -> x1, Pallas kernels: 2.82 us -> 1.81 us  [prepare(): pl.pallas_call(kernel, out_shape=shapes, in_specs=[VMEM_ONLY] * (number +...]
    ppermute x6, waiting for transfers between devices: 8.16 us -> 8.73 us  [exchange(): lax.ppermute(blocks[m], 'region', [(i, i ^ m) for i in range(regions)])]
  transfers between devices with their start and end apart: 9 -> 9, of which waited for: 8 -> 8; matrix products, arithmetic and copies ran while one was open for 2% -> 0% of each run, Pallas kernels for 7% -> 4%
where the time goes in v9:
time: 42.5 us; the launch traced here: 42.2 us
  waiting for transfers between devices  14.4 us (34%)
  Pallas kernels  13.1 us (31%)
  starting transfers between devices  11 us (26%)
  local copies, waits for them, and re-layouts  2.32 us (5%)
  between operations  1.42 us (3%)
    ppermute x6, starting transfers between devices, exchange(): lax.ppermute(blocks[m], 'region', [(i, i ^ m) for i in range(regions)])  9.26 us
    ppermute x6, waiting for transfers between devices, exchange(): lax.ppermute(blocks[m], 'region', [(i, i ^ m) for i in range(regions)])  8.73 us
    pallas_call x1, Pallas kernels, locate(): correlate(regions, per_block, pair_cap, segment, slots, nch, ready)  8.57 us
    ppermute x1, waiting for transfers between devices, locate(): other = lax.ppermute(sent, 'stn', [(i, i ^ step) for i in range(count)])  2.78 us
    unnamed x12, local copies, waits for them, and re-layouts  2.32 us
    pallas_call x1, Pallas kernels, pack(): pl.pallas_call(kernel, out_shape=block_shapes(regions, (nch, segment + fi...  1.97 us
    pallas_call x1, Pallas kernels, prepare(): pl.pallas_call(kernel, out_shape=shapes, in_specs=[VMEM_ONLY] * (number +...  1.81 us
    ppermute x1, starting transfers between devices, locate(): other = lax.ppermute(sent, 'stn', [(i, i ^ step) for i in range(count)])  1.55 us
  transfers between devices with their start and end apart: 9, of which 8 were waited for; matrix products, arithmetic and copies ran while one was open for 0% of the time, Pallas kernels for 4%

profile of v9, /device:TPU:0, one launch (start us, length us, event | category | flops | bytes accessed | tf_op | source)
XLA Modules:
  0.0 42.2 jit_solution(7865413370107932829)
XLA Ops:
  0.6 0.0 copy-start
  1.3 0.0 copy-start.1
  1.4 2.0 %pack.1 = (bf16[4,8704]{1,0:T(4,128)(2,1)}, bf16[4,8704]{1,0:T(4,128)(2,1)}, bf16[4,8704]{1,0:T(4,128)(2,1)}, bf16[4,8704]{1,0:T(4,128)(2,1)}) custom-call(bf16[10,3,8192]{2,1,0:T(4,128)(2,1)} %refs_0_.1, s32[1,64]{1,0:T(1,128)} %bitcast.24, s32[20,256]{1,0:T(8,128)} %bitcast.19, s32[1,512]{1,0:T(1,128)} %bitcast.22, s32[1,512]{1,0:T(1,128)} %bitcast.23, ...), custom_call_target="tpu_custom_call" | custom-call | tf_op jit(solution)/shard_map/pack/pallas_call | solution.py:168
  3.3 3.1 %collective-permute-start = (bf16[4,8704]{1,0:T(4,128)(2,1)}, bf16[4,8704]{1,0:T(4,128)(2,1)S(1)}, u32[]{:S(2)}, u32[]{:S(2)}) collective-permute-start(bf16[4,8704]{1,0:T(4,128)(2,1)} %get-tuple-element.12), channel_id=1, source_target_pairs={{0,4},{4,0},{8,12},{12,8},{1,5},{5,1},{9,13},{13,9},{2,6},{6,2},{1... | collective-permute-start | bytes 208904 | tf_op jit(solution)/shard_map/ppermute | solution.py:102
  6.5 2.6 %collective-permute-start.1 = (bf16[4,8704]{1,0:T(4,128)(2,1)}, bf16[4,8704]{1,0:T(4,128)(2,1)S(1)}, u32[]{:S(2)}, u32[]{:S(2)}) collective-permute-start(bf16[4,8704]{1,0:T(4,128)(2,1)} %get-tuple-element.13), channel_id=1, source_target_pairs={{0,8},{4,12},{8,0},{12,4},{1,9},{5,13},{9,1},{13,5},{2,10},{6,14},... | collective-permute-start | bytes 208904 | tf_op jit(solution)/shard_map/ppermute | solution.py:102
  9.0 0.0 collective-permute-start.2
  9.0 0.0 copy-done
  9.0 0.0 copy-start.2
  9.0 0.9 %copy-done.2 = bf16[4,8704]{1,0:T(4,128)(2,1)S(1)} copy-done((bf16[4,8704]{1,0:T(4,128)(2,1)S(1)}, bf16[4,8704]{1,0:T(4,128)(2,1)}, u32[]{:S(2)}) %copy-start.2) | copy-done | bytes 69656
  9.9 0.0 copy-start.4
  9.9 0.7 %copy-done.4 = s32[256,20]{0,1:T(8,128)S(1)} copy-done((s32[256,20]{0,1:T(8,128)S(1)}, s32[256,20]{0,1:T(8,128)}, u32[]{:S(2)}) %copy-start.4) | copy-done | bytes 20504
  10.7 0.0 copy-start.5
  10.7 0.7 %copy-done.5 = s32[256]{0:T(256)S(1)} copy-done((s32[256]{0:T(256)S(1)}, s32[256]{0:T(256)}, u32[]{:S(2)}) %copy-start.5) | copy-done | bytes 1048
  11.3 0.0 copy-start.3
  11.4 1.8 %prepare.1 = (bf16[512,128]{1,0:T(8,128)(2,1)S(1)}, f32[1024,128]{1,0:T(8,128)S(1)}, f32[1024,128]{1,0:T(8,128)S(1)}) custom-call(bf16[4,8704]{1,0:T(4,128)(2,1)S(1)} %copy-done.2, s32[20,256]{1,0:T(8,128)S(1)} %bitcast.20, s32[1,256]{1,0:T(1,128)S(1)} %bitcast.21, bf16[512,512]{1,0:T(8,128)(2,1)S(1)} %copy-done), custom_call_target="tpu_custom_call" | custom-call | tf_op jit(solution)/shard_map/prepare/pallas_call | solution.py:338
  13.2 0.0 collective-permute-done.refs_1_
  13.2 1.0 %collective-permute-done.1.refs_2_ = bf16[4,8704]{1,0:T(4,128)(2,1)S(1)} collective-permute-done((bf16[4,8704]{1,0:T(4,128)(2,1)}, bf16[4,8704]{1,0:T(4,128)(2,1)S(1)}, u32[]{:S(2)}, u32[]{:S(2)}) %collective-permute-start.1) | collective-permute-done | bytes 69664 | tf_op jit(solution)/shard_map/ppermute | solution.py:102
  14.2 1.3 %collective-permute-done.2.refs_3_ = bf16[4,8704]{1,0:T(4,128)(2,1)S(1)} collective-permute-done((bf16[4,8704]{1,0:T(4,128)(2,1)}, bf16[4,8704]{1,0:T(4,128)(2,1)S(1)}, u32[]{:S(2)}, u32[]{:S(2)}) %collective-permute-start.2) | collective-permute-done | bytes 69664 | tf_op jit(solution)/shard_map/ppermute | solution.py:102
  15.5 0.0 copy-done.1
  15.5 0.0 copy-done.3
  15.5 8.6 %correlate.1 = (f32[4,256,128]{2,1,0:T(8,128)S(1)}, bf16[4,256,128]{2,1,0:T(8,128)(2,1)S(1)}) custom-call(bf16[4,8704]{1,0:T(4,128)(2,1)S(1)} %copy-done.3, bf16[4,8704]{1,0:T(4,128)(2,1)S(1)} %collective-permute-done.refs_1_, bf16[4,8704]{1,0:T(4,128)(2,1)S(1)} %collective-permute-done.1.refs_2_, bf16[4,8704]{1,0:T(4,128)(2,1)S(1)} %collective-permute-done.2.refs_3_, ...), custom_call_target="tpu_custom_call" | custom-call | tf_op jit(solution)/shard_map/correlate/pallas_call | solution.py:590
  24.0 0.1 collective-permute-start.3
  24.1 1.5 %collective-permute-done.3 = bf16[4,256,128]{2,1,0:T(8,128)(2,1)S(1)} collective-permute-done((bf16[4,256,128]{2,1,0:T(8,128)(2,1)S(1)}, bf16[4,256,128]{2,1,0:T(8,128)(2,1)S(1)}, u32[]{:S(2)}, u32[]{:S(2)}) %collective-permute-start.3) | collective-permute-done | bytes 262176 | tf_op jit(solution)/shard_map/ppermute | solution.py:594
  25.7 0.9 %collective-permute-start.4 = (bf16[256,128]{1,0:T(8,128)(2,1)S(1)}, bf16[256,128]{1,0:T(8,128)(2,1)S(1)}, u32[]{:S(2)}, u32[]{:S(2)}) collective-permute-start(bf16[256,128]{1,0:T(8,128)(2,1)S(1)} %get-tuple-element.20), channel_id=1, source_target_pairs={{0,4},{4,0},{8,12},{12,8},{1,5},{5,1},{9,13},{13,9},{2,6},{6,2},{1... | collective-permute-start | bytes 196616 | tf_op jit(solution)/shard_map/ppermute | solution.py:102
  26.5 2.5 %collective-permute-start.6 = (bf16[256,128]{1,0:T(8,128)(2,1)S(1)}, bf16[256,128]{1,0:T(8,128)(2,1)S(1)}, u32[]{:S(2)}, u32[]{:S(2)}) collective-permute-start(bf16[256,128]{1,0:T(8,128)(2,1)S(1)} %get-tuple-element.21), channel_id=1, source_target_pairs={{0,12},{4,8},{8,4},{12,0},{1,13},{5,9},{9,5},{13,1},{2,14},{6,10},... | collective-permute-start | bytes 196616 | tf_op jit(solution)/shard_map/ppermute | solution.py:102
  29.0 0.2 collective-permute-start.5
  29.2 0.8 %collective-permute-done.4 = bf16[256,128]{1,0:T(8,128)(2,1)S(1)} collective-permute-done((bf16[256,128]{1,0:T(8,128)(2,1)S(1)}, bf16[256,128]{1,0:T(8,128)(2,1)S(1)}, u32[]{:S(2)}, u32[]{:S(2)}) %collective-permute-start.4) | collective-permute-done | bytes 65568 | tf_op jit(solution)/shard_map/ppermute | solution.py:102
  30.0 3.4 %collective-permute-done.6 = bf16[256,128]{1,0:T(8,128)(2,1)S(1)} collective-permute-done((bf16[256,128]{1,0:T(8,128)(2,1)S(1)}, bf16[256,128]{1,0:T(8,128)(2,1)S(1)}, u32[]{:S(2)}, u32[]{:S(2)}) %collective-permute-start.6) | collective-permute-done | bytes 65568 | tf_op jit(solution)/shard_map/ppermute | solution.py:102
  33.4 2.3 %collective-permute-done.5 = bf16[256,128]{1,0:T(8,128)(2,1)S(1)} collective-permute-done((bf16[256,128]{1,0:T(8,128)(2,1)S(1)}, bf16[256,128]{1,0:T(8,128)(2,1)S(1)}, u32[]{:S(2)}, u32[]{:S(2)}) %collective-permute-start.5) | collective-permute-done | bytes 65568 | tf_op jit(solution)/shard_map/ppermute | solution.py:102
  35.7 1.6 %collective-permute-start.7 = (bf16[256,128]{1,0:T(8,128)(2,1)S(1)}, bf16[256,128]{1,0:T(8,128)(2,1)S(1)}, u32[]{:S(2)}, u32[]{:S(2)}) collective-permute-start(bf16[256,128]{1,0:T(8,128)(2,1)S(1)} %fusion.2), channel_id=1, source_target_pairs={{0,2},{2,0},{1,3},{3,1},{4,6},{6,4},{5,7},{7,5},{8,10},{10,8},{9,1... | collective-permute-start | bytes 196616 | tf_op jit(solution)/shard_map/ppermute | solution.py:608
  37.3 2.8 %collective-permute-done.7 = bf16[256,128]{1,0:T(8,128)(2,1)S(1)} collective-permute-done((bf16[256,128]{1,0:T(8,128)(2,1)S(1)}, bf16[256,128]{1,0:T(8,128)(2,1)S(1)}, u32[]{:S(2)}, u32[]{:S(2)}) %collective-permute-start.7) | collective-permute-done | bytes 65568 | tf_op jit(solution)/shard_map/ppermute | solution.py:608
  40.1 0.1 collective-permute-start.8
  40.2 1.3 %collective-permute-done.8.other = f32[256,128]{1,0:T(8,128)S(1)} collective-permute-done((f32[256,128]{1,0:T(8,128)S(1)}, f32[256,128]{1,0:T(8,128)S(1)}, u32[]{:S(2)}, u32[]{:S(2)}) %collective-permute-start.8) | collective-permute-done | bytes 131104 | tf_op jit(solution)/shard_map/ppermute | solution.py:611
  41.5 0.7 %assemble.1 = (f32[101,512]{1,0:T(8,128)}, f32[101,128]{1,0:T(8,128)}) custom-call(f32[256,128]{1,0:T(8,128)S(1)} %convert_add_fusion.whole, f32[256,128]{1,0:T(8,128)S(1)} %collective-permute-done.8.other), custom_call_target="tpu_custom_call" | custom-call | tf_op jit(solution)/shard_map/assemble/pallas_call | solution.py:557
  (3 shorter events, 0.1 us)
Async XLA Ops:
  0.6 8.4 %copy-start = (bf16[512,512]{1,0:T(8,128)(2,1)S(1)}, bf16[512,512]{1,0:T(8,128)(2,1)}, u32[]{:S(2)}) copy-start(bf16[512,512]{1,0:T(8,128)(2,1)} %constant.7.refs_3_.refs_7_) | copy-start | bytes 1572868
  1.3 14.1 %copy-start.1 = (bf16[2,256,512]{2,1,0:T(8,128)(2,1)S(1)}, bf16[2,256,512]{2,1,0:T(8,128)(2,1)}, u32[]{:S(2)}) copy-start(bf16[2,256,512]{2,1,0:T(8,128)(2,1)} %constant.12.refs_8_) | copy-start | bytes 1572868
  3.3 9.8 %collective-permute-start = (bf16[4,8704]{1,0:T(4,128)(2,1)}, bf16[4,8704]{1,0:T(4,128)(2,1)S(1)}, u32[]{:S(2)}, u32[]{:S(2)}) collective-permute-start(bf16[4,8704]{1,0:T(4,128)(2,1)} %get-tuple-element.12), channel_id=1, source_target_pairs={{0,4},{4,0},{8,12},{12,8},{1,5},{5,1},{9,13},{13,9},{2,6},{6,2},{1... | collective-permute-start | bytes 208904 | tf_op jit(solution)/shard_map/ppermute | solution.py:102
  6.5 7.7 %collective-permute-start.1 = (bf16[4,8704]{1,0:T(4,128)(2,1)}, bf16[4,8704]{1,0:T(4,128)(2,1)S(1)}, u32[]{:S(2)}, u32[]{:S(2)}) collective-permute-start(bf16[4,8704]{1,0:T(4,128)(2,1)} %get-tuple-element.13), channel_id=1, source_target_pairs={{0,8},{4,12},{8,0},{12,4},{1,9},{5,13},{9,1},{13,5},{2,10},{6,14},... | collective-permute-start | bytes 208904 | tf_op jit(solution)/shard_map/ppermute | solution.py:102
  9.0 6.4 %collective-permute-start.2 = (bf16[4,8704]{1,0:T(4,128)(2,1)}, bf16[4,8704]{1,0:T(4,128)(2,1)S(1)}, u32[]{:S(2)}, u32[]{:S(2)}) collective-permute-start(bf16[4,8704]{1,0:T(4,128)(2,1)} %get-tuple-element.14), channel_id=1, source_target_pairs={{0,12},{4,8},{8,4},{12,0},{1,13},{5,9},{9,5},{13,1},{2,14},{6,10},... | collective-permute-start | bytes 208904 | tf_op jit(solution)/shard_map/ppermute | solution.py:102
  9.0 0.9 %copy-start.2 = (bf16[4,8704]{1,0:T(4,128)(2,1)S(1)}, bf16[4,8704]{1,0:T(4,128)(2,1)}, u32[]{:S(2)}) copy-start(bf16[4,8704]{1,0:T(4,128)(2,1)} %get-tuple-element.11.refs_0_) | copy-start | bytes 208900
  9.9 0.7 %copy-start.4 = (s32[256,20]{0,1:T(8,128)S(1)}, s32[256,20]{0,1:T(8,128)}, u32[]{:S(2)}) copy-start(s32[256,20]{0,1:T(8,128)} %param.12) | copy-start | bytes 61444
  10.7 0.7 %copy-start.5 = (s32[256]{0:T(256)S(1)}, s32[256]{0:T(256)}, u32[]{:S(2)}) copy-start(s32[256]{0:T(256)} %param.11) | copy-start | bytes 3076
  11.3 4.1 %copy-start.3 = (bf16[4,8704]{1,0:T(4,128)(2,1)S(1)}, bf16[4,8704]{1,0:T(4,128)(2,1)}, u32[]{:S(2)}) copy-start(bf16[4,8704]{1,0:T(4,128)(2,1)} %get-tuple-element.11.refs_0_) | copy-start | bytes 208900
  24.0 1.6 %collective-permute-start.3 = (bf16[4,256,128]{2,1,0:T(8,128)(2,1)S(1)}, bf16[4,256,128]{2,1,0:T(8,128)(2,1)S(1)}, u32[]{:S(2)}, u32[]{:S(2)}) collective-permute-start(bf16[4,256,128]{2,1,0:T(8,128)(2,1)S(1)} %get-tuple-element.19), channel_id=1, source_target_pairs={{0,1},{1,0},{2,3},{3,2},{4,5},{5,4},{6,7},{7,6},{8,9},{9,8},{10,11... | collective-permute-start | bytes 786440 | tf_op jit(solution)/shard_map/ppermute | solution.py:594
  25.7 4.3 %collective-permute-start.4 = (bf16[256,128]{1,0:T(8,128)(2,1)S(1)}, bf16[256,128]{1,0:T(8,128)(2,1)S(1)}, u32[]{:S(2)}, u32[]{:S(2)}) collective-permute-start(bf16[256,128]{1,0:T(8,128)(2,1)S(1)} %get-tuple-element.20), channel_id=1, source_target_pairs={{0,4},{4,0},{8,12},{12,8},{1,5},{5,1},{9,13},{13,9},{2,6},{6,2},{1... | collective-permute-start | bytes 196616 | tf_op jit(solution)/shard_map/ppermute | solution.py:102
  26.5 6.9 %collective-permute-start.6 = (bf16[256,128]{1,0:T(8,128)(2,1)S(1)}, bf16[256,128]{1,0:T(8,128)(2,1)S(1)}, u32[]{:S(2)}, u32[]{:S(2)}) collective-permute-start(bf16[256,128]{1,0:T(8,128)(2,1)S(1)} %get-tuple-element.21), channel_id=1, source_target_pairs={{0,12},{4,8},{8,4},{12,0},{1,13},{5,9},{9,5},{13,1},{2,14},{6,10},... | collective-permute-start | bytes 196616 | tf_op jit(solution)/shard_map/ppermute | solution.py:102
  29.0 6.7 %collective-permute-start.5 = (bf16[256,128]{1,0:T(8,128)(2,1)S(1)}, bf16[256,128]{1,0:T(8,128)(2,1)S(1)}, u32[]{:S(2)}, u32[]{:S(2)}) collective-permute-start(bf16[256,128]{1,0:T(8,128)(2,1)S(1)} %get-tuple-element.22), channel_id=1, source_target_pairs={{0,8},{4,12},{8,0},{12,4},{1,9},{5,13},{9,1},{13,5},{2,10},{6,14},... | collective-permute-start | bytes 196616 | tf_op jit(solution)/shard_map/ppermute | solution.py:102
  35.7 4.3 %collective-permute-start.7 = (bf16[256,128]{1,0:T(8,128)(2,1)S(1)}, bf16[256,128]{1,0:T(8,128)(2,1)S(1)}, u32[]{:S(2)}, u32[]{:S(2)}) collective-permute-start(bf16[256,128]{1,0:T(8,128)(2,1)S(1)} %fusion.2), channel_id=1, source_target_pairs={{0,2},{2,0},{1,3},{3,1},{4,6},{6,4},{5,7},{7,5},{8,10},{10,8},{9,1... | collective-permute-start | bytes 196616 | tf_op jit(solution)/shard_map/ppermute | solution.py:608
  40.1 1.4 %collective-permute-start.8 = (f32[256,128]{1,0:T(8,128)S(1)}, f32[256,128]{1,0:T(8,128)S(1)}, u32[]{:S(2)}, u32[]{:S(2)}) collective-permute-start(f32[256,128]{1,0:T(8,128)S(1)} %convert_add_fusion.whole), channel_id=1, source_target_pairs={{0,1},{1,0},{2,3},{3,2},{4,5},{5,4},{6,7},{7,6},{8,9},{9,8},{10,11... | collective-permute-start | bytes 393224 | tf_op jit(solution)/shard_map/ppermute | solution.py:611

commit v10 on v9

--- a/solution.py
+++ b/solution.py
@@ -204,12 +204,18 @@
         first = slot * (self.tiles * rows)
         if not isinstance(slot, int):
             first = pl.multiple_of(first, rows)
-        for k in range(self.tiles + 2):
-            data = source[:, k * LANES : (k + 1) * LANES].astype(jnp.float32)
-            if k < self.tiles:
-                shifted[pl.ds(first + k * rows, nch, stride=2), :] = data
-            if k >= 2:
-                shifted[pl.ds(first + (k - 2) * rows + 1, nch, stride=2), :] = data
+        group = self.tiles // 2 if self.tiles % 2 == 0 else self.tiles
+
+        def some_tiles(step, carry):
+            for k in range(group):
+                tile = step * group + k
+                row = pl.multiple_of(first + tile * rows, rows)
+                for ahead in range(2):
+                    lane = pl.multiple_of((tile + 2 * ahead) * LANES, LANES)
+                    shifted[pl.ds(row + ahead, nch, stride=2), :] = source[:, pl.ds(lane, LANES)].astype(jnp.float32)
+            return carry
+
+        lax.fori_loop(0, self.tiles // group, some_tiles, 0)
 
     def cut(self, word_of, shifted, windows, slot):
         rows = self.rows

time: 42.5 us -> 42.4 us (level)
  Pallas kernels: 13.1 us -> 12.5 us
  transfers between devices with their start and end apart: 9 -> 9, of which waited for: 8 -> 8; matrix products, arithmetic and copies ran while one was open for 0% -> 0% of each run, Pallas kernels for 4% -> 3%
where the time goes in v10:
time: 42.4 us; the launch traced here: 42.1 us
  waiting for transfers between devices  14.8 us (35%)
  Pallas kernels  12.5 us (29%)
  starting transfers between devices  11 us (26%)
  local copies, waits for them, and re-layouts  2.32 us (5%)
  between operations  1.42 us (3%)
    ppermute x6, starting transfers between devices, exchange(): lax.ppermute(blocks[m], 'region', [(i, i ^ m) for i in range(regions)])  9.26 us
    ppermute x6, waiting for transfers between devices, exchange(): lax.ppermute(blocks[m], 'region', [(i, i ^ m) for i in range(regions)])  9.15 us
    pallas_call x1, Pallas kernels, locate(): correlate(regions, per_block, pair_cap, segment, slots, nch, ready)  8.46 us
    ppermute x1, waiting for transfers between devices, locate(): other = lax.ppermute(sent, 'stn', [(i, i ^ step) for i in range(count)])  2.78 us
    unnamed x12, local copies, waits for them, and re-layouts  2.32 us
    pallas_call x1, Pallas kernels, pack(): pl.pallas_call(kernel, out_shape=block_shapes(regions, (nch, segment + fi...  1.97 us
    ppermute x1, starting transfers between devices, locate(): other = lax.ppermute(sent, 'stn', [(i, i ^ step) for i in range(count)])  1.55 us
    ppermute x1, waiting for transfers between devices, locate(): swapped = lax.ppermute(given, 'chan', swap)  1.52 us
  transfers between devices with their start and end apart: 9, of which 8 were waited for; matrix products, arithmetic and copies ran while one was open for 0% of the time, Pallas kernels for 3%

profile of v10, /device:TPU:0, one launch (start us, length us, event | category | flops | bytes accessed | tf_op | source)
XLA Modules:
  0.0 42.1 jit_solution(11779956617542312709)
XLA Ops:
  0.6 0.0 copy-start
  1.3 0.0 copy-start.1
  1.4 2.0 %pack.1 = (bf16[4,8704]{1,0:T(4,128)(2,1)}, bf16[4,8704]{1,0:T(4,128)(2,1)}, bf16[4,8704]{1,0:T(4,128)(2,1)}, bf16[4,8704]{1,0:T(4,128)(2,1)}) custom-call(bf16[10,3,8192]{2,1,0:T(4,128)(2,1)} %refs_0_.1, s32[1,64]{1,0:T(1,128)} %bitcast.24, s32[20,256]{1,0:T(8,128)} %bitcast.19, s32[1,512]{1,0:T(1,128)} %bitcast.22, s32[1,512]{1,0:T(1,128)} %bitcast.23, ...), custom_call_target="tpu_custom_call" | custom-call | tf_op jit(solution)/shard_map/pack/pallas_call | solution.py:168
  3.3 3.1 %collective-permute-start = (bf16[4,8704]{1,0:T(4,128)(2,1)}, bf16[4,8704]{1,0:T(4,128)(2,1)S(1)}, u32[]{:S(2)}, u32[]{:S(2)}) collective-permute-start(bf16[4,8704]{1,0:T(4,128)(2,1)} %get-tuple-element.12), channel_id=1, source_target_pairs={{0,4},{4,0},{8,12},{12,8},{1,5},{5,1},{9,13},{13,9},{2,6},{6,2},{1... | collective-permute-start | bytes 208904 | tf_op jit(solution)/shard_map/ppermute | solution.py:102
  6.5 2.6 %collective-permute-start.1 = (bf16[4,8704]{1,0:T(4,128)(2,1)}, bf16[4,8704]{1,0:T(4,128)(2,1)S(1)}, u32[]{:S(2)}, u32[]{:S(2)}) collective-permute-start(bf16[4,8704]{1,0:T(4,128)(2,1)} %get-tuple-element.13), channel_id=1, source_target_pairs={{0,8},{4,12},{8,0},{12,4},{1,9},{5,13},{9,1},{13,5},{2,10},{6,14},... | collective-permute-start | bytes 208904 | tf_op jit(solution)/shard_map/ppermute | solution.py:102
  9.0 0.0 collective-permute-start.2
  9.0 0.0 copy-done
  9.0 0.0 copy-start.2
  9.0 0.9 %copy-done.2 = bf16[4,8704]{1,0:T(4,128)(2,1)S(1)} copy-done((bf16[4,8704]{1,0:T(4,128)(2,1)S(1)}, bf16[4,8704]{1,0:T(4,128)(2,1)}, u32[]{:S(2)}) %copy-start.2) | copy-done | bytes 69656
  9.9 0.0 copy-start.4
  9.9 0.7 %copy-done.4 = s32[256,20]{0,1:T(8,128)S(1)} copy-done((s32[256,20]{0,1:T(8,128)S(1)}, s32[256,20]{0,1:T(8,128)}, u32[]{:S(2)}) %copy-start.4) | copy-done | bytes 20504
  10.7 0.0 copy-start.5
  10.7 0.7 %copy-done.5 = s32[256]{0:T(256)S(1)} copy-done((s32[256]{0:T(256)S(1)}, s32[256]{0:T(256)}, u32[]{:S(2)}) %copy-start.5) | copy-done | bytes 1048
  11.3 0.0 copy-start.3
  11.4 1.4 %prepare.1 = (bf16[512,128]{1,0:T(8,128)(2,1)S(1)}, f32[1024,128]{1,0:T(8,128)S(1)}, f32[1024,128]{1,0:T(8,128)S(1)}) custom-call(bf16[4,8704]{1,0:T(4,128)(2,1)S(1)} %copy-done.2, s32[20,256]{1,0:T(8,128)S(1)} %bitcast.20, s32[1,256]{1,0:T(1,128)S(1)} %bitcast.21, bf16[512,512]{1,0:T(8,128)(2,1)S(1)} %copy-done), custom_call_target="tpu_custom_call" | custom-call | tf_op jit(solution)/shard_map/prepare/pallas_call | solution.py:344
  12.8 0.0 collective-permute-done.refs_1_
  12.8 1.4 %collective-permute-done.1.refs_2_ = bf16[4,8704]{1,0:T(4,128)(2,1)S(1)} collective-permute-done((bf16[4,8704]{1,0:T(4,128)(2,1)}, bf16[4,8704]{1,0:T(4,128)(2,1)S(1)}, u32[]{:S(2)}, u32[]{:S(2)}) %collective-permute-start.1) | collective-permute-done | bytes 69664 | tf_op jit(solution)/shard_map/ppermute | solution.py:102
  14.2 1.3 %collective-permute-done.2.refs_3_ = bf16[4,8704]{1,0:T(4,128)(2,1)S(1)} collective-permute-done((bf16[4,8704]{1,0:T(4,128)(2,1)}, bf16[4,8704]{1,0:T(4,128)(2,1)S(1)}, u32[]{:S(2)}, u32[]{:S(2)}) %collective-permute-start.2) | collective-permute-done | bytes 69664 | tf_op jit(solution)/shard_map/ppermute | solution.py:102
  15.5 0.0 copy-done.1
  15.5 0.0 copy-done.3
  15.5 8.5 %correlate.1 = (f32[4,256,128]{2,1,0:T(8,128)S(1)}, bf16[4,256,128]{2,1,0:T(8,128)(2,1)S(1)}) custom-call(bf16[4,8704]{1,0:T(4,128)(2,1)S(1)} %copy-done.3, bf16[4,8704]{1,0:T(4,128)(2,1)S(1)} %collective-permute-done.refs_1_, bf16[4,8704]{1,0:T(4,128)(2,1)S(1)} %collective-permute-done.1.refs_2_, bf16[4,8704]{1,0:T(4,128)(2,1)S(1)} %collective-permute-done.2.refs_3_, ...), custom_call_target="tpu_custom_call" | custom-call | tf_op jit(solution)/shard_map/correlate/pallas_call | solution.py:596
  23.9 0.1 collective-permute-start.3
  24.0 1.5 %collective-permute-done.3 = bf16[4,256,128]{2,1,0:T(8,128)(2,1)S(1)} collective-permute-done((bf16[4,256,128]{2,1,0:T(8,128)(2,1)S(1)}, bf16[4,256,128]{2,1,0:T(8,128)(2,1)S(1)}, u32[]{:S(2)}, u32[]{:S(2)}) %collective-permute-start.3) | collective-permute-done | bytes 262176 | tf_op jit(solution)/shard_map/ppermute | solution.py:600
  25.6 0.9 %collective-permute-start.4 = (bf16[256,128]{1,0:T(8,128)(2,1)S(1)}, bf16[256,128]{1,0:T(8,128)(2,1)S(1)}, u32[]{:S(2)}, u32[]{:S(2)}) collective-permute-start(bf16[256,128]{1,0:T(8,128)(2,1)S(1)} %get-tuple-element.20), channel_id=1, source_target_pairs={{0,4},{4,0},{8,12},{12,8},{1,5},{5,1},{9,13},{13,9},{2,6},{6,2},{1... | collective-permute-start | bytes 196616 | tf_op jit(solution)/shard_map/ppermute | solution.py:102
  26.4 2.5 %collective-permute-start.6 = (bf16[256,128]{1,0:T(8,128)(2,1)S(1)}, bf16[256,128]{1,0:T(8,128)(2,1)S(1)}, u32[]{:S(2)}, u32[]{:S(2)}) collective-permute-start(bf16[256,128]{1,0:T(8,128)(2,1)S(1)} %get-tuple-element.21), channel_id=1, source_target_pairs={{0,12},{4,8},{8,4},{12,0},{1,13},{5,9},{9,5},{13,1},{2,14},{6,10},... | collective-permute-start | bytes 196616 | tf_op jit(solution)/shard_map/ppermute | solution.py:102
  28.9 0.2 collective-permute-start.5
  29.1 0.8 %collective-permute-done.4 = bf16[256,128]{1,0:T(8,128)(2,1)S(1)} collective-permute-done((bf16[256,128]{1,0:T(8,128)(2,1)S(1)}, bf16[256,128]{1,0:T(8,128)(2,1)S(1)}, u32[]{:S(2)}, u32[]{:S(2)}) %collective-permute-start.4) | collective-permute-done | bytes 65568 | tf_op jit(solution)/shard_map/ppermute | solution.py:102
  29.9 3.4 %collective-permute-done.6 = bf16[256,128]{1,0:T(8,128)(2,1)S(1)} collective-permute-done((bf16[256,128]{1,0:T(8,128)(2,1)S(1)}, bf16[256,128]{1,0:T(8,128)(2,1)S(1)}, u32[]{:S(2)}, u32[]{:S(2)}) %collective-permute-start.6) | collective-permute-done | bytes 65568 | tf_op jit(solution)/shard_map/ppermute | solution.py:102
  33.3 2.3 %collective-permute-done.5 = bf16[256,128]{1,0:T(8,128)(2,1)S(1)} collective-permute-done((bf16[256,128]{1,0:T(8,128)(2,1)S(1)}, bf16[256,128]{1,0:T(8,128)(2,1)S(1)}, u32[]{:S(2)}, u32[]{:S(2)}) %collective-permute-start.5) | collective-permute-done | bytes 65568 | tf_op jit(solution)/shard_map/ppermute | solution.py:102
  35.6 1.6 %collective-permute-start.7 = (bf16[256,128]{1,0:T(8,128)(2,1)S(1)}, bf16[256,128]{1,0:T(8,128)(2,1)S(1)}, u32[]{:S(2)}, u32[]{:S(2)}) collective-permute-start(bf16[256,128]{1,0:T(8,128)(2,1)S(1)} %fusion.2), channel_id=1, source_target_pairs={{0,2},{2,0},{1,3},{3,1},{4,6},{6,4},{5,7},{7,5},{8,10},{10,8},{9,1... | collective-permute-start | bytes 196616 | tf_op jit(solution)/shard_map/ppermute | solution.py:614
  37.2 2.8 %collective-permute-done.7 = bf16[256,128]{1,0:T(8,128)(2,1)S(1)} collective-permute-done((bf16[256,128]{1,0:T(8,128)(2,1)S(1)}, bf16[256,128]{1,0:T(8,128)(2,1)S(1)}, u32[]{:S(2)}, u32[]{:S(2)}) %collective-permute-start.7) | collective-permute-done | bytes 65568 | tf_op jit(solution)/shard_map/ppermute | solution.py:614
  40.0 0.1 collective-permute-start.8
  40.1 1.3 %collective-permute-done.8.other = f32[256,128]{1,0:T(8,128)S(1)} collective-permute-done((f32[256,128]{1,0:T(8,128)S(1)}, f32[256,128]{1,0:T(8,128)S(1)}, u32[]{:S(2)}, u32[]{:S(2)}) %collective-permute-start.8) | collective-permute-done | bytes 131104 | tf_op jit(solution)/shard_map/ppermute | solution.py:617
  41.4 0.7 %assemble.1 = (f32[101,512]{1,0:T(8,128)}, f32[101,128]{1,0:T(8,128)}) custom-call(f32[256,128]{1,0:T(8,128)S(1)} %convert_add_fusion.whole, f32[256,128]{1,0:T(8,128)S(1)} %collective-permute-done.8.other), custom_call_target="tpu_custom_call" | custom-call | tf_op jit(solution)/shard_map/assemble/pallas_call | solution.py:563
  (3 shorter events, 0.1 us)
Async XLA Ops:
  0.6 8.4 %copy-start = (bf16[512,512]{1,0:T(8,128)(2,1)S(1)}, bf16[512,512]{1,0:T(8,128)(2,1)}, u32[]{:S(2)}) copy-start(bf16[512,512]{1,0:T(8,128)(2,1)} %constant.7.refs_3_.refs_7_) | copy-start | bytes 1572868
  1.3 14.1 %copy-start.1 = (bf16[2,256,512]{2,1,0:T(8,128)(2,1)S(1)}, bf16[2,256,512]{2,1,0:T(8,128)(2,1)}, u32[]{:S(2)}) copy-start(bf16[2,256,512]{2,1,0:T(8,128)(2,1)} %constant.12.refs_8_) | copy-start | bytes 1572868
  3.3 9.4 %collective-permute-start = (bf16[4,8704]{1,0:T(4,128)(2,1)}, bf16[4,8704]{1,0:T(4,128)(2,1)S(1)}, u32[]{:S(2)}, u32[]{:S(2)}) collective-permute-start(bf16[4,8704]{1,0:T(4,128)(2,1)} %get-tuple-element.12), channel_id=1, source_target_pairs={{0,4},{4,0},{8,12},{12,8},{1,5},{5,1},{9,13},{13,9},{2,6},{6,2},{1... | collective-permute-start | bytes 208904 | tf_op jit(solution)/shard_map/ppermute | solution.py:102
  6.5 7.7 %collective-permute-start.1 = (bf16[4,8704]{1,0:T(4,128)(2,1)}, bf16[4,8704]{1,0:T(4,128)(2,1)S(1)}, u32[]{:S(2)}, u32[]{:S(2)}) collective-permute-start(bf16[4,8704]{1,0:T(4,128)(2,1)} %get-tuple-element.13), channel_id=1, source_target_pairs={{0,8},{4,12},{8,0},{12,4},{1,9},{5,13},{9,1},{13,5},{2,10},{6,14},... | collective-permute-start | bytes 208904 | tf_op jit(solution)/shard_map/ppermute | solution.py:102
  9.0 6.4 %collective-permute-start.2 = (bf16[4,8704]{1,0:T(4,128)(2,1)}, bf16[4,8704]{1,0:T(4,128)(2,1)S(1)}, u32[]{:S(2)}, u32[]{:S(2)}) collective-permute-start(bf16[4,8704]{1,0:T(4,128)(2,1)} %get-tuple-element.14), channel_id=1, source_target_pairs={{0,12},{4,8},{8,4},{12,0},{1,13},{5,9},{9,5},{13,1},{2,14},{6,10},... | collective-permute-start | bytes 208904 | tf_op jit(solution)/shard_map/ppermute | solution.py:102
  9.0 0.9 %copy-start.2 = (bf16[4,8704]{1,0:T(4,128)(2,1)S(1)}, bf16[4,8704]{1,0:T(4,128)(2,1)}, u32[]{:S(2)}) copy-start(bf16[4,8704]{1,0:T(4,128)(2,1)} %get-tuple-element.11.refs_0_) | copy-start | bytes 208900
  9.9 0.7 %copy-start.4 = (s32[256,20]{0,1:T(8,128)S(1)}, s32[256,20]{0,1:T(8,128)}, u32[]{:S(2)}) copy-start(s32[256,20]{0,1:T(8,128)} %param.12) | copy-start | bytes 61444
  10.7 0.7 %copy-start.5 = (s32[256]{0:T(256)S(1)}, s32[256]{0:T(256)}, u32[]{:S(2)}) copy-start(s32[256]{0:T(256)} %param.11) | copy-start | bytes 3076
  11.3 4.1 %copy-start.3 = (bf16[4,8704]{1,0:T(4,128)(2,1)S(1)}, bf16[4,8704]{1,0:T(4,128)(2,1)}, u32[]{:S(2)}) copy-start(bf16[4,8704]{1,0:T(4,128)(2,1)} %get-tuple-element.11.refs_0_) | copy-start | bytes 208900
  23.9 1.6 %collective-permute-start.3 = (bf16[4,256,128]{2,1,0:T(8,128)(2,1)S(1)}, bf16[4,256,128]{2,1,0:T(8,128)(2,1)S(1)}, u32[]{:S(2)}, u32[]{:S(2)}) collective-permute-start(bf16[4,256,128]{2,1,0:T(8,128)(2,1)S(1)} %get-tuple-element.19), channel_id=1, source_target_pairs={{0,1},{1,0},{2,3},{3,2},{4,5},{5,4},{6,7},{7,6},{8,9},{9,8},{10,11... | collective-permute-start | bytes 786440 | tf_op jit(solution)/shard_map/ppermute | solution.py:600
  25.6 4.3 %collective-permute-start.4 = (bf16[256,128]{1,0:T(8,128)(2,1)S(1)}, bf16[256,128]{1,0:T(8,128)(2,1)S(1)}, u32[]{:S(2)}, u32[]{:S(2)}) collective-permute-start(bf16[256,128]{1,0:T(8,128)(2,1)S(1)} %get-tuple-element.20), channel_id=1, source_target_pairs={{0,4},{4,0},{8,12},{12,8},{1,5},{5,1},{9,13},{13,9},{2,6},{6,2},{1... | collective-permute-start | bytes 196616 | tf_op jit(solution)/shard_map/ppermute | solution.py:102
  26.4 6.9 %collective-permute-start.6 = (bf16[256,128]{1,0:T(8,128)(2,1)S(1)}, bf16[256,128]{1,0:T(8,128)(2,1)S(1)}, u32[]{:S(2)}, u32[]{:S(2)}) collective-permute-start(bf16[256,128]{1,0:T(8,128)(2,1)S(1)} %get-tuple-element.21), channel_id=1, source_target_pairs={{0,12},{4,8},{8,4},{12,0},{1,13},{5,9},{9,5},{13,1},{2,14},{6,10},... | collective-permute-start | bytes 196616 | tf_op jit(solution)/shard_map/ppermute | solution.py:102
  28.9 6.7 %collective-permute-start.5 = (bf16[256,128]{1,0:T(8,128)(2,1)S(1)}, bf16[256,128]{1,0:T(8,128)(2,1)S(1)}, u32[]{:S(2)}, u32[]{:S(2)}) collective-permute-start(bf16[256,128]{1,0:T(8,128)(2,1)S(1)} %get-tuple-element.22), channel_id=1, source_target_pairs={{0,8},{4,12},{8,0},{12,4},{1,9},{5,13},{9,1},{13,5},{2,10},{6,14},... | collective-permute-start | bytes 196616 | tf_op jit(solution)/shard_map/ppermute | solution.py:102
  35.6 4.3 %collective-permute-start.7 = (bf16[256,128]{1,0:T(8,128)(2,1)S(1)}, bf16[256,128]{1,0:T(8,128)(2,1)S(1)}, u32[]{:S(2)}, u32[]{:S(2)}) collective-permute-start(bf16[256,128]{1,0:T(8,128)(2,1)S(1)} %fusion.2), channel_id=1, source_target_pairs={{0,2},{2,0},{1,3},{3,1},{4,6},{6,4},{5,7},{7,5},{8,10},{10,8},{9,1... | collective-permute-start | bytes 196616 | tf_op jit(solution)/shard_map/ppermute | solution.py:614
  40.0 1.4 %collective-permute-start.8 = (f32[256,128]{1,0:T(8,128)S(1)}, f32[256,128]{1,0:T(8,128)S(1)}, u32[]{:S(2)}, u32[]{:S(2)}) collective-permute-start(f32[256,128]{1,0:T(8,128)S(1)} %convert_add_fusion.whole), channel_id=1, source_target_pairs={{0,1},{1,0},{2,3},{3,2},{4,5},{5,4},{6,7},{7,6},{8,9},{9,8},{10,11... | collective-permute-start | bytes 393224 | tf_op jit(solution)/shard_map/ppermute | solution.py:617

commit v11 on v10

--- a/solution.py
+++ b/solution.py
@@ -19,6 +19,8 @@
 HALF_LAGS = 51
 HALF_ROWS = 56
 TILE_ROWS = 48
+STEP_BITS = 7
+STEP = 1 << STEP_BITS
 VMEM_ONLY = pl.BlockSpec(memory_space=pltpu.VMEM)
 SMEM_ONLY = pl.BlockSpec(memory_space=pltpu.SMEM)
 NT = (((1,), (1,)), ((), ()))
@@ -357,6 +359,7 @@
     rows, tiles = cutter.rows, cutter.tiles
     events = regions * per_block
     cols = pair_cap // LANES
+    lines = pair_cap // STEP
     width = cols + slots // LANES
     batch = regions if separate(regions) else 1
     digits = digit_count(events)
@@ -387,13 +390,13 @@
             rows_out = []
             for k in range(2):
                 event = (listed(part, k).astype(jnp.int32) ^ (region << shift)) * (2 * rows)
-                rows_out += [event[:, c * LANES : (c + 1) * LANES] for c in range(cols)]
+                rows_out += [event[:, c * STEP : (c + 1) * STEP] for c in range(lines)]
             scalars = field(part, scalar_field(events))
             rows_out += [scalars[:, LANES : 2 * LANES].astype(jnp.int32)]
             for row, value in enumerate(rows_out):
-                index_vmem[part, row : row + 1, :] = value
+                index_vmem[part, row : row + 1, : value.shape[1]] = value
             slot = part - ready if static else part
-            index_vmem[part, 2 * cols + 1 : 2 * cols + 2, :per_block] = cutter.words(scalars, slot)
+            index_vmem[part, 2 * lines + 1 : 2 * lines + 2, :per_block] = cutter.words(scalars, slot)
         copy = pltpu.make_async_copy(index_vmem, index, sem)
         copy.start()
         if static:
@@ -410,17 +413,18 @@
         copy.wait()
 
         def cut(slot, carry):
-            cutter.cut(lambda event: index[slot + ready, 2 * cols + 1, event], shifted, windows, slot)
+            cutter.cut(lambda event: index[slot + ready, 2 * lines + 1, event], shifted, windows, slot)
             return carry
 
         def cut_and_transform(part, carry):
-            cutter.cut(lambda event: index[part, 2 * cols + 1, event], shifted, windows, 0)
+            cutter.cut(lambda event: index[part, 2 * lines + 1, event], shifted, windows, 0)
             place = pl.multiple_of(part * cutter.spec_rows, cutter.spec_rows)
             cutter.transform(windows, 0, weight_rows, part, table, spec, place)
             return carry
 
         if static:
-            lax.fori_loop(0, regions - ready, cut, 0)
+            for slot in range(regions - ready):
+                cut(slot, 0)
             for part in range(ready, regions):
                 cutter.transform(windows, part - ready, weight_rows, part, table, spec, part * cutter.spec_rows)
         else:
@@ -435,9 +439,9 @@
         def one_group(group, carry):
             def some_pairs(member, row):
                 part = group * batch + member
-                for step in range(LANES):
+                for step in range(STEP):
                     a = pl.multiple_of(index[part, row, step], 2 * rows)
-                    b = pl.multiple_of(index[part, cols + row, step], 2 * rows)
+                    b = pl.multiple_of(index[part, lines + row, step], 2 * rows)
                     cos_a, sin_a = spec[pl.ds(a, rows), :], spec[pl.ds(a + rows, rows), :]
                     cos_b, sin_b = spec[pl.ds(b, rows), :], spec[pl.ds(b + rows, rows), :]
                     sines = sin_a * sin_b
@@ -445,18 +449,19 @@
                     odd = jnp.where(special, sines, sin_a * cos_b - cos_a * sin_b)
                     even += pltpu.roll(even, nch, 0)
                     odd += pltpu.roll(odd, nch, 0)
-                    place = pl.multiple_of(((member * cols + row) * LANES + step) * rows, rows)
+                    place = pl.multiple_of((member * pair_cap + row * STEP + step) * rows, rows)
                     prod[pl.ds(place, rows), :] = jnp.where(upper, even, odd)
                 return member
 
             def pairs_of(member, inner):
                 part = group * batch + member
-                pairs = index[part, 2 * cols, 0] * LANES + index[part, 2 * cols, per_block]
-                lax.fori_loop(0, jnp.minimum((pairs + LANES - 1) // LANES, cols), lambda row, m: some_pairs(m, row),
+                pairs = index[part, 2 * lines, 0] * LANES + index[part, 2 * lines, per_block]
+                lax.fori_loop(0, jnp.minimum((pairs + STEP - 1) >> STEP_BITS, lines), lambda row, m: some_pairs(m, row),
                               member)
                 return inner
 
-            lax.fori_loop(0, batch, pairs_of, 0)
+            for member in range(batch):
+                pairs_of(member, 0)
             for member in range(batch):
                 part = group * batch + member
                 first_row = member * pair_cap * rows
@@ -517,10 +522,14 @@
             given[part] = folded[part].astype(jnp.bfloat16)
             return carry
 
-        lax.fori_loop(0, regions, finish, 0)
+        if static:
+            for part in range(regions):
+                finish(part, 0)
+        else:
+            lax.fori_loop(0, regions, finish, 0)
 
     shape = (regions, folded_rows(pair_cap + slots), LANES)
-    index_rows = 8 * -(-(2 * cols + 2) // 8)
+    index_rows = 8 * -(-(2 * lines + 2) // 8)
     used = regions * (tiles * rows + 3 * HALF_ROWS * width + 3 * LANES + index_rows + 4 * tiles + slots) + ready * cutter.spec_rows
     used += (2 * per_block * batch + 2 * events + batch * pair_cap) * rows + events * nch + 3 * NFFT
     return pl.pallas_call(

time: 42.4 us -> 41.6 us (0.981)
  Pallas kernels: 12.5 us -> 11.8 us
    pallas_call x1, Pallas kernels: 8.46 us -> 7.71 us  [locate(): correlate(regions, per_block, pair_cap, segment, slots, nch, ready)]
where the time goes in v11:
time: 41.6 us; the launch traced here: 41.4 us
  waiting for transfers between devices  14.8 us (36%)
  Pallas kernels  11.8 us (28%)
  starting transfers between devices  11 us (26%)
  local copies, waits for them, and re-layouts  2.32 us (6%)
  between operations  1.42 us (3%)
    ppermute x6, starting transfers between devices, exchange(): lax.ppermute(blocks[m], 'region', [(i, i ^ m) for i in range(regions)])  9.26 us
    ppermute x6, waiting for transfers between devices, exchange(): lax.ppermute(blocks[m], 'region', [(i, i ^ m) for i in range(regions)])  9.15 us
    pallas_call x1, Pallas kernels, locate(): correlate(regions, per_block, pair_cap, segment, slots, nch, ready)  7.71 us
    ppermute x1, waiting for transfers between devices, locate(): other = lax.ppermute(sent, 'stn', [(i, i ^ step) for i in range(count)])  2.77 us
    unnamed x12, local copies, waits for them, and re-layouts  2.32 us
    pallas_call x1, Pallas kernels, pack(): pl.pallas_call(kernel, out_shape=block_shapes(regions, (nch, segment + fi...  1.97 us
    ppermute x1, starting transfers between devices, locate(): other = lax.ppermute(sent, 'stn', [(i, i ^ step) for i in range(count)])  1.56 us
    ppermute x1, waiting for transfers between devices, locate(): swapped = lax.ppermute(given, 'chan', swap)  1.52 us
  transfers between devices with their start and end apart: 9, of which 8 were waited for; matrix products, arithmetic and copies ran while one was open for 0% of the time, Pallas kernels for 3%

profile of v11, /device:TPU:0, one launch (start us, length us, event | category | flops | bytes accessed | tf_op | source)
XLA Modules:
  0.0 41.4 jit_solution(10789297176022433899)
XLA Ops:
  0.6 0.0 copy-start
  1.3 0.0 copy-start.1
  1.4 2.0 %pack.1 = (bf16[4,8704]{1,0:T(4,128)(2,1)}, bf16[4,8704]{1,0:T(4,128)(2,1)}, bf16[4,8704]{1,0:T(4,128)(2,1)}, bf16[4,8704]{1,0:T(4,128)(2,1)}) custom-call(bf16[10,3,8192]{2,1,0:T(4,128)(2,1)} %refs_0_.1, s32[1,64]{1,0:T(1,128)} %bitcast.24, s32[20,256]{1,0:T(8,128)} %bitcast.19, s32[1,512]{1,0:T(1,128)} %bitcast.22, s32[1,512]{1,0:T(1,128)} %bitcast.23, ...), custom_call_target="tpu_custom_call" | custom-call | tf_op jit(solution)/shard_map/pack/pallas_call | solution.py:170
  3.3 3.1 %collective-permute-start = (bf16[4,8704]{1,0:T(4,128)(2,1)}, bf16[4,8704]{1,0:T(4,128)(2,1)S(1)}, u32[]{:S(2)}, u32[]{:S(2)}) collective-permute-start(bf16[4,8704]{1,0:T(4,128)(2,1)} %get-tuple-element.12), channel_id=1, source_target_pairs={{0,4},{4,0},{8,12},{12,8},{1,5},{5,1},{9,13},{13,9},{2,6},{6,2},{1... | collective-permute-start | bytes 208904 | tf_op jit(solution)/shard_map/ppermute | solution.py:104
  6.5 2.6 %collective-permute-start.1 = (bf16[4,8704]{1,0:T(4,128)(2,1)}, bf16[4,8704]{1,0:T(4,128)(2,1)S(1)}, u32[]{:S(2)}, u32[]{:S(2)}) collective-permute-start(bf16[4,8704]{1,0:T(4,128)(2,1)} %get-tuple-element.13), channel_id=1, source_target_pairs={{0,8},{4,12},{8,0},{12,4},{1,9},{5,13},{9,1},{13,5},{2,10},{6,14},... | collective-permute-start | bytes 208904 | tf_op jit(solution)/shard_map/ppermute | solution.py:104
  9.0 0.0 collective-permute-start.2
  9.0 0.0 copy-done
  9.0 0.0 copy-start.2
  9.0 0.9 %copy-done.2 = bf16[4,8704]{1,0:T(4,128)(2,1)S(1)} copy-done((bf16[4,8704]{1,0:T(4,128)(2,1)S(1)}, bf16[4,8704]{1,0:T(4,128)(2,1)}, u32[]{:S(2)}) %copy-start.2) | copy-done | bytes 69656
  9.9 0.0 copy-start.4
  9.9 0.7 %copy-done.4 = s32[256,20]{0,1:T(8,128)S(1)} copy-done((s32[256,20]{0,1:T(8,128)S(1)}, s32[256,20]{0,1:T(8,128)}, u32[]{:S(2)}) %copy-start.4) | copy-done | bytes 20504
  10.7 0.0 copy-start.5
  10.7 0.7 %copy-done.5 = s32[256]{0:T(256)S(1)} copy-done((s32[256]{0:T(256)S(1)}, s32[256]{0:T(256)}, u32[]{:S(2)}) %copy-start.5) | copy-done | bytes 1048
  11.3 0.0 copy-start.3
  11.4 1.4 %prepare.1 = (bf16[512,128]{1,0:T(8,128)(2,1)S(1)}, f32[1024,128]{1,0:T(8,128)S(1)}, f32[1024,128]{1,0:T(8,128)S(1)}) custom-call(bf16[4,8704]{1,0:T(4,128)(2,1)S(1)} %copy-done.2, s32[20,256]{1,0:T(8,128)S(1)} %bitcast.20, s32[1,256]{1,0:T(1,128)S(1)} %bitcast.21, bf16[512,512]{1,0:T(8,128)(2,1)S(1)} %copy-done), custom_call_target="tpu_custom_call" | custom-call | tf_op jit(solution)/shard_map/prepare/pallas_call | solution.py:346
  12.8 0.0 collective-permute-done.refs_1_
  12.8 1.4 %collective-permute-done.1.refs_2_ = bf16[4,8704]{1,0:T(4,128)(2,1)S(1)} collective-permute-done((bf16[4,8704]{1,0:T(4,128)(2,1)}, bf16[4,8704]{1,0:T(4,128)(2,1)S(1)}, u32[]{:S(2)}, u32[]{:S(2)}) %collective-permute-start.1) | collective-permute-done | bytes 69664 | tf_op jit(solution)/shard_map/ppermute | solution.py:104
  14.2 1.3 %collective-permute-done.2.refs_3_ = bf16[4,8704]{1,0:T(4,128)(2,1)S(1)} collective-permute-done((bf16[4,8704]{1,0:T(4,128)(2,1)}, bf16[4,8704]{1,0:T(4,128)(2,1)S(1)}, u32[]{:S(2)}, u32[]{:S(2)}) %collective-permute-start.2) | collective-permute-done | bytes 69664 | tf_op jit(solution)/shard_map/ppermute | solution.py:104
  15.5 0.0 copy-done.1
  15.5 0.0 copy-done.3
  15.5 7.7 %correlate.1 = (f32[4,256,128]{2,1,0:T(8,128)S(1)}, bf16[4,256,128]{2,1,0:T(8,128)(2,1)S(1)}) custom-call(bf16[4,8704]{1,0:T(4,128)(2,1)S(1)} %copy-done.3, bf16[4,8704]{1,0:T(4,128)(2,1)S(1)} %collective-permute-done.refs_1_, bf16[4,8704]{1,0:T(4,128)(2,1)S(1)} %collective-permute-done.1.refs_2_, bf16[4,8704]{1,0:T(4,128)(2,1)S(1)} %collective-permute-done.2.refs_3_, ...), custom_call_target="tpu_custom_call" | custom-call | tf_op jit(solution)/shard_map/correlate/pallas_call | solution.py:605
  23.2 0.1 collective-permute-start.3
  23.3 1.5 %collective-permute-done.3 = bf16[4,256,128]{2,1,0:T(8,128)(2,1)S(1)} collective-permute-done((bf16[4,256,128]{2,1,0:T(8,128)(2,1)S(1)}, bf16[4,256,128]{2,1,0:T(8,128)(2,1)S(1)}, u32[]{:S(2)}, u32[]{:S(2)}) %collective-permute-start.3) | collective-permute-done | bytes 262176 | tf_op jit(solution)/shard_map/ppermute | solution.py:609
  24.8 0.9 %collective-permute-start.4 = (bf16[256,128]{1,0:T(8,128)(2,1)S(1)}, bf16[256,128]{1,0:T(8,128)(2,1)S(1)}, u32[]{:S(2)}, u32[]{:S(2)}) collective-permute-start(bf16[256,128]{1,0:T(8,128)(2,1)S(1)} %get-tuple-element.20), channel_id=1, source_target_pairs={{0,4},{4,0},{8,12},{12,8},{1,5},{5,1},{9,13},{13,9},{2,6},{6,2},{1... | collective-permute-start | bytes 196616 | tf_op jit(solution)/shard_map/ppermute | solution.py:104
  25.7 2.5 %collective-permute-start.6 = (bf16[256,128]{1,0:T(8,128)(2,1)S(1)}, bf16[256,128]{1,0:T(8,128)(2,1)S(1)}, u32[]{:S(2)}, u32[]{:S(2)}) collective-permute-start(bf16[256,128]{1,0:T(8,128)(2,1)S(1)} %get-tuple-element.21), channel_id=1, source_target_pairs={{0,12},{4,8},{8,4},{12,0},{1,13},{5,9},{9,5},{13,1},{2,14},{6,10},... | collective-permute-start | bytes 196616 | tf_op jit(solution)/shard_map/ppermute | solution.py:104
  28.2 0.2 collective-permute-start.5
  28.4 0.8 %collective-permute-done.4 = bf16[256,128]{1,0:T(8,128)(2,1)S(1)} collective-permute-done((bf16[256,128]{1,0:T(8,128)(2,1)S(1)}, bf16[256,128]{1,0:T(8,128)(2,1)S(1)}, u32[]{:S(2)}, u32[]{:S(2)}) %collective-permute-start.4) | collective-permute-done | bytes 65568 | tf_op jit(solution)/shard_map/ppermute | solution.py:104
  29.2 3.4 %collective-permute-done.6 = bf16[256,128]{1,0:T(8,128)(2,1)S(1)} collective-permute-done((bf16[256,128]{1,0:T(8,128)(2,1)S(1)}, bf16[256,128]{1,0:T(8,128)(2,1)S(1)}, u32[]{:S(2)}, u32[]{:S(2)}) %collective-permute-start.6) | collective-permute-done | bytes 65568 | tf_op jit(solution)/shard_map/ppermute | solution.py:104
  32.6 2.3 %collective-permute-done.5 = bf16[256,128]{1,0:T(8,128)(2,1)S(1)} collective-permute-done((bf16[256,128]{1,0:T(8,128)(2,1)S(1)}, bf16[256,128]{1,0:T(8,128)(2,1)S(1)}, u32[]{:S(2)}, u32[]{:S(2)}) %collective-permute-start.5) | collective-permute-done | bytes 65568 | tf_op jit(solution)/shard_map/ppermute | solution.py:104
  34.9 1.6 %collective-permute-start.7 = (bf16[256,128]{1,0:T(8,128)(2,1)S(1)}, bf16[256,128]{1,0:T(8,128)(2,1)S(1)}, u32[]{:S(2)}, u32[]{:S(2)}) collective-permute-start(bf16[256,128]{1,0:T(8,128)(2,1)S(1)} %fusion.2), channel_id=1, source_target_pairs={{0,2},{2,0},{1,3},{3,1},{4,6},{6,4},{5,7},{7,5},{8,10},{10,8},{9,1... | collective-permute-start | bytes 196616 | tf_op jit(solution)/shard_map/ppermute | solution.py:623
  36.4 2.8 %collective-permute-done.7 = bf16[256,128]{1,0:T(8,128)(2,1)S(1)} collective-permute-done((bf16[256,128]{1,0:T(8,128)(2,1)S(1)}, bf16[256,128]{1,0:T(8,128)(2,1)S(1)}, u32[]{:S(2)}, u32[]{:S(2)}) %collective-permute-start.7) | collective-permute-done | bytes 65568 | tf_op jit(solution)/shard_map/ppermute | solution.py:623
  39.2 0.1 collective-permute-start.8
  39.3 1.3 %collective-permute-done.8.other = f32[256,128]{1,0:T(8,128)S(1)} collective-permute-done((f32[256,128]{1,0:T(8,128)S(1)}, f32[256,128]{1,0:T(8,128)S(1)}, u32[]{:S(2)}, u32[]{:S(2)}) %collective-permute-start.8) | collective-permute-done | bytes 131104 | tf_op jit(solution)/shard_map/ppermute | solution.py:626
  40.7 0.7 %assemble.1 = (f32[101,512]{1,0:T(8,128)}, f32[101,128]{1,0:T(8,128)}) custom-call(f32[256,128]{1,0:T(8,128)S(1)} %convert_add_fusion.whole, f32[256,128]{1,0:T(8,128)S(1)} %collective-permute-done.8.other), custom_call_target="tpu_custom_call" | custom-call | tf_op jit(solution)/shard_map/assemble/pallas_call | solution.py:572
  (3 shorter events, 0.1 us)
Async XLA Ops:
  0.6 8.4 %copy-start = (bf16[512,512]{1,0:T(8,128)(2,1)S(1)}, bf16[512,512]{1,0:T(8,128)(2,1)}, u32[]{:S(2)}) copy-start(bf16[512,512]{1,0:T(8,128)(2,1)} %constant.7.refs_3_.refs_7_) | copy-start | bytes 1572868
  1.3 14.1 %copy-start.1 = (bf16[2,256,512]{2,1,0:T(8,128)(2,1)S(1)}, bf16[2,256,512]{2,1,0:T(8,128)(2,1)}, u32[]{:S(2)}) copy-start(bf16[2,256,512]{2,1,0:T(8,128)(2,1)} %constant.12.refs_8_) | copy-start | bytes 1572868
  3.3 9.4 %collective-permute-start = (bf16[4,8704]{1,0:T(4,128)(2,1)}, bf16[4,8704]{1,0:T(4,128)(2,1)S(1)}, u32[]{:S(2)}, u32[]{:S(2)}) collective-permute-start(bf16[4,8704]{1,0:T(4,128)(2,1)} %get-tuple-element.12), channel_id=1, source_target_pairs={{0,4},{4,0},{8,12},{12,8},{1,5},{5,1},{9,13},{13,9},{2,6},{6,2},{1... | collective-permute-start | bytes 208904 | tf_op jit(solution)/shard_map/ppermute | solution.py:104
  6.5 7.7 %collective-permute-start.1 = (bf16[4,8704]{1,0:T(4,128)(2,1)}, bf16[4,8704]{1,0:T(4,128)(2,1)S(1)}, u32[]{:S(2)}, u32[]{:S(2)}) collective-permute-start(bf16[4,8704]{1,0:T(4,128)(2,1)} %get-tuple-element.13), channel_id=1, source_target_pairs={{0,8},{4,12},{8,0},{12,4},{1,9},{5,13},{9,1},{13,5},{2,10},{6,14},... | collective-permute-start | bytes 208904 | tf_op jit(solution)/shard_map/ppermute | solution.py:104
  9.0 6.4 %collective-permute-start.2 = (bf16[4,8704]{1,0:T(4,128)(2,1)}, bf16[4,8704]{1,0:T(4,128)(2,1)S(1)}, u32[]{:S(2)}, u32[]{:S(2)}) collective-permute-start(bf16[4,8704]{1,0:T(4,128)(2,1)} %get-tuple-element.14), channel_id=1, source_target_pairs={{0,12},{4,8},{8,4},{12,0},{1,13},{5,9},{9,5},{13,1},{2,14},{6,10},... | collective-permute-start | bytes 208904 | tf_op jit(solution)/shard_map/ppermute | solution.py:104
  9.0 0.9 %copy-start.2 = (bf16[4,8704]{1,0:T(4,128)(2,1)S(1)}, bf16[4,8704]{1,0:T(4,128)(2,1)}, u32[]{:S(2)}) copy-start(bf16[4,8704]{1,0:T(4,128)(2,1)} %get-tuple-element.11.refs_0_) | copy-start | bytes 208900
  9.9 0.7 %copy-start.4 = (s32[256,20]{0,1:T(8,128)S(1)}, s32[256,20]{0,1:T(8,128)}, u32[]{:S(2)}) copy-start(s32[256,20]{0,1:T(8,128)} %param.12) | copy-start | bytes 61444
  10.7 0.7 %copy-start.5 = (s32[256]{0:T(256)S(1)}, s32[256]{0:T(256)}, u32[]{:S(2)}) copy-start(s32[256]{0:T(256)} %param.11) | copy-start | bytes 3076
  11.3 4.1 %copy-start.3 = (bf16[4,8704]{1,0:T(4,128)(2,1)S(1)}, bf16[4,8704]{1,0:T(4,128)(2,1)}, u32[]{:S(2)}) copy-start(bf16[4,8704]{1,0:T(4,128)(2,1)} %get-tuple-element.11.refs_0_) | copy-start | bytes 208900
  23.2 1.6 %collective-permute-start.3 = (bf16[4,256,128]{2,1,0:T(8,128)(2,1)S(1)}, bf16[4,256,128]{2,1,0:T(8,128)(2,1)S(1)}, u32[]{:S(2)}, u32[]{:S(2)}) collective-permute-start(bf16[4,256,128]{2,1,0:T(8,128)(2,1)S(1)} %get-tuple-element.19), channel_id=1, source_target_pairs={{0,1},{1,0},{2,3},{3,2},{4,5},{5,4},{6,7},{7,6},{8,9},{9,8},{10,11... | collective-permute-start | bytes 786440 | tf_op jit(solution)/shard_map/ppermute | solution.py:609
  24.8 4.3 %collective-permute-start.4 = (bf16[256,128]{1,0:T(8,128)(2,1)S(1)}, bf16[256,128]{1,0:T(8,128)(2,1)S(1)}, u32[]{:S(2)}, u32[]{:S(2)}) collective-permute-start(bf16[256,128]{1,0:T(8,128)(2,1)S(1)} %get-tuple-element.20), channel_id=1, source_target_pairs={{0,4},{4,0},{8,12},{12,8},{1,5},{5,1},{9,13},{13,9},{2,6},{6,2},{1... | collective-permute-start | bytes 196616 | tf_op jit(solution)/shard_map/ppermute | solution.py:104
  25.7 6.9 %collective-permute-start.6 = (bf16[256,128]{1,0:T(8,128)(2,1)S(1)}, bf16[256,128]{1,0:T(8,128)(2,1)S(1)}, u32[]{:S(2)}, u32[]{:S(2)}) collective-permute-start(bf16[256,128]{1,0:T(8,128)(2,1)S(1)} %get-tuple-element.21), channel_id=1, source_target_pairs={{0,12},{4,8},{8,4},{12,0},{1,13},{5,9},{9,5},{13,1},{2,14},{6,10},... | collective-permute-start | bytes 196616 | tf_op jit(solution)/shard_map/ppermute | solution.py:104
  28.2 6.7 %collective-permute-start.5 = (bf16[256,128]{1,0:T(8,128)(2,1)S(1)}, bf16[256,128]{1,0:T(8,128)(2,1)S(1)}, u32[]{:S(2)}, u32[]{:S(2)}) collective-permute-start(bf16[256,128]{1,0:T(8,128)(2,1)S(1)} %get-tuple-element.22), channel_id=1, source_target_pairs={{0,8},{4,12},{8,0},{12,4},{1,9},{5,13},{9,1},{13,5},{2,10},{6,14},... | collective-permute-start | bytes 196616 | tf_op jit(solution)/shard_map/ppermute | solution.py:104
  34.9 4.3 %collective-permute-start.7 = (bf16[256,128]{1,0:T(8,128)(2,1)S(1)}, bf16[256,128]{1,0:T(8,128)(2,1)S(1)}, u32[]{:S(2)}, u32[]{:S(2)}) collective-permute-start(bf16[256,128]{1,0:T(8,128)(2,1)S(1)} %fusion.2), channel_id=1, source_target_pairs={{0,2},{2,0},{1,3},{3,1},{4,6},{6,4},{5,7},{7,5},{8,10},{10,8},{9,1... | collective-permute-start | bytes 196616 | tf_op jit(solution)/shard_map/ppermute | solution.py:623
  39.2 1.4 %collective-permute-start.8 = (f32[256,128]{1,0:T(8,128)S(1)}, f32[256,128]{1,0:T(8,128)S(1)}, u32[]{:S(2)}, u32[]{:S(2)}) collective-permute-start(f32[256,128]{1,0:T(8,128)S(1)} %convert_add_fusion.whole), channel_id=1, source_target_pairs={{0,1},{1,0},{2,3},{3,2},{4,5},{5,4},{6,7},{7,6},{8,9},{9,8},{10,11... | collective-permute-start | bytes 393224 | tf_op jit(solution)/shard_map/ppermute | solution.py:626

commit v12 on v11

--- a/solution.py
+++ b/solution.py
@@ -1,3 +1,4 @@
+import functools
 import math
 
 import jax
@@ -447,17 +448,20 @@
                     sines = sin_a * sin_b
                     even = cos_a * cos_b + sines
                     odd = jnp.where(special, sines, sin_a * cos_b - cos_a * sin_b)
-                    even += pltpu.roll(even, nch, 0)
-                    odd += pltpu.roll(odd, nch, 0)
+                    first, other = jnp.where(upper, even, odd), jnp.where(upper, odd, even)
                     place = pl.multiple_of((member * pair_cap + row * STEP + step) * rows, rows)
-                    prod[pl.ds(place, rows), :] = jnp.where(upper, even, odd)
-                return member
+                    prod[pl.ds(place, rows), :] = first + pltpu.roll(other, nch, 0)
+                return None if static else member
 
             def pairs_of(member, inner):
                 part = group * batch + member
                 pairs = index[part, 2 * lines, 0] * LANES + index[part, 2 * lines, per_block]
-                lax.fori_loop(0, jnp.minimum((pairs + STEP - 1) >> STEP_BITS, lines), lambda row, m: some_pairs(m, row),
-                              member)
+                if static:
+                    for row in range(lines):
+                        pl.when(row * STEP < pairs)(functools.partial(some_pairs, member, row))
+                else:
+                    lax.fori_loop(0, jnp.minimum((pairs + STEP - 1) >> STEP_BITS, lines),
+                                  lambda row, m: some_pairs(m, row), member)
                 return inner
 
             for member in range(batch):

time: 41.6 us -> 41.4 us (level)
  no operation moved by 1% of the time
where the time goes in v12:
time: 41.4 us; the launch traced here: 41.1 us
  waiting for transfers between devices  14.8 us (36%)
  Pallas kernels  11.6 us (28%)
  starting transfers between devices  11 us (27%)
  local copies, waits for them, and re-layouts  2.32 us (6%)
  between operations  1.42 us (3%)
    ppermute x6, starting transfers between devices, exchange(): lax.ppermute(blocks[m], 'region', [(i, i ^ m) for i in range(regions)])  9.26 us
    ppermute x6, waiting for transfers between devices, exchange(): lax.ppermute(blocks[m], 'region', [(i, i ^ m) for i in range(regions)])  9.15 us
    pallas_call x1, Pallas kernels, locate(): correlate(regions, per_block, pair_cap, segment, slots, nch, ready)  7.47 us
    ppermute x1, waiting for transfers between devices, locate(): other = lax.ppermute(sent, 'stn', [(i, i ^ step) for i in range(count)])  2.76 us
    unnamed x12, local copies, waits for them, and re-layouts  2.32 us
    pallas_call x1, Pallas kernels, pack(): pl.pallas_call(kernel, out_shape=block_shapes(regions, (nch, segment + fi...  1.97 us
    ppermute x1, starting transfers between devices, locate(): other = lax.ppermute(sent, 'stn', [(i, i ^ step) for i in range(count)])  1.57 us
    ppermute x1, waiting for transfers between devices, locate(): swapped = lax.ppermute(given, 'chan', swap)  1.52 us
  transfers between devices with their start and end apart: 9, of which 8 were waited for; matrix products, arithmetic and copies ran while one was open for 0% of the time, Pallas kernels for 3%

profile of v12, /device:TPU:0, one launch (start us, length us, event | category | flops | bytes accessed | tf_op | source)
XLA Modules:
  0.0 41.1 jit_solution(9141736713381836612)
XLA Ops:
  0.6 0.0 copy-start
  1.3 0.0 copy-start.1
  1.4 2.0 %pack.1 = (bf16[4,8704]{1,0:T(4,128)(2,1)}, bf16[4,8704]{1,0:T(4,128)(2,1)}, bf16[4,8704]{1,0:T(4,128)(2,1)}, bf16[4,8704]{1,0:T(4,128)(2,1)}) custom-call(bf16[10,3,8192]{2,1,0:T(4,128)(2,1)} %refs_0_.1, s32[1,64]{1,0:T(1,128)} %bitcast.24, s32[20,256]{1,0:T(8,128)} %bitcast.19, s32[1,512]{1,0:T(1,128)} %bitcast.22, s32[1,512]{1,0:T(1,128)} %bitcast.23, ...), custom_call_target="tpu_custom_call" | custom-call | tf_op jit(solution)/shard_map/pack/pallas_call | solution.py:171
  3.3 3.1 %collective-permute-start = (bf16[4,8704]{1,0:T(4,128)(2,1)}, bf16[4,8704]{1,0:T(4,128)(2,1)S(1)}, u32[]{:S(2)}, u32[]{:S(2)}) collective-permute-start(bf16[4,8704]{1,0:T(4,128)(2,1)} %get-tuple-element.12), channel_id=1, source_target_pairs={{0,4},{4,0},{8,12},{12,8},{1,5},{5,1},{9,13},{13,9},{2,6},{6,2},{1... | collective-permute-start | bytes 208904 | tf_op jit(solution)/shard_map/ppermute | solution.py:105
  6.5 2.6 %collective-permute-start.1 = (bf16[4,8704]{1,0:T(4,128)(2,1)}, bf16[4,8704]{1,0:T(4,128)(2,1)S(1)}, u32[]{:S(2)}, u32[]{:S(2)}) collective-permute-start(bf16[4,8704]{1,0:T(4,128)(2,1)} %get-tuple-element.13), channel_id=1, source_target_pairs={{0,8},{4,12},{8,0},{12,4},{1,9},{5,13},{9,1},{13,5},{2,10},{6,14},... | collective-permute-start | bytes 208904 | tf_op jit(solution)/shard_map/ppermute | solution.py:105
  9.0 0.0 collective-permute-start.2
  9.0 0.0 copy-done
  9.0 0.0 copy-start.2
  9.0 0.9 %copy-done.2 = bf16[4,8704]{1,0:T(4,128)(2,1)S(1)} copy-done((bf16[4,8704]{1,0:T(4,128)(2,1)S(1)}, bf16[4,8704]{1,0:T(4,128)(2,1)}, u32[]{:S(2)}) %copy-start.2) | copy-done | bytes 69656
  9.9 0.0 copy-start.4
  9.9 0.7 %copy-done.4 = s32[256,20]{0,1:T(8,128)S(1)} copy-done((s32[256,20]{0,1:T(8,128)S(1)}, s32[256,20]{0,1:T(8,128)}, u32[]{:S(2)}) %copy-start.4) | copy-done | bytes 20504
  10.7 0.0 copy-start.5
  10.7 0.7 %copy-done.5 = s32[256]{0:T(256)S(1)} copy-done((s32[256]{0:T(256)S(1)}, s32[256]{0:T(256)}, u32[]{:S(2)}) %copy-start.5) | copy-done | bytes 1048
  11.3 0.0 copy-start.3
  11.4 1.4 %prepare.1 = (bf16[512,128]{1,0:T(8,128)(2,1)S(1)}, f32[1024,128]{1,0:T(8,128)S(1)}, f32[1024,128]{1,0:T(8,128)S(1)}) custom-call(bf16[4,8704]{1,0:T(4,128)(2,1)S(1)} %copy-done.2, s32[20,256]{1,0:T(8,128)S(1)} %bitcast.20, s32[1,256]{1,0:T(1,128)S(1)} %bitcast.21, bf16[512,512]{1,0:T(8,128)(2,1)S(1)} %copy-done), custom_call_target="tpu_custom_call" | custom-call | tf_op jit(solution)/shard_map/prepare/pallas_call | solution.py:347
  12.8 0.0 collective-permute-done.refs_1_
  12.8 1.4 %collective-permute-done.1.refs_2_ = bf16[4,8704]{1,0:T(4,128)(2,1)S(1)} collective-permute-done((bf16[4,8704]{1,0:T(4,128)(2,1)}, bf16[4,8704]{1,0:T(4,128)(2,1)S(1)}, u32[]{:S(2)}, u32[]{:S(2)}) %collective-permute-start.1) | collective-permute-done | bytes 69664 | tf_op jit(solution)/shard_map/ppermute | solution.py:105
  14.2 1.3 %collective-permute-done.2.refs_3_ = bf16[4,8704]{1,0:T(4,128)(2,1)S(1)} collective-permute-done((bf16[4,8704]{1,0:T(4,128)(2,1)}, bf16[4,8704]{1,0:T(4,128)(2,1)S(1)}, u32[]{:S(2)}, u32[]{:S(2)}) %collective-permute-start.2) | collective-permute-done | bytes 69664 | tf_op jit(solution)/shard_map/ppermute | solution.py:105
  15.5 0.0 copy-done.1
  15.5 0.0 copy-done.3
  15.5 7.5 %correlate.1 = (f32[4,256,128]{2,1,0:T(8,128)S(1)}, bf16[4,256,128]{2,1,0:T(8,128)(2,1)S(1)}) custom-call(bf16[4,8704]{1,0:T(4,128)(2,1)S(1)} %copy-done.3, bf16[4,8704]{1,0:T(4,128)(2,1)S(1)} %collective-permute-done.refs_1_, bf16[4,8704]{1,0:T(4,128)(2,1)S(1)} %collective-permute-done.1.refs_2_, bf16[4,8704]{1,0:T(4,128)(2,1)S(1)} %collective-permute-done.2.refs_3_, ...), custom_call_target="tpu_custom_call" | custom-call | tf_op jit(solution)/shard_map/correlate/pallas_call | solution.py:609
  22.9 0.1 collective-permute-start.3
  23.0 1.5 %collective-permute-done.3 = bf16[4,256,128]{2,1,0:T(8,128)(2,1)S(1)} collective-permute-done((bf16[4,256,128]{2,1,0:T(8,128)(2,1)S(1)}, bf16[4,256,128]{2,1,0:T(8,128)(2,1)S(1)}, u32[]{:S(2)}, u32[]{:S(2)}) %collective-permute-start.3) | collective-permute-done | bytes 262176 | tf_op jit(solution)/shard_map/ppermute | solution.py:613
  24.6 0.9 %collective-permute-start.4 = (bf16[256,128]{1,0:T(8,128)(2,1)S(1)}, bf16[256,128]{1,0:T(8,128)(2,1)S(1)}, u32[]{:S(2)}, u32[]{:S(2)}) collective-permute-start(bf16[256,128]{1,0:T(8,128)(2,1)S(1)} %get-tuple-element.20), channel_id=1, source_target_pairs={{0,4},{4,0},{8,12},{12,8},{1,5},{5,1},{9,13},{13,9},{2,6},{6,2},{1... | collective-permute-start | bytes 196616 | tf_op jit(solution)/shard_map/ppermute | solution.py:105
  25.5 2.5 %collective-permute-start.6 = (bf16[256,128]{1,0:T(8,128)(2,1)S(1)}, bf16[256,128]{1,0:T(8,128)(2,1)S(1)}, u32[]{:S(2)}, u32[]{:S(2)}) collective-permute-start(bf16[256,128]{1,0:T(8,128)(2,1)S(1)} %get-tuple-element.21), channel_id=1, source_target_pairs={{0,12},{4,8},{8,4},{12,0},{1,13},{5,9},{9,5},{13,1},{2,14},{6,10},... | collective-permute-start | bytes 196616 | tf_op jit(solution)/shard_map/ppermute | solution.py:105
  27.9 0.2 collective-permute-start.5
  28.1 0.8 %collective-permute-done.4 = bf16[256,128]{1,0:T(8,128)(2,1)S(1)} collective-permute-done((bf16[256,128]{1,0:T(8,128)(2,1)S(1)}, bf16[256,128]{1,0:T(8,128)(2,1)S(1)}, u32[]{:S(2)}, u32[]{:S(2)}) %collective-permute-start.4) | collective-permute-done | bytes 65568 | tf_op jit(solution)/shard_map/ppermute | solution.py:105
  28.9 3.4 %collective-permute-done.6 = bf16[256,128]{1,0:T(8,128)(2,1)S(1)} collective-permute-done((bf16[256,128]{1,0:T(8,128)(2,1)S(1)}, bf16[256,128]{1,0:T(8,128)(2,1)S(1)}, u32[]{:S(2)}, u32[]{:S(2)}) %collective-permute-start.6) | collective-permute-done | bytes 65568 | tf_op jit(solution)/shard_map/ppermute | solution.py:105
  32.3 2.3 %collective-permute-done.5 = bf16[256,128]{1,0:T(8,128)(2,1)S(1)} collective-permute-done((bf16[256,128]{1,0:T(8,128)(2,1)S(1)}, bf16[256,128]{1,0:T(8,128)(2,1)S(1)}, u32[]{:S(2)}, u32[]{:S(2)}) %collective-permute-start.5) | collective-permute-done | bytes 65568 | tf_op jit(solution)/shard_map/ppermute | solution.py:105
  34.6 1.6 %collective-permute-start.7 = (bf16[256,128]{1,0:T(8,128)(2,1)S(1)}, bf16[256,128]{1,0:T(8,128)(2,1)S(1)}, u32[]{:S(2)}, u32[]{:S(2)}) collective-permute-start(bf16[256,128]{1,0:T(8,128)(2,1)S(1)} %fusion.2), channel_id=1, source_target_pairs={{0,2},{2,0},{1,3},{3,1},{4,6},{6,4},{5,7},{7,5},{8,10},{10,8},{9,1... | collective-permute-start | bytes 196616 | tf_op jit(solution)/shard_map/ppermute | solution.py:627
  36.2 2.8 %collective-permute-done.7 = bf16[256,128]{1,0:T(8,128)(2,1)S(1)} collective-permute-done((bf16[256,128]{1,0:T(8,128)(2,1)S(1)}, bf16[256,128]{1,0:T(8,128)(2,1)S(1)}, u32[]{:S(2)}, u32[]{:S(2)}) %collective-permute-start.7) | collective-permute-done | bytes 65568 | tf_op jit(solution)/shard_map/ppermute | solution.py:627
  39.0 0.1 collective-permute-start.8
  39.1 1.3 %collective-permute-done.8.other = f32[256,128]{1,0:T(8,128)S(1)} collective-permute-done((f32[256,128]{1,0:T(8,128)S(1)}, f32[256,128]{1,0:T(8,128)S(1)}, u32[]{:S(2)}, u32[]{:S(2)}) %collective-permute-start.8) | collective-permute-done | bytes 131104 | tf_op jit(solution)/shard_map/ppermute | solution.py:630
  40.4 0.7 %assemble.1 = (f32[101,512]{1,0:T(8,128)}, f32[101,128]{1,0:T(8,128)}) custom-call(f32[256,128]{1,0:T(8,128)S(1)} %convert_add_fusion.whole, f32[256,128]{1,0:T(8,128)S(1)} %collective-permute-done.8.other), custom_call_target="tpu_custom_call" | custom-call | tf_op jit(solution)/shard_map/assemble/pallas_call | solution.py:576
  (3 shorter events, 0.1 us)
Async XLA Ops:
  0.6 8.4 %copy-start = (bf16[512,512]{1,0:T(8,128)(2,1)S(1)}, bf16[512,512]{1,0:T(8,128)(2,1)}, u32[]{:S(2)}) copy-start(bf16[512,512]{1,0:T(8,128)(2,1)} %constant.7.refs_3_.refs_7_) | copy-start | bytes 1572868
  1.3 14.1 %copy-start.1 = (bf16[2,256,512]{2,1,0:T(8,128)(2,1)S(1)}, bf16[2,256,512]{2,1,0:T(8,128)(2,1)}, u32[]{:S(2)}) copy-start(bf16[2,256,512]{2,1,0:T(8,128)(2,1)} %constant.12.refs_8_) | copy-start | bytes 1572868
  3.3 9.4 %collective-permute-start = (bf16[4,8704]{1,0:T(4,128)(2,1)}, bf16[4,8704]{1,0:T(4,128)(2,1)S(1)}, u32[]{:S(2)}, u32[]{:S(2)}) collective-permute-start(bf16[4,8704]{1,0:T(4,128)(2,1)} %get-tuple-element.12), channel_id=1, source_target_pairs={{0,4},{4,0},{8,12},{12,8},{1,5},{5,1},{9,13},{13,9},{2,6},{6,2},{1... | collective-permute-start | bytes 208904 | tf_op jit(solution)/shard_map/ppermute | solution.py:105
  6.5 7.7 %collective-permute-start.1 = (bf16[4,8704]{1,0:T(4,128)(2,1)}, bf16[4,8704]{1,0:T(4,128)(2,1)S(1)}, u32[]{:S(2)}, u32[]{:S(2)}) collective-permute-start(bf16[4,8704]{1,0:T(4,128)(2,1)} %get-tuple-element.13), channel_id=1, source_target_pairs={{0,8},{4,12},{8,0},{12,4},{1,9},{5,13},{9,1},{13,5},{2,10},{6,14},... | collective-permute-start | bytes 208904 | tf_op jit(solution)/shard_map/ppermute | solution.py:105
  9.0 6.4 %collective-permute-start.2 = (bf16[4,8704]{1,0:T(4,128)(2,1)}, bf16[4,8704]{1,0:T(4,128)(2,1)S(1)}, u32[]{:S(2)}, u32[]{:S(2)}) collective-permute-start(bf16[4,8704]{1,0:T(4,128)(2,1)} %get-tuple-element.14), channel_id=1, source_target_pairs={{0,12},{4,8},{8,4},{12,0},{1,13},{5,9},{9,5},{13,1},{2,14},{6,10},... | collective-permute-start | bytes 208904 | tf_op jit(solution)/shard_map/ppermute | solution.py:105
  9.0 0.9 %copy-start.2 = (bf16[4,8704]{1,0:T(4,128)(2,1)S(1)}, bf16[4,8704]{1,0:T(4,128)(2,1)}, u32[]{:S(2)}) copy-start(bf16[4,8704]{1,0:T(4,128)(2,1)} %get-tuple-element.11.refs_0_) | copy-start | bytes 208900
  9.9 0.7 %copy-start.4 = (s32[256,20]{0,1:T(8,128)S(1)}, s32[256,20]{0,1:T(8,128)}, u32[]{:S(2)}) copy-start(s32[256,20]{0,1:T(8,128)} %param.12) | copy-start | bytes 61444
  10.7 0.7 %copy-start.5 = (s32[256]{0:T(256)S(1)}, s32[256]{0:T(256)}, u32[]{:S(2)}) copy-start(s32[256]{0:T(256)} %param.11) | copy-start | bytes 3076
  11.3 4.1 %copy-start.3 = (bf16[4,8704]{1,0:T(4,128)(2,1)S(1)}, bf16[4,8704]{1,0:T(4,128)(2,1)}, u32[]{:S(2)}) copy-start(bf16[4,8704]{1,0:T(4,128)(2,1)} %get-tuple-element.11.refs_0_) | copy-start | bytes 208900
  22.9 1.6 %collective-permute-start.3 = (bf16[4,256,128]{2,1,0:T(8,128)(2,1)S(1)}, bf16[4,256,128]{2,1,0:T(8,128)(2,1)S(1)}, u32[]{:S(2)}, u32[]{:S(2)}) collective-permute-start(bf16[4,256,128]{2,1,0:T(8,128)(2,1)S(1)} %get-tuple-element.19), channel_id=1, source_target_pairs={{0,1},{1,0},{2,3},{3,2},{4,5},{5,4},{6,7},{7,6},{8,9},{9,8},{10,11... | collective-permute-start | bytes 786440 | tf_op jit(solution)/shard_map/ppermute | solution.py:613
  24.6 4.3 %collective-permute-start.4 = (bf16[256,128]{1,0:T(8,128)(2,1)S(1)}, bf16[256,128]{1,0:T(8,128)(2,1)S(1)}, u32[]{:S(2)}, u32[]{:S(2)}) collective-permute-start(bf16[256,128]{1,0:T(8,128)(2,1)S(1)} %get-tuple-element.20), channel_id=1, source_target_pairs={{0,4},{4,0},{8,12},{12,8},{1,5},{5,1},{9,13},{13,9},{2,6},{6,2},{1... | collective-permute-start | bytes 196616 | tf_op jit(solution)/shard_map/ppermute | solution.py:105
  25.5 6.9 %collective-permute-start.6 = (bf16[256,128]{1,0:T(8,128)(2,1)S(1)}, bf16[256,128]{1,0:T(8,128)(2,1)S(1)}, u32[]{:S(2)}, u32[]{:S(2)}) collective-permute-start(bf16[256,128]{1,0:T(8,128)(2,1)S(1)} %get-tuple-element.21), channel_id=1, source_target_pairs={{0,12},{4,8},{8,4},{12,0},{1,13},{5,9},{9,5},{13,1},{2,14},{6,10},... | collective-permute-start | bytes 196616 | tf_op jit(solution)/shard_map/ppermute | solution.py:105
  27.9 6.7 %collective-permute-start.5 = (bf16[256,128]{1,0:T(8,128)(2,1)S(1)}, bf16[256,128]{1,0:T(8,128)(2,1)S(1)}, u32[]{:S(2)}, u32[]{:S(2)}) collective-permute-start(bf16[256,128]{1,0:T(8,128)(2,1)S(1)} %get-tuple-element.22), channel_id=1, source_target_pairs={{0,8},{4,12},{8,0},{12,4},{1,9},{5,13},{9,1},{13,5},{2,10},{6,14},... | collective-permute-start | bytes 196616 | tf_op jit(solution)/shard_map/ppermute | solution.py:105
  34.6 4.3 %collective-permute-start.7 = (bf16[256,128]{1,0:T(8,128)(2,1)S(1)}, bf16[256,128]{1,0:T(8,128)(2,1)S(1)}, u32[]{:S(2)}, u32[]{:S(2)}) collective-permute-start(bf16[256,128]{1,0:T(8,128)(2,1)S(1)} %fusion.2), channel_id=1, source_target_pairs={{0,2},{2,0},{1,3},{3,1},{4,6},{6,4},{5,7},{7,5},{8,10},{10,8},{9,1... | collective-permute-start | bytes 196616 | tf_op jit(solution)/shard_map/ppermute | solution.py:627
  39.0 1.4 %collective-permute-start.8 = (f32[256,128]{1,0:T(8,128)S(1)}, f32[256,128]{1,0:T(8,128)S(1)}, u32[]{:S(2)}, u32[]{:S(2)}) collective-permute-start(f32[256,128]{1,0:T(8,128)S(1)} %convert_add_fusion.whole), channel_id=1, source_target_pairs={{0,1},{1,0},{2,3},{3,2},{4,5},{5,4},{6,7},{7,6},{8,9},{9,8},{10,11... | collective-permute-start | bytes 393224 | tf_op jit(solution)/shard_map/ppermute | solution.py:630
